TPU v7x, 256 devices: a whole 4x4x8 slice. The times are simulated.
256 devices in a mesh: expert: 64 (over x, z, core), replica: 4 (over y).
Axes of the slice: x: 4, y: 4, z: 8, core: 2. Of those that a mesh axis runs over, the one named last changes fastest.
Arguments:
- tokens: bfloat16 [8192, 2560], P('expert'), may hold values from -6 to 6
- expert_ids: int32 [8192, 6], P('expert'), may hold values from 0 to 63, all different within a row; in each aligned block of 128 rows (0 to 127, 128 to 255, ...) at most 16 rows name the same one
- route_weights: float32 [8192, 6], P('expert'), may hold values from 0.05 to 0.5
- w_gate: bfloat16 [64, 2560, 1536], P('expert', None, 'replica'), may hold values from -0.125 to 0.125
- w_up: bfloat16 [64, 2560, 1536], P('expert', None, 'replica'), may hold values from -0.125 to 0.125
- w_down: bfloat16 [64, 1536, 2560], P('expert', 'replica'), may hold values from -0.15625 to 0.15625
- cotangent: bfloat16 [8192, 2560], P('expert'), may hold values from -6 to 6
Outputs:
- mixed: bfloat16 [8192, 2560], P('expert', 'replica')
- tokens_grad: bfloat16 [8192, 2560], P('expert', 'replica')
Inputs may be any that keep to these rules, and one draw needn't show every extreme that they name: `expert_ids`: each row names 6 different experts. In each aligned block of 128 rows no expert is named by more than 16 rows, a bound that some block reaches.
All inputs are finite; a program needn't handle non-finite values.
Results may differ from a plain program's by a relative error of at most 0.0064.
Values may be sent and summed in bfloat16 or wider, within the bound.
No kernel may reach another device: no remote copies, remote signals or barrier semaphores. Data moves between devices by JAX's collectives and lax.ppermute only.
A program may use at most 128 MiB of HBM per device.

v0:
```python
import jax
import jax.numpy as jnp
from jax import lax
from jax.sharding import PartitionSpec as P


def slot_table(expert_ids, num_experts, capacity):
    flat_ids = expert_ids.reshape(-1)
    one_hot = (flat_ids[:, None] == jnp.arange(num_experts, dtype=jnp.int32)[None, :]).astype(
        jnp.int32
    )
    earlier = jnp.cumsum(one_hot, axis=0) - one_hot
    slots = jnp.sum(earlier * one_hot, axis=1)
    positions = flat_ids * capacity + slots
    numbering = jnp.arange(flat_ids.shape[0], dtype=jnp.int32) + 1
    owners = jnp.zeros((num_experts * capacity,), jnp.int32).at[positions].set(numbering)
    return (positions, owners)


def pack_rows(source, owners, divisor):
    present = owners > 0
    index_rows = jnp.maximum(owners - 1, 0) // divisor
    picked = jnp.take(source, index_rows, axis=0)
    return jnp.where(present[:, None], picked, jnp.zeros_like(picked))


def send_to_experts(packed, num_experts, capacity):
    width = packed.shape[1]
    arrived = lax.all_to_all(
        packed.reshape(num_experts, capacity, width),
        "expert",
        split_axis=0,
        concat_axis=0,
        tiled=True,
    )
    return arrived.reshape(num_experts * capacity, width)


def return_rows(partial_value, num_experts, capacity):
    summed = lax.psum_scatter(partial_value, "replica", scatter_dimension=1, tiled=True).astype(
        jnp.bfloat16
    )
    share = summed.shape[1]
    moved = lax.all_to_all(
        summed.reshape(num_experts, capacity, share),
        "expert",
        split_axis=0,
        concat_axis=0,
        tiled=True,
    )
    return moved.reshape(num_experts * capacity, share)


def gather_slots(returned, positions, tok_rows, top):
    picked = jnp.take(returned, positions, axis=0).reshape(tok_rows, top, returned.shape[1])
    return picked.astype(jnp.float32)


def per_device(tokens, expert_ids, route_weights, w_gate, w_up, w_down, cotangent):
    num_experts = lax.axis_size("expert")
    tok_rows, top = expert_ids.shape
    capacity = tok_rows * top * 4 // (num_experts * 3)
    positions, owners = slot_table(expert_ids, num_experts, capacity)
    contract = (((1,), (1,)), ((), ()))
    flat_weights = route_weights.reshape(-1)
    slot_weight = jnp.where(owners > 0, jnp.take(flat_weights, jnp.maximum(owners - 1, 0)), 0.0)
    packed_rows = pack_rows(tokens, owners, top)
    packed_grad = pack_rows(cotangent, owners, top)
    scaled = (packed_grad.astype(jnp.float32) * slot_weight[:, None]).astype(jnp.bfloat16)
    gate_w = w_gate[0]
    up_w = w_up[0]
    down_w = w_down[0]
    rows = send_to_experts(packed_rows, num_experts, capacity)
    gate = jnp.dot(rows, gate_w, preferred_element_type=jnp.float32)
    up = jnp.dot(rows, up_w, preferred_element_type=jnp.float32)
    sig = jax.nn.sigmoid(gate)
    act = gate * sig
    hidden = (act * up).astype(jnp.bfloat16)
    down_out = jnp.dot(hidden, down_w, preferred_element_type=jnp.float32)
    outputs = return_rows(down_out, num_experts, capacity)
    grad_rows = send_to_experts(scaled, num_experts, capacity)
    per_slot = gather_slots(outputs, positions, tok_rows, top)
    mixed = jnp.sum(per_slot * route_weights[:, :, None], axis=1).astype(jnp.bfloat16)
    hidden_grad = lax.dot_general(grad_rows, down_w, contract, preferred_element_type=jnp.float32)
    gate_grad = (hidden_grad * up * sig * (1.0 + gate * (1.0 - sig))).astype(jnp.bfloat16)
    up_grad = (hidden_grad * act).astype(jnp.bfloat16)
    partial_value = lax.dot_general(gate_grad, gate_w, contract, preferred_element_type=jnp.float32)
    partial_value = partial_value + lax.dot_general(
        up_grad, up_w, contract, preferred_element_type=jnp.float32
    )
    returned = return_rows(partial_value, num_experts, capacity)
    tokens_grad = jnp.sum(gather_slots(returned, positions, tok_rows, top), axis=1).astype(
        jnp.bfloat16
    )
    return (mixed, tokens_grad)


def solution(mesh):
    in_specs = (
        P("expert", None),
        P("expert", None),
        P("expert", None),
        P("expert", None, "replica"),
        P("expert", None, "replica"),
        P("expert", "replica", None),
        P("expert", None),
    )
    out_specs = (P("expert", "replica"), P("expert", "replica"))
    return jax.shard_map(
        per_device, mesh=mesh, in_specs=in_specs, out_specs=out_specs, check_vma=False
    )
```

profile of v0, /device:TPU:1, one launch (start us, length us, event | category | flops | bytes accessed | tf_op | source)
XLA Modules:
  0.0 570.6 jit_solution(3254719742088907695)
XLA Ops:
  11.7 3.4 scatter_custom_fusion
  15.1 6.3 %gather_fusion.1 = bf16[1024,2560]{1,0:T(8,128)(2,1)} fusion(bf16[128,2560]{1,0:T(8,128)(2,1)S(1)} %copy-done.1, s32[1024]{0:T(1024)S(1)} %get-tuple-element.7), kind=kCustom, calls=%fused_computation.clone | custom fusion | bytes 10489856 | tf_op jit(solution)/shard_map/jit(_take)/gather | solution.py:23
  21.4 6.3 %select_select_fusion.1 = bf16[1024,2560]{1,0:T(8,128)(2,1)} fusion(bf16[1024,2560]{1,0:T(8,128)(2,1)} %gather_fusion.1, pred[1024]{0:T(1024)(128)(4,1)S(1)} %get-tuple-element.9, pred[1024]{0:T(1024)(128)(4,1)S(1)} %get-tuple-element.8), kind=kLoop, calls=%fused_computation.9 | loop fusion | flops 5242880 | bytes 10487808 | tf_op jit(solution)/shard_map/jit(_where)/select_n | solution.py:24
  27.7 13.3 %all-to-all-start = ((bf16[64,16,2560]{2,1,0:T(8,128)(2,1)}), bf16[64,16,2560]{2,1,0:T(8,128)(2,1)}, u32[]{:S(2)}, u32[]{:S(2)}) async-start(bf16[64,16,2560]{2,1,0:T(8,128)(2,1)} %bitcast.48), calls=%async_computation | async-start | bytes 10485760 | tf_op jit(solution)/shard_map/all_to_all | solution.py:29
  41.3 6.3 %gather_fusion.3 = bf16[1024,2560]{1,0:T(8,128)(2,1)} fusion(bf16[128,2560]{1,0:T(8,128)(2,1)S(1)} %copy-done.2, s32[1024]{0:T(1024)S(1)} %get-tuple-element.7), kind=kCustom, calls=%fused_computation.2.clone | custom fusion | bytes 10489856 | tf_op jit(solution)/shard_map/jit(_take)/gather | solution.py:23
  47.6 4.5 gather_fusion
  52.2 7.0 %multiply_convert_fusion = bf16[1024,2560]{1,0:T(8,128)(2,1)} fusion(bf16[1024,2560]{1,0:T(8,128)(2,1)} %gather_fusion.3, f32[1024]{0:T(1024)S(1)} %select_select_fusion.2, pred[1024]{0:T(1024)(128)(4,1)S(1)} %get-tuple-element.9, pred[1024]{0:T(1024)(128)(4,1)S(1)} %get-tuple-element.8), kind=kLoop, calls=%fused_computation.6 | loop fusion | flops 13107200 | bytes 10491904 | tf_op jit(solution)/shard_map/convert_element_type | solution.py:69
  59.1 100.2 %all-to-all-done = bf16[64,16,2560]{2,1,0:T(8,128)(2,1)} async-done(((bf16[64,16,2560]{2,1,0:T(8,128)(2,1)}), bf16[64,16,2560]{2,1,0:T(8,128)(2,1)}, u32[]{:S(2)}, u32[]{:S(2)}) %all-to-all-start) | async-done | bytes 5242912 | tf_op jit(solution)/shard_map/all_to_all | solution.py:29
  159.4 6.0 %all-to-all-start.2 = ((bf16[64,16,2560]{2,1,0:T(8,128)(2,1)}), bf16[64,16,2560]{2,1,0:T(8,128)(2,1)}, u32[]{:S(2)}, u32[]{:S(2)}) async-start(bf16[64,16,2560]{2,1,0:T(8,128)(2,1)} %bitcast.49), calls=%async_computation.3 | async-start | bytes 10485760 | tf_op jit(solution)/shard_map/all_to_all | solution.py:29
  165.6 4.9 fusion.9
  170.5 6.5 %fusion.5 = f32[1024,384]{1,0:T(8,128)} fusion(bf16[1024,2560]{1,0:T(8,128)(2,1)} %bitcast.2, bf16[1,2560,384]{2,1,0:T(8,128)(2,1)S(1)} %copy-done.5), kind=kOutput, calls=%fused_computation.16 | convolution fusion | flops 2013265920 | bytes 8781824 | tf_op jit(solution)/shard_map/dot_general | solution.py:75
  177.1 106.6 %all-to-all-done.2 = bf16[64,16,2560]{2,1,0:T(8,128)(2,1)} async-done(((bf16[64,16,2560]{2,1,0:T(8,128)(2,1)}), bf16[64,16,2560]{2,1,0:T(8,128)(2,1)}, u32[]{:S(2)}, u32[]{:S(2)}) %all-to-all-start.2) | async-done | bytes 5242912 | tf_op jit(solution)/shard_map/all_to_all | solution.py:29
  283.7 5.5 fusion
  289.3 3.2 fusion.7
  292.5 5.8 %convolution_add_fusion = f32[1024,2560]{1,0:T(8,128)} fusion(f32[1024,2560]{1,0:T(8,128)S(1)} %fusion.7, bf16[1,2560,384]{2,1,0:T(8,128)(2,1)S(1)} %copy-done.6, f32[1024,384]{1,0:T(8,128)S(1)} %fusion, f32[1024,384]{1,0:T(8,128)S(1)} %fusion.9), kind=kOutput, calls=%fused_computation.7 | convolution fusion | flops 2018246656 | bytes 26083328 | tf_op jit(solution)/shard_map/dot_general | solution.py:88
  298.3 9.4 %fusion.2 = f32[1024,2560]{1,0:T(8,128)} fusion(bf16[1,384,2560]{2,1,0:T(8,128)(2,1)} %param.16, f32[1024,384]{1,0:T(8,128)} %fusion.5, f32[1024,384]{1,0:T(8,128)S(1)} %fusion.9), kind=kOutput, calls=%fused_computation.13 | convolution fusion | flops 2015625216 | bytes 15597568 | tf_op jit(solution)/shard_map/dot_general | solution.py:79
  307.7 87.4 %reduce-scatter.5.cloned.1.call-done = f32[1024,640]{1,0:T(8,128)} async-done(((f32[1024,2560]{1,0:T(8,128)}), f32[1024,640]{1,0:T(8,128)}) %reduce-scatter.5.cloned.1.call-update) | async-done | bytes 2621456 | tf_op jit(solution)/shard_map/reduce_scatter | solution.py:40
  398.0 10.7 %all-to-all-start.3 = ((bf16[64,16,640]{2,1,0:T(8,128)(2,1)}), bf16[64,16,640]{2,1,0:T(8,128)(2,1)S(1)}, u32[]{:S(2)}, u32[]{:S(2)}) async-start(bf16[64,16,640]{2,1,0:T(8,128)(2,1)} %bitcast.51), calls=%async_computation.5 | async-start | bytes 2621440 | tf_op jit(solution)/shard_map/all_to_all | solution.py:44
  408.8 88.8 %reduce-scatter.3.cloned.1.call-done = f32[1024,640]{1,0:T(8,128)} async-done(((f32[1024,2560]{1,0:T(8,128)}), f32[1024,640]{1,0:T(8,128)}) %reduce-scatter.3.cloned.1.call-update) | async-done | bytes 2621456 | tf_op jit(solution)/shard_map/reduce_scatter | solution.py:40
  500.6 10.9 %all-to-all-start.1 = ((bf16[64,16,640]{2,1,0:T(8,128)(2,1)}), bf16[64,16,640]{2,1,0:T(8,128)(2,1)}, u32[]{:S(2)}, u32[]{:S(2)}) async-start(bf16[64,16,640]{2,1,0:T(8,128)(2,1)} %bitcast.50), calls=%async_computation.2 | async-start | bytes 2621440 | tf_op jit(solution)/shard_map/all_to_all | solution.py:44
  511.5 3.4 gather_fusion.4
  514.9 30.6 %all-to-all-done.1 = bf16[64,16,640]{2,1,0:T(8,128)(2,1)} async-done(((bf16[64,16,640]{2,1,0:T(8,128)(2,1)}), bf16[64,16,640]{2,1,0:T(8,128)(2,1)}, u32[]{:S(2)}, u32[]{:S(2)}) %all-to-all-start.1) | async-done | bytes 1310752 | tf_op jit(solution)/shard_map/all_to_all | solution.py:44
  545.6 5.2 gather_fusion.2
  559.0 3.3 multiply_reduce_fusion
  (51 shorter events, 20.8 us)
Async XLA Ops:
  7.2 158.4 %copy-start = (bf16[1,2560,384]{2,1,0:T(8,128)(2,1)S(1)}, bf16[1,2560,384]{2,1,0:T(8,128)(2,1)}, u32[]{:S(2)}) copy-start(bf16[1,2560,384]{2,1,0:T(8,128)(2,1)} %param.14) | copy-start | bytes 5898244
  7.2 7.9 %copy-start.1 = (bf16[128,2560]{1,0:T(8,128)(2,1)S(1)}, bf16[128,2560]{1,0:T(8,128)(2,1)}, u32[]{:S(2)}) copy-start(bf16[128,2560]{1,0:T(8,128)(2,1)} %param.11) | copy-start | bytes 1966084
  27.7 13.3 %copy-start.9 = (f32[128,6]{0,1:T(8,128)S(1)}, f32[128,6]{0,1:T(8,128)}, u32[]{:S(2)}) copy-start(f32[128,6]{0,1:T(8,128)} %param.13) | copy-start | bytes 9220
  27.7 13.6 %copy-start.2 = (bf16[128,2560]{1,0:T(8,128)(2,1)S(1)}, bf16[128,2560]{1,0:T(8,128)(2,1)}, u32[]{:S(2)}) copy-start(bf16[128,2560]{1,0:T(8,128)(2,1)} %param.17) | copy-start | bytes 1966084
  27.7 131.6 %all-to-all-start = ((bf16[64,16,2560]{2,1,0:T(8,128)(2,1)}), bf16[64,16,2560]{2,1,0:T(8,128)(2,1)}, u32[]{:S(2)}, u32[]{:S(2)}) async-start(bf16[64,16,2560]{2,1,0:T(8,128)(2,1)} %bitcast.48), calls=%async_computation | async-start | bytes 10485760 | tf_op jit(solution)/shard_map/all_to_all | solution.py:29
  41.1 6.5 %copy-start.7 = (f32[128,6]{1,0:T(8,128)}, f32[128,6]{1,0:T(8,128)S(1)}, u32[]{:S(2)}) copy-start(f32[128,6]{1,0:T(8,128)S(1)} %copy.14) | copy-start | bytes 9220
  159.4 124.3 %all-to-all-start.2 = ((bf16[64,16,2560]{2,1,0:T(8,128)(2,1)}), bf16[64,16,2560]{2,1,0:T(8,128)(2,1)}, u32[]{:S(2)}, u32[]{:S(2)}) async-start(bf16[64,16,2560]{2,1,0:T(8,128)(2,1)} %bitcast.49), calls=%async_computation.3 | async-start | bytes 10485760 | tf_op jit(solution)/shard_map/all_to_all | solution.py:29
  165.3 229.8 %reduce-scatter.5.cloned.1.call-start = ((), (), s32[]{:S(2)}) async-start(), calls=%async_computation.7 | async-start | bytes 13107200 | tf_op jit(solution)/shard_map/reduce_scatter | solution.py:40
  165.6 5.0 copy-start.5
  283.7 5.6 copy-start.3
  289.2 3.2 copy-start.6
  298.3 199.3 %reduce-scatter.3.cloned.1.call-start = ((), (), s32[]{:S(2)}) async-start(), calls=%async_computation.6 | async-start | bytes 13107200 | tf_op jit(solution)/shard_map/reduce_scatter | solution.py:40
  398.0 102.5 %all-to-all-start.3 = ((bf16[64,16,640]{2,1,0:T(8,128)(2,1)}), bf16[64,16,640]{2,1,0:T(8,128)(2,1)S(1)}, u32[]{:S(2)}, u32[]{:S(2)}) async-start(bf16[64,16,640]{2,1,0:T(8,128)(2,1)} %bitcast.51), calls=%async_computation.5 | async-start | bytes 2621440 | tf_op jit(solution)/shard_map/all_to_all | solution.py:44
  500.6 45.0 %all-to-all-start.1 = ((bf16[64,16,640]{2,1,0:T(8,128)(2,1)}), bf16[64,16,640]{2,1,0:T(8,128)(2,1)}, u32[]{:S(2)}, u32[]{:S(2)}) async-start(bf16[64,16,640]{2,1,0:T(8,128)(2,1)} %bitcast.50), calls=%async_computation.2 | async-start | bytes 2621440 | tf_op jit(solution)/shard_map/all_to_all | solution.py:44
  545.6 5.2 copy-start.4
  555.9 3.1 copy-start.8
Sparse Core Ops, SparseCore 0:
  298.4 96.6 reduce-scatter.4
  397.7 99.8 reduce-scatter.2
where the time goes:
time: 572 us; the launch traced here: 571 us
  waiting for transfers between devices  414 us (72%)
  starting transfers between devices  41.1 us (7%)
  local copies, waits for them, and re-layouts  36.1 us (6%)
  matrix products  35.3 us (6%)
  other arithmetic  30 us (5%)
  between operations  14.3 us (2%)
    all_to_all x2, waiting for transfers between devices, send_to_experts(): lax.all_to_all(packed.reshape(num_experts, capacity, width), 'expert', sp...  207 us
    reduce_scatter x2, waiting for transfers between devices, return_rows(): lax.psum_scatter(partial_value, 'replica', scatter_dimension=1, tiled=True)  176 us
    all_to_all x2, waiting for transfers between devices, return_rows(): lax.all_to_all(summed.reshape(num_experts, capacity, share), 'expert', sp...  30.6 us
    all_to_all x2, starting transfers between devices, return_rows(): lax.all_to_all(summed.reshape(num_experts, capacity, share), 'expert', sp...  21.6 us
    all_to_all x2, starting transfers between devices, send_to_experts(): lax.all_to_all(packed.reshape(num_experts, capacity, width), 'expert', sp...  19.2 us
    gather x2, local copies, waits for them, and re-layouts, pack_rows(): picked = jnp.take(source, index_rows, axis=0)  12.6 us
  transfers between devices with their start and end apart: 6, of which 5 were waited for; matrix products, arithmetic and copies ran while one was open for 8% of the time, Pallas kernels for 0%

commit v1 on v0

v1 whole, which is shorter than its diff:
```python
import jax
import jax.numpy as jnp
from jax import lax
from jax.sharding import PartitionSpec as P


BF = jnp.bfloat16
F32 = jnp.float32
B_PAIRS = [(0, 1), (1, 0), (2, 3), (3, 2)]
A_PAIRS = [(0, 3), (3, 0), (1, 2), (2, 1)]


def swap_b(value):
    return lax.ppermute(value, "replica", B_PAIRS)


def swap_a(value):
    return lax.ppermute(value, "replica", A_PAIRS)


def dot(lhs, rhs, ldim=1, rdim=0):
    return lax.dot_general(lhs, rhs, (((ldim,), (rdim,)), ((), ())), preferred_element_type=F32)


def halves(value, axis, first):
    low, high = jnp.split(value, 2, axis=axis)
    return jnp.where(first == 0, low, high), jnp.where(first == 0, high, low)


def exchange(rows, num_experts):
    width = rows.shape[1]
    moved = lax.all_to_all(
        rows.reshape(num_experts, -1, width), "expert", split_axis=0, concat_axis=0, tiled=True
    )
    return moved.reshape(-1, width)


def layer(tokens, expert_ids, route_weights, w_gate, w_up, w_down, cotangent):
    num_experts = lax.axis_size("expert")
    tok_rows, top = expert_ids.shape
    capacity = tok_rows * top * 4 // (num_experts * 3)
    slots = capacity // 2
    y = lax.axis_index("replica")
    a = y >> 1
    b = ((y + 1) >> 1) & 1
    gate_w, up_w, down_w = w_gate[0], w_up[0], w_down[0]

    gate_b = swap_b(gate_w)
    up_b = swap_b(up_w)
    down_own, down_far = halves(down_w, 1, a)
    down_a = swap_a(down_far)
    down_b = swap_b(down_own)
    down_ab = swap_b(down_a)

    experts = jnp.arange(num_experts, dtype=jnp.int32)
    hit = expert_ids.T[None, :, :] == experts[:, None, None]
    chosen = jnp.sum(hit.astype(F32), axis=1)
    weight = jnp.sum(jnp.where(hit, route_weights.T[None, :, :], 0.0), axis=1)
    before = jnp.arange(tok_rows)[:, None] < jnp.arange(tok_rows)[None, :]
    rank = dot(chosen.astype(BF), before.astype(BF))
    place = jnp.where(chosen > 0, rank.astype(jnp.int32) - slots * b, -1)
    pick = place[:, None, :] == jnp.arange(slots, dtype=jnp.int32)[None, :, None]
    pick_w = jnp.where(pick, weight[:, None, :], 0.0).reshape(-1, tok_rows)
    pick = pick.astype(BF).reshape(-1, tok_rows)
    slot_weight = jnp.sum(pick_w, axis=1, keepdims=True)
    pick_hi = pick_w.astype(BF)
    pick_lo = (pick_w - pick_hi.astype(F32)).astype(BF)

    tok_half, _ = halves(tokens, 1, a)
    cot_half, _ = halves(cotangent, 1, a)
    packed = dot(pick, tok_half).astype(BF)
    rows_near = exchange(packed, num_experts)
    rows_far = swap_a(rows_near)
    packed_grad = (dot(pick, cot_half) * slot_weight).astype(BF)
    grad_rows = exchange(packed_grad, num_experts)

    gate_1n, gate_1f = halves(gate_w, 0, a)
    up_1n, up_1f = halves(up_w, 0, a)
    gate_2n, gate_2f = halves(gate_b, 0, a)
    up_2n, up_2f = halves(up_b, 0, a)

    def forward(gate_n, gate_f, up_n, up_f):
        gate = dot(rows_near, gate_n) + dot(rows_far, gate_f)
        up = dot(rows_near, up_n) + dot(rows_far, up_f)
        hidden = (gate * jax.nn.sigmoid(gate) * up).astype(BF)
        return lax.optimization_barrier((gate, up, hidden))

    def backward(hidden_grad, gate, up):
        sig = jax.nn.sigmoid(gate)
        act = gate * sig
        gate_grad = (hidden_grad * up * sig * (1.0 + gate * (1.0 - sig))).astype(BF)
        return gate_grad, (hidden_grad * act).astype(BF)

    gate_1, up_1, hidden_1 = forward(gate_1n, gate_1f, up_1n, up_1f)
    gate_2, up_2, hidden_2 = forward(gate_2n, gate_2f, up_2n, up_2f)
    hidden_3 = swap_a(hidden_1)
    hidden_4 = swap_a(hidden_2)
    hgrad_3 = dot(grad_rows, down_a, 1, 1).astype(BF)
    hgrad_3 = swap_a(hgrad_3)
    hgrad_4 = dot(grad_rows, down_ab, 1, 1).astype(BF)
    hgrad_4 = swap_a(hgrad_4)

    mixed_rows = dot(hidden_1, down_own) + dot(hidden_3, down_a)
    mixed_rows = mixed_rows + dot(hidden_2, down_b) + dot(hidden_4, down_ab)
    mixed_back = exchange(mixed_rows.astype(BF), num_experts)

    hgrad_1 = dot(grad_rows, down_own, 1, 1)
    hgrad_2 = dot(grad_rows, down_b, 1, 1)
    gg_1, ug_1 = backward(hgrad_1 + hgrad_3.astype(F32), gate_1, up_1)
    gg_2, ug_2 = backward(hgrad_2 + hgrad_4.astype(F32), gate_2, up_2)
    far = dot(gg_1, gate_1f, 1, 1) + dot(ug_1, up_1f, 1, 1)
    far = far + dot(gg_2, gate_2f, 1, 1) + dot(ug_2, up_2f, 1, 1)
    far = far.astype(BF)
    far = swap_a(far)
    near = dot(gg_1, gate_1n, 1, 1) + dot(ug_1, up_1n, 1, 1)
    near = near + dot(gg_2, gate_2n, 1, 1) + dot(ug_2, up_2n, 1, 1)
    near = near + far.astype(F32)
    grad_back = exchange(near.astype(BF), num_experts)

    def finish(partial):
        keep, give = halves(partial, 1, y & 1)
        return (keep + swap_b(give.astype(BF)).astype(F32)).astype(BF)

    mixed = finish(dot(pick_hi, mixed_back, 0, 0) + dot(pick_lo, mixed_back, 0, 0))
    tokens_grad = finish(dot(pick, grad_back, 0, 0))
    return (mixed, tokens_grad)


def solution(mesh):
    in_specs = (
        P("expert", None),
        P("expert", None),
        P("expert", None),
        P("expert", None, "replica"),
        P("expert", None, "replica"),
        P("expert", "replica", None),
        P("expert", None),
    )
    out_specs = (P("expert", "replica"), P("expert", "replica"))
    return jax.shard_map(
        layer, mesh=mesh, in_specs=in_specs, out_specs=out_specs, check_vma=False
    )
```

time: 572 us -> 340 us (0.59)
  waiting for transfers between devices: 414 us -> 209 us
  local copies, waits for them, and re-layouts: 36.1 us -> 0.53 us
  matrix products: 35.3 us -> 64.9 us
  other arithmetic: 30 us -> 3.38 us
  starting transfers between devices: 41.1 us -> 59.9 us
  between operations: 14.3 us -> 1.02 us
    reduce_scatter x2 -> x0, waiting for transfers between devices: 176 us -> none  [return_rows(): lax.psum_scatter(partial_value, 'replica', scatter_dimension=1, tiled=True)]
    all_to_all x4, waiting for transfers between devices: 237 us -> 65.4 us  [exchange(): lax.all_to_all(rows.reshape(num_experts, -1, width), 'expert', split_axis...]
    ppermute x0 -> x13, waiting for transfers between devices: none -> 144 us  [the longest x6 98.4 us: swap_b(): return lax.ppermute(value, 'replica', B_PAIRS)]
    dot_general x6 -> x30, matrix products: 35.3 us -> 64.9 us  [dot(): lax.dot_general(lhs, rhs, (((ldim,), (rdim,)), ((), ())), preferred_eleme...]
    gather x5 -> x0, local copies, waits for them, and re-layouts: 25.7 us -> none  [the longest x2 12.6 us: pack_rows(): picked = jnp.take(source, index_rows, axis=0)]
    ppermute x0 -> x13, starting transfers between devices: none -> 16.8 us  [the longest x7 13.6 us: swap_a(): return lax.ppermute(value, 'replica', A_PAIRS)]
    convert_element_type x4 -> x6, other arithmetic: 12.9 us -> 2.36 us  [the longest x4 1.49 us: finish(): return (keep + swap_b(give.astype(BF)).astype(F32)).astype(BF)]
    select_n x4 -> x1, other arithmetic: 9.47 us -> 0.13 us  [halves(): return (jnp.where(first == 0, low, high), jnp.where(first == 0, high, low))]
  transfers between devices with their start and end apart: 6 -> 17, of which waited for: 5 -> 9; matrix products, arithmetic and copies ran while one was open for 8% -> 18% of each run, Pallas kernels for 0% -> 0%
where the time goes in v1:
time: 340 us; the launch traced here: 339 us
  waiting for transfers between devices  209 us (61%)
  matrix products  64.9 us (19%)
  starting transfers between devices  59.9 us (18%)
    ppermute x6, waiting for transfers between devices, swap_b(): return lax.ppermute(value, 'replica', B_PAIRS)  98.4 us
    all_to_all x4, waiting for transfers between devices, exchange(): lax.all_to_all(rows.reshape(num_experts, -1, width), 'expert', split_axis...  65.4 us
    dot_general x30, matrix products, dot(): lax.dot_general(lhs, rhs, (((ldim,), (rdim,)), ((), ())), preferred_eleme...  64.9 us
    ppermute x7, waiting for transfers between devices, swap_a(): return lax.ppermute(value, 'replica', A_PAIRS)  45.4 us
    all_to_all x4, starting transfers between devices, exchange(): lax.all_to_all(rows.reshape(num_experts, -1, width), 'expert', split_axis...  43.2 us
    ppermute x7, starting transfers between devices, swap_a(): return lax.ppermute(value, 'replica', A_PAIRS)  13.6 us
  transfers between devices with their start and end apart: 17, of which 9 were waited for; matrix products, arithmetic and copies ran while one was open for 18% of the time, Pallas kernels for 0%

profile of v1, /device:TPU:1, one launch (start us, length us, event | category | flops | bytes accessed | tf_op | source)
XLA Modules:
  0.0 339.0 jit_solution(15169833058589024707)
XLA Ops:
  1.6 2.8 fusion.7
  4.4 13.1 %all-to-all-start = ((bf16[64,8,1280]{2,1,0:T(8,128)(2,1)}), bf16[64,8,1280]{2,1,0:T(8,128)(2,1)}, u32[]{:S(2)}, u32[]{:S(2)}) async-start(bf16[64,8,1280]{2,1,0:T(8,128)(2,1)} %fusion.7), calls=%async_computation | async-start | bytes 2621440 | tf_op jit(solution)/shard_map/all_to_all | solution.py:32
  19.4 32.2 %all-to-all-done = bf16[64,8,1280]{2,1,0:T(8,128)(2,1)} async-done(((bf16[64,8,1280]{2,1,0:T(8,128)(2,1)}), bf16[64,8,1280]{2,1,0:T(8,128)(2,1)}, u32[]{:S(2)}, u32[]{:S(2)}) %all-to-all-start) | async-done | bytes 1310752 | tf_op jit(solution)/shard_map/all_to_all | solution.py:32
  51.6 6.3 %all-to-all-start.2 = ((bf16[64,8,1280]{2,1,0:T(8,128)(2,1)}), bf16[64,8,1280]{2,1,0:T(8,128)(2,1)}, u32[]{:S(2)}, u32[]{:S(2)}) async-start(bf16[64,8,1280]{2,1,0:T(8,128)(2,1)} %fusion.8), calls=%async_computation.2 | async-start | bytes 2621440 | tf_op jit(solution)/shard_map/all_to_all | solution.py:32
  58.1 2.8 collective-permute-start.2
  60.9 21.5 %collective-permute-done.2 = bf16[384,1280]{1,0:T(8,128)(2,1)S(1)} collective-permute-done((bf16[384,1280]{1,0:T(8,128)(2,1)S(1)}, bf16[384,1280]{1,0:T(8,128)(2,1)S(1)}, u32[]{:S(2)}, u32[]{:S(2)}) %collective-permute-start.2) | collective-permute-done | bytes 983072 | tf_op jit(solution)/shard_map/ppermute | solution.py:18
  88.0 16.6 %collective-permute-done.7 = bf16[384,1280]{1,0:T(8,128)(2,1)} collective-permute-done((bf16[384,1280]{1,0:T(8,128)(2,1)S(1)}, bf16[384,1280]{1,0:T(8,128)(2,1)}, u32[]{:S(2)}, u32[]{:S(2)}) %collective-permute-start.7) | collective-permute-done | bytes 983072 | tf_op jit(solution)/shard_map/ppermute | solution.py:14
  112.5 2.8 fusion.34
  119.7 6.0 %collective-permute-done.5 = bf16[384,1280]{1,0:T(8,128)(2,1)} collective-permute-done((bf16[384,1280]{1,0:T(8,128)(2,1)S(1)}, bf16[384,1280]{1,0:T(8,128)(2,1)}, u32[]{:S(2)}, u32[]{:S(2)}) %collective-permute-start.5) | collective-permute-done | bytes 983072 | tf_op jit(solution)/shard_map/ppermute | solution.py:14
  130.7 2.8 convolution_add_fusion.10
  133.5 2.8 multiply_convert_fusion.5
  136.6 31.3 %collective-permute-done.4 = bf16[2560,384]{1,0:T(8,128)(2,1)} collective-permute-done((bf16[2560,384]{1,0:T(8,128)(2,1)}, bf16[2560,384]{1,0:T(8,128)(2,1)}, u32[]{:S(2)}, u32[]{:S(2)}) %collective-permute-start.4) | collective-permute-done | bytes 1966112 | tf_op jit(solution)/shard_map/ppermute | solution.py:14
  170.6 39.3 %collective-permute-done.3 = bf16[2560,384]{1,0:T(8,128)(2,1)S(1)} collective-permute-done((bf16[2560,384]{1,0:T(8,128)(2,1)}, bf16[2560,384]{1,0:T(8,128)(2,1)S(1)}, u32[]{:S(2)}, u32[]{:S(2)}) %collective-permute-start.3) | collective-permute-done | bytes 1966112 | tf_op jit(solution)/shard_map/ppermute | solution.py:14
  209.9 2.9 fusion.52
  214.9 2.8 multiply_convert_fusion.4
  221.7 3.9 %fusion.36 = f32[512,1280]{1,0:T(8,128)} fusion(bf16[512,384]{1,0:T(8,128)(2,1)S(1)} %get-tuple-element.17, pred[]{:T(512)S(6)} %eq.73, bf16[1,2560,384]{2,1,0:T(8,128)(2,1)} %param.10), kind=kOutput, calls=%fused_computation.47 | convolution fusion | flops 503808000 | bytes 4980737 | tf_op jit(solution)/shard_map/dot_general | solution.py:22
  226.1 3.9 %fusion.54 = f32[512,1280]{1,0:T(8,128)} fusion(bf16[512,384]{1,0:T(8,128)(2,1)S(1)} %get-tuple-element.21, pred[]{:T(512)S(6)} %eq.73, bf16[2560,384]{1,0:T(8,128)(2,1)} %collective-permute-done.4), kind=kOutput, calls=%fused_computation.96 | convolution fusion | flops 503808000 | bytes 4980737 | tf_op jit(solution)/shard_map/dot_general | solution.py:22
  232.9 3.1 fusion.10
  236.0 12.5 %all-to-all-start.1 = ((bf16[64,8,1280]{2,1,0:T(8,128)(2,1)}), bf16[64,8,1280]{2,1,0:T(8,128)(2,1)S(1)}, u32[]{:S(2)}, u32[]{:S(2)}) async-start(bf16[64,8,1280]{2,1,0:T(8,128)(2,1)} %fusion.10), calls=%async_computation.1 | async-start | bytes 2621440 | tf_op jit(solution)/shard_map/all_to_all | solution.py:32
  248.5 3.4 convolution_add_fusion.1
  260.4 23.9 %collective-permute-done.11 = bf16[512,1280]{1,0:T(8,128)(2,1)S(1)} collective-permute-done((bf16[512,1280]{1,0:T(8,128)(2,1)S(1)}, bf16[512,1280]{1,0:T(8,128)(2,1)S(1)}, u32[]{:S(2)}, u32[]{:S(2)}) %collective-permute-start.11) | collective-permute-done | bytes 1310752 | tf_op jit(solution)/shard_map/ppermute | solution.py:18
  286.4 11.3 %all-to-all-start.3 = ((bf16[64,8,1280]{2,1,0:T(8,128)(2,1)}), bf16[64,8,1280]{2,1,0:T(8,128)(2,1)S(1)}, u32[]{:S(2)}, u32[]{:S(2)}) async-start(bf16[64,8,1280]{2,1,0:T(8,128)(2,1)} %fusion.9), calls=%async_computation.3 | async-start | bytes 2621440 | tf_op jit(solution)/shard_map/all_to_all | solution.py:32
  298.6 33.2 %all-to-all-done.3 = bf16[64,8,1280]{2,1,0:T(8,128)(2,1)S(1)} async-done(((bf16[64,8,1280]{2,1,0:T(8,128)(2,1)}), bf16[64,8,1280]{2,1,0:T(8,128)(2,1)S(1)}, u32[]{:S(2)}, u32[]{:S(2)}) %all-to-all-start.3) | async-done | bytes 1310752 | tf_op jit(solution)/shard_map/all_to_all | solution.py:32
  333.0 5.2 %collective-permute-done.12 = bf16[128,640]{1,0:T(8,128)(2,1)S(1)} collective-permute-done((bf16[128,640]{1,0:T(8,128)(2,1)S(1)}, bf16[128,640]{1,0:T(8,128)(2,1)S(1)}, u32[]{:S(2)}, u32[]{:S(2)}) %collective-permute-start.12) | collective-permute-done | bytes 163872 | tf_op jit(solution)/shard_map/ppermute | solution.py:14
  (66 shorter events, 51.6 us)
Async XLA Ops:
  1.6 16.1 %copy-start.6 = (bf16[128,2560]{1,0:T(8,128)(2,1)S(1)}, bf16[128,2560]{1,0:T(8,128)(2,1)}, u32[]{:S(2)}) copy-start(bf16[128,2560]{1,0:T(8,128)(2,1)} %param.13) | copy-start | bytes 1966084
  4.4 47.2 %all-to-all-start = ((bf16[64,8,1280]{2,1,0:T(8,128)(2,1)}), bf16[64,8,1280]{2,1,0:T(8,128)(2,1)}, u32[]{:S(2)}, u32[]{:S(2)}) async-start(bf16[64,8,1280]{2,1,0:T(8,128)(2,1)} %fusion.7), calls=%async_computation | async-start | bytes 2621440 | tf_op jit(solution)/shard_map/all_to_all | solution.py:32
  17.8 40.2 %copy-start.1 = (bf16[1,384,2560]{2,1,0:T(8,128)(2,1)S(1)}, bf16[1,384,2560]{2,1,0:T(8,128)(2,1)}, u32[]{:S(2)}) copy-start(bf16[1,384,2560]{2,1,0:T(8,128)(2,1)} %param.12) | copy-start | bytes 5898244
  51.6 53.0 %all-to-all-start.2 = ((bf16[64,8,1280]{2,1,0:T(8,128)(2,1)}), bf16[64,8,1280]{2,1,0:T(8,128)(2,1)}, u32[]{:S(2)}, u32[]{:S(2)}) async-start(bf16[64,8,1280]{2,1,0:T(8,128)(2,1)} %fusion.8), calls=%async_computation.2 | async-start | bytes 2621440 | tf_op jit(solution)/shard_map/all_to_all | solution.py:32
  58.1 24.3 %collective-permute-start.2 = (bf16[384,1280]{1,0:T(8,128)(2,1)S(1)}, bf16[384,1280]{1,0:T(8,128)(2,1)S(1)}, u32[]{:S(2)}, u32[]{:S(2)}) collective-permute-start(bf16[384,1280]{1,0:T(8,128)(2,1)S(1)} %get-tuple-element.18), channel_id=1, source_target_pairs={{0,3},{3,0},{1,2},{2,1},{4,7},{7,4},{5,6},{6,5},{8,11},{11,8},{9,1... | collective-permute-start | bytes 2949128 | tf_op jit(solution)/shard_map/ppermute | solution.py:18
  82.4 1.5 copy-start.4
  82.4 22.2 %collective-permute-start.7 = (bf16[384,1280]{1,0:T(8,128)(2,1)S(1)}, bf16[384,1280]{1,0:T(8,128)(2,1)}, u32[]{:S(2)}, u32[]{:S(2)}) collective-permute-start(bf16[384,1280]{1,0:T(8,128)(2,1)S(1)} %collective-permute-done.2), channel_id=1, source_target_pairs={{0,1},{1,0},{2,3},{3,2},{4,5},{5,4},{6,7},{7,6},{8,9},{9,8},{10,11... | collective-permute-start | bytes 2949128 | tf_op jit(solution)/shard_map/ppermute | solution.py:14
  82.4 43.3 %collective-permute-start.5 = (bf16[384,1280]{1,0:T(8,128)(2,1)S(1)}, bf16[384,1280]{1,0:T(8,128)(2,1)}, u32[]{:S(2)}, u32[]{:S(2)}) collective-permute-start(bf16[384,1280]{1,0:T(8,128)(2,1)S(1)} %get-tuple-element.19), channel_id=1, source_target_pairs={{0,1},{1,0},{2,3},{3,2},{4,5},{5,4},{6,7},{7,6},{8,9},{9,8},{10,11... | collective-permute-start | bytes 2949128 | tf_op jit(solution)/shard_map/ppermute | solution.py:14
  83.9 83.9 %collective-permute-start.4 = (bf16[2560,384]{1,0:T(8,128)(2,1)}, bf16[2560,384]{1,0:T(8,128)(2,1)}, u32[]{:S(2)}, u32[]{:S(2)}) collective-permute-start(bf16[2560,384]{1,0:T(8,128)(2,1)} %bitcast.11), channel_id=1, source_target_pairs={{0,1},{1,0},{2,3},{3,2},{4,5},{5,4},{6,7},{7,6},{8,9},{9,8},{10,11... | collective-permute-start | bytes 5898248 | tf_op jit(solution)/shard_map/ppermute | solution.py:14
  83.9 125.9 %collective-permute-start.3 = (bf16[2560,384]{1,0:T(8,128)(2,1)}, bf16[2560,384]{1,0:T(8,128)(2,1)S(1)}, u32[]{:S(2)}, u32[]{:S(2)}) collective-permute-start(bf16[2560,384]{1,0:T(8,128)(2,1)} %bitcast.10), channel_id=1, source_target_pairs={{0,1},{1,0},{2,3},{3,2},{4,5},{5,4},{6,7},{7,6},{8,9},{9,8},{10,11... | collective-permute-start | bytes 5898248 | tf_op jit(solution)/shard_map/ppermute | solution.py:14
  85.4 45.4 %collective-permute-start = (bf16[512,1280]{1,0:T(8,128)(2,1)}, bf16[512,1280]{1,0:T(8,128)(2,1)}, u32[]{:S(2)}, u32[]{:S(2)}) collective-permute-start(bf16[512,1280]{1,0:T(8,128)(2,1)} %bitcast.4), channel_id=1, source_target_pairs={{0,3},{3,0},{1,2},{2,1},{4,7},{7,4},{5,6},{6,5},{8,11},{11,8},{9,1... | collective-permute-start | bytes 3932168 | tf_op jit(solution)/shard_map/ppermute | solution.py:18
  107.1 21.2 %collective-permute-start.10 = (bf16[512,384]{1,0:T(8,128)(2,1)S(1)}, bf16[512,384]{1,0:T(8,128)(2,1)S(1)}, u32[]{:S(2)}, u32[]{:S(2)}) collective-permute-start(bf16[512,384]{1,0:T(8,128)(2,1)S(1)} %fusion.26), channel_id=1, source_target_pairs={{0,3},{3,0},{1,2},{2,1},{4,7},{7,4},{5,6},{6,5},{8,11},{11,8},{9,1... | collective-permute-start | bytes 1179656 | tf_op jit(solution)/shard_map/ppermute | solution.py:18
  112.5 2.8 copy-start.5
  125.7 95.6 %collective-permute-start.9 = (bf16[512,384]{1,0:T(8,128)(2,1)S(1)}, bf16[512,384]{1,0:T(8,128)(2,1)S(1)}, u32[]{:S(2)}, u32[]{:S(2)}) collective-permute-start(bf16[512,384]{1,0:T(8,128)(2,1)S(1)} %fusion.23), channel_id=1, source_target_pairs={{0,3},{3,0},{1,2},{2,1},{4,7},{7,4},{5,6},{6,5},{8,11},{11,8},{9,1... | collective-permute-start | bytes 1179656 | tf_op jit(solution)/shard_map/ppermute | solution.py:18
  136.4 93.6 %collective-permute-start.1 = (bf16[512,384]{1,0:T(8,128)(2,1)S(1)}, bf16[512,384]{1,0:T(8,128)(2,1)S(1)}, u32[]{:S(2)}, u32[]{:S(2)}) collective-permute-start(bf16[512,384]{1,0:T(8,128)(2,1)S(1)} %get-tuple-element.8), channel_id=1, source_target_pairs={{0,3},{3,0},{1,2},{2,1},{4,7},{7,4},{5,6},{6,5},{8,11},{11,8},{9,1... | collective-permute-start | bytes 1179656 | tf_op jit(solution)/shard_map/ppermute | solution.py:18
  209.9 2.9 copy-start.2
  217.8 15.1 %collective-permute-start.6 = (bf16[512,384]{1,0:T(8,128)(2,1)S(1)}, bf16[512,384]{1,0:T(8,128)(2,1)S(1)}, u32[]{:S(2)}, u32[]{:S(2)}) collective-permute-start(bf16[512,384]{1,0:T(8,128)(2,1)S(1)} %get-tuple-element.9), channel_id=1, source_target_pairs={{0,3},{3,0},{1,2},{2,1},{4,7},{7,4},{5,6},{6,5},{8,11},{11,8},{9,1... | collective-permute-start | bytes 1179656 | tf_op jit(solution)/shard_map/ppermute | solution.py:18
  236.0 50.4 %all-to-all-start.1 = ((bf16[64,8,1280]{2,1,0:T(8,128)(2,1)}), bf16[64,8,1280]{2,1,0:T(8,128)(2,1)S(1)}, u32[]{:S(2)}, u32[]{:S(2)}) async-start(bf16[64,8,1280]{2,1,0:T(8,128)(2,1)} %fusion.10), calls=%async_computation.1 | async-start | bytes 2621440 | tf_op jit(solution)/shard_map/all_to_all | solution.py:32
  248.5 3.4 %copy-start = (f32[512,1280]{1,0:T(8,128)S(1)}, f32[512,1280]{1,0:T(8,128)}, u32[]{:S(2)}) copy-start(f32[512,1280]{1,0:T(8,128)} %fusion.54) | copy-start | bytes 7864324
  248.5 3.7 %copy-start.3 = (bf16[2560,384]{1,0:T(8,128)(2,1)S(1)}, bf16[2560,384]{1,0:T(8,128)(2,1)}, u32[]{:S(2)}) copy-start(bf16[2560,384]{1,0:T(8,128)(2,1)} %copy-done.2) | copy-start | bytes 5898244
  253.1 31.2 %collective-permute-start.11 = (bf16[512,1280]{1,0:T(8,128)(2,1)S(1)}, bf16[512,1280]{1,0:T(8,128)(2,1)S(1)}, u32[]{:S(2)}, u32[]{:S(2)}) collective-permute-start(bf16[512,1280]{1,0:T(8,128)(2,1)S(1)} %fusion.3), channel_id=1, source_target_pairs={{0,3},{3,0},{1,2},{2,1},{4,7},{7,4},{5,6},{6,5},{8,11},{11,8},{9,1... | collective-permute-start | bytes 3932168 | tf_op jit(solution)/shard_map/ppermute | solution.py:18
  286.4 45.4 %all-to-all-start.3 = ((bf16[64,8,1280]{2,1,0:T(8,128)(2,1)}), bf16[64,8,1280]{2,1,0:T(8,128)(2,1)S(1)}, u32[]{:S(2)}, u32[]{:S(2)}) async-start(bf16[64,8,1280]{2,1,0:T(8,128)(2,1)} %fusion.9), calls=%async_computation.3 | async-start | bytes 2621440 | tf_op jit(solution)/shard_map/all_to_all | solution.py:32
  298.5 33.8 %collective-permute-start.8 = (bf16[128,640]{1,0:T(8,128)(2,1)S(1)}, bf16[128,640]{1,0:T(8,128)(2,1)S(1)}, u32[]{:S(2)}, u32[]{:S(2)}) collective-permute-start(bf16[128,640]{1,0:T(8,128)(2,1)S(1)} %select_convert_fusion.2), channel_id=1, source_target_pairs={{0,1},{1,0},{2,3},{3,2},{4,5},{5,4},{6,7},{7,6},{8,9},{9,8},{10,11... | collective-permute-start | bytes 491528 | tf_op jit(solution)/shard_map/ppermute | solution.py:14
  332.2 6.0 %collective-permute-start.12 = (bf16[128,640]{1,0:T(8,128)(2,1)S(1)}, bf16[128,640]{1,0:T(8,128)(2,1)S(1)}, u32[]{:S(2)}, u32[]{:S(2)}) collective-permute-start(bf16[128,640]{1,0:T(8,128)(2,1)S(1)} %select_convert_fusion.1), channel_id=1, source_target_pairs={{0,1},{1,0},{2,3},{3,2},{4,5},{5,4},{6,7},{7,6},{8,9},{9,8},{10,11... | collective-permute-start | bytes 491528 | tf_op jit(solution)/shard_map/ppermute | solution.py:14

commit v2 on v1

--- a/solution.py
+++ b/solution.py
@@ -49,8 +49,10 @@
     up_b = swap_b(up_w)
     down_own, down_far = halves(down_w, 1, a)
     down_a = swap_a(down_far)
-    down_b = swap_b(down_own)
     down_ab = swap_b(down_a)
+    cut = down_own.shape[0] * 2 // 3
+    down_b1 = swap_b(down_own[:cut])
+    down_b2 = swap_b(down_own[cut:])
 
     experts = jnp.arange(num_experts, dtype=jnp.int32)
     hit = expert_ids.T[None, :, :] == experts[:, None, None]
@@ -91,6 +93,9 @@
         gate_grad = (hidden_grad * up * sig * (1.0 + gate * (1.0 - sig))).astype(BF)
         return gate_grad, (hidden_grad * act).astype(BF)
 
+    late_n = lax.optimization_barrier(jnp.concatenate([gate_2n[:, cut:], up_2n[:, cut:]], axis=1))
+    late_f = lax.optimization_barrier(jnp.concatenate([gate_2f[:, cut:], up_2f[:, cut:]], axis=1))
+
     gate_1, up_1, hidden_1 = forward(gate_1n, gate_1f, up_1n, up_1f)
     gate_2, up_2, hidden_2 = forward(gate_2n, gate_2f, up_2n, up_2f)
     hidden_3 = swap_a(hidden_1)
@@ -101,19 +106,27 @@
     hgrad_4 = swap_a(hgrad_4)
 
     mixed_rows = dot(hidden_1, down_own) + dot(hidden_3, down_a)
-    mixed_rows = mixed_rows + dot(hidden_2, down_b) + dot(hidden_4, down_ab)
+    mixed_rows = mixed_rows + dot(hidden_2[:, :cut], down_b1) + dot(hidden_4, down_ab)
+    mixed_rows = lax.optimization_barrier(mixed_rows)
+    mixed_rows = mixed_rows + dot(hidden_2[:, cut:], down_b2)
     mixed_back = exchange(mixed_rows.astype(BF), num_experts)
 
     hgrad_1 = dot(grad_rows, down_own, 1, 1)
-    hgrad_2 = dot(grad_rows, down_b, 1, 1)
     gg_1, ug_1 = backward(hgrad_1 + hgrad_3.astype(F32), gate_1, up_1)
-    gg_2, ug_2 = backward(hgrad_2 + hgrad_4.astype(F32), gate_2, up_2)
+    hgrad_2 = dot(grad_rows, down_b1, 1, 1)
+    gg_2, ug_2 = backward(hgrad_2 + hgrad_4[:, :cut].astype(F32), gate_2[:, :cut], up_2[:, :cut])
+    hgrad_2 = dot(grad_rows, down_b2, 1, 1)
+    late = backward(hgrad_2 + hgrad_4[:, cut:].astype(F32), gate_2[:, cut:], up_2[:, cut:])
+    grads_3 = jnp.concatenate(late, axis=1)
     far = dot(gg_1, gate_1f, 1, 1) + dot(ug_1, up_1f, 1, 1)
-    far = far + dot(gg_2, gate_2f, 1, 1) + dot(ug_2, up_2f, 1, 1)
-    far = far.astype(BF)
+    far = far + dot(gg_2, gate_2f[:, :cut], 1, 1) + dot(ug_2, up_2f[:, :cut], 1, 1)
+    far = lax.optimization_barrier(far)
+    far = (far + dot(grads_3, late_f, 1, 1)).astype(BF)
     far = swap_a(far)
     near = dot(gg_1, gate_1n, 1, 1) + dot(ug_1, up_1n, 1, 1)
-    near = near + dot(gg_2, gate_2n, 1, 1) + dot(ug_2, up_2n, 1, 1)
+    near = near + dot(gg_2, gate_2n[:, :cut], 1, 1) + dot(ug_2, up_2n[:, :cut], 1, 1)
+    near = lax.optimization_barrier(near)
+    near = near + dot(grads_3, late_n, 1, 1)
     near = near + far.astype(F32)
     grad_back = exchange(near.astype(BF), num_experts)
 
@@ -137,6 +150,4 @@
         P("expert", None),
     )
     out_specs = (P("expert", "replica"), P("expert", "replica"))
-    return jax.shard_map(
-        layer, mesh=mesh, in_specs=in_specs, out_specs=out_specs, check_vma=False
-    )
+    return jax.shard_map(layer, mesh=mesh, in_specs=in_specs, out_specs=out_specs, check_vma=False)

time: 340 us -> 298 us (0.88)
  waiting for transfers between devices: 209 us -> 163 us
  other arithmetic: 3.38 us -> 10.5 us
  matrix products: 64.9 us -> 58.7 us
    ppermute x6 -> x7, waiting for transfers between devices: 98.4 us -> 78.2 us  [swap_b(): return lax.ppermute(value, 'replica', B_PAIRS)]
    ppermute x7, waiting for transfers between devices: 45.4 us -> 26.2 us  [swap_a(): return lax.ppermute(value, 'replica', A_PAIRS)]
    all_to_all x4, waiting for transfers between devices: 65.4 us -> 58.9 us  [exchange(): lax.all_to_all(rows.reshape(num_experts, -1, width), 'expert', split_axis...]
    dot_general x30 -> x34, matrix products: 64.9 us -> 58.7 us  [dot(): lax.dot_general(lhs, rhs, (((ldim,), (rdim,)), ((), ())), preferred_eleme...]
    select_n x1 -> x3, other arithmetic: 0.13 us -> 4.54 us  [halves(): return (jnp.where(first == 0, low, high), jnp.where(first == 0, high, low))]
  transfers between devices with their start and end apart: 17 -> 18, of which waited for: 9 -> 6; matrix products, arithmetic and copies ran while one was open for 18% -> 21% of each run, Pallas kernels for 0% -> 0%
where the time goes in v2:
time: 298 us; the launch traced here: 297 us
  waiting for transfers between devices  163 us (55%)
  starting transfers between devices  59.3 us (20%)
  matrix products  58.7 us (20%)
  other arithmetic  10.5 us (4%)
  local copies, waits for them, and re-layouts  3.92 us (1%)
    ppermute x7, waiting for transfers between devices, swap_b(): return lax.ppermute(value, 'replica', B_PAIRS)  78.2 us
    all_to_all x4, waiting for transfers between devices, exchange(): lax.all_to_all(rows.reshape(num_experts, -1, width), 'expert', split_axis...  58.9 us
    dot_general x34, matrix products, dot(): lax.dot_general(lhs, rhs, (((ldim,), (rdim,)), ((), ())), preferred_eleme...  58.7 us
    all_to_all x4, starting transfers between devices, exchange(): lax.all_to_all(rows.reshape(num_experts, -1, width), 'expert', split_axis...  43.1 us
    ppermute x7, waiting for transfers between devices, swap_a(): return lax.ppermute(value, 'replica', A_PAIRS)  26.2 us
    ppermute x7, starting transfers between devices, swap_a(): return lax.ppermute(value, 'replica', A_PAIRS)  11.7 us
  transfers between devices with their start and end apart: 18, of which 6 were waited for; matrix products, arithmetic and copies ran while one was open for 21% of the time, Pallas kernels for 0%

profile of v2, /device:TPU:1, one launch (start us, length us, event | category | flops | bytes accessed | tf_op | source)
XLA Modules:
  0.0 297.0 jit_solution(2943935221360323967)
XLA Ops:
  1.6 2.9 fusion.4
  4.5 13.1 %all-to-all-start = ((bf16[64,8,1280]{2,1,0:T(8,128)(2,1)}), bf16[64,8,1280]{2,1,0:T(8,128)(2,1)}, u32[]{:S(2)}, u32[]{:S(2)}) async-start(bf16[64,8,1280]{2,1,0:T(8,128)(2,1)} %fusion.4), calls=%async_computation | async-start | bytes 2621440 | tf_op jit(solution)/shard_map/all_to_all | solution.py:32
  20.4 2.7 collective-permute-start.2
  23.4 2.7 fusion.5
  26.1 25.7 %all-to-all-done = bf16[64,8,1280]{2,1,0:T(8,128)(2,1)} async-done(((bf16[64,8,1280]{2,1,0:T(8,128)(2,1)}), bf16[64,8,1280]{2,1,0:T(8,128)(2,1)}, u32[]{:S(2)}, u32[]{:S(2)}) %all-to-all-start) | async-done | bytes 1310752 | tf_op jit(solution)/shard_map/all_to_all | solution.py:32
  51.8 6.3 %all-to-all-start.2 = ((bf16[64,8,1280]{2,1,0:T(8,128)(2,1)}), bf16[64,8,1280]{2,1,0:T(8,128)(2,1)}, u32[]{:S(2)}, u32[]{:S(2)}) async-start(bf16[64,8,1280]{2,1,0:T(8,128)(2,1)} %fusion.5), calls=%async_computation.2 | async-start | bytes 2621440 | tf_op jit(solution)/shard_map/all_to_all | solution.py:32
  64.2 39.8 %collective-permute-done.3 = bf16[2560,384]{1,0:T(8,128)(2,1)} collective-permute-done((bf16[2560,384]{1,0:T(8,128)(2,1)}, bf16[2560,384]{1,0:T(8,128)(2,1)}, u32[]{:S(2)}, u32[]{:S(2)}) %collective-permute-start.3) | collective-permute-done | bytes 1966112 | tf_op jit(solution)/shard_map/ppermute | solution.py:14
  107.7 2.7 collective-permute-start
  110.5 2.4 fusion.19
  113.0 33.2 %collective-permute-done.7 = bf16[384,1280]{1,0:T(8,128)(2,1)} collective-permute-done((bf16[384,1280]{1,0:T(8,128)(2,1)}, bf16[384,1280]{1,0:T(8,128)(2,1)}, u32[]{:S(2)}, u32[]{:S(2)}) %collective-permute-start.7) | collective-permute-done | bytes 983072 | tf_op jit(solution)/shard_map/ppermute | solution.py:14
  146.2 2.4 fusion.22
  148.7 3.0 %collective-permute-start.11 = (bf16[512,384]{1,0:T(8,128)(2,1)S(1)}, bf16[512,384]{1,0:T(8,128)(2,1)S(1)}, u32[]{:S(2)}, u32[]{:S(2)}) collective-permute-start(bf16[512,384]{1,0:T(8,128)(2,1)S(1)} %fusion.22), channel_id=1, source_target_pairs={{0,3},{3,0},{1,2},{2,1},{4,7},{7,4},{5,6},{6,5},{8,11},{11,8},{9,1... | collective-permute-start | bytes 1179656 | tf_op jit(solution)/shard_map/ppermute | solution.py:18
  160.4 2.3 multiply_convert_fusion.3
  167.4 2.5 fusion.86
  169.9 2.3 multiply_convert_fusion.2
  172.2 2.8 collective-permute-start.6
  176.3 3.0 %multiply_convert_fusion.5 = (bf16[512,256]{1,0:T(8,128)(2,1)}, bf16[512,256]{1,0:T(8,128)(2,1)S(1)}) fusion(f32[512,384]{1,0:T(8,128)S(1)} %get-tuple-element.12, f32[512,384]{1,0:T(8,128)S(1)} %convolution_add_fusion.10, bf16[512,384]{1,0:T(8,128)(2,1)S(1)} %collective-permute-done.11, bf16[256,1280]{1,0:T(8,128)(2,1)} %collective-permute-done.5, ...), kind=kOutput, calls=%fused_computation.83 | convolution fusion | flops 337510400 | bytes 3801088 | tf_op jit(solution)/shard_map/dot_general | solution.py:22
  183.7 2.4 convolution_add_fusion.2
  193.3 12.2 %all-to-all-start.1 = ((bf16[64,8,1280]{2,1,0:T(8,128)(2,1)}), bf16[64,8,1280]{2,1,0:T(8,128)(2,1)S(1)}, u32[]{:S(2)}, u32[]{:S(2)}) async-start(bf16[64,8,1280]{2,1,0:T(8,128)(2,1)} %fusion.7), calls=%async_computation.1 | async-start | bytes 2621440 | tf_op jit(solution)/shard_map/all_to_all | solution.py:32
  205.4 3.2 %fusion = f32[512,1280]{1,0:T(8,128)S(1)} fusion(f32[512,1280]{1,0:T(8,128)} %fusion.45, f32[512,1280]{1,0:T(8,128)} %convolution_add_fusion.2, bf16[512,256]{1,0:T(8,128)(2,1)} %get-tuple-element.24, bf16[1280,384]{1,0:T(8,128)(2,1)S(1)} %get-tuple-element.21), kind=kOutput, calls=%fused_computation.2 | convolution fusion | flops 336855040 | bytes 8781824 | tf_op jit(solution)/shard_map/dot_general | solution.py:22
  216.4 26.2 %collective-permute-done.12 = bf16[512,1280]{1,0:T(8,128)(2,1)S(1)} collective-permute-done((bf16[512,1280]{1,0:T(8,128)(2,1)S(1)}, bf16[512,1280]{1,0:T(8,128)(2,1)S(1)}, u32[]{:S(2)}, u32[]{:S(2)}) %collective-permute-start.12) | collective-permute-done | bytes 1310752 | tf_op jit(solution)/shard_map/ppermute | solution.py:18
  244.2 11.5 %all-to-all-start.3 = ((bf16[64,8,1280]{2,1,0:T(8,128)(2,1)}), bf16[64,8,1280]{2,1,0:T(8,128)(2,1)S(1)}, u32[]{:S(2)}, u32[]{:S(2)}) async-start(bf16[64,8,1280]{2,1,0:T(8,128)(2,1)} %fusion.8), calls=%async_computation.3 | async-start | bytes 2621440 | tf_op jit(solution)/shard_map/all_to_all | solution.py:32
  256.6 33.2 %all-to-all-done.3 = bf16[64,8,1280]{2,1,0:T(8,128)(2,1)S(1)} async-done(((bf16[64,8,1280]{2,1,0:T(8,128)(2,1)}), bf16[64,8,1280]{2,1,0:T(8,128)(2,1)S(1)}, u32[]{:S(2)}, u32[]{:S(2)}) %all-to-all-start.3) | async-done | bytes 1310752 | tf_op jit(solution)/shard_map/all_to_all | solution.py:32
  291.1 5.2 %collective-permute-done.13 = bf16[128,640]{1,0:T(8,128)(2,1)S(1)} collective-permute-done((bf16[128,640]{1,0:T(8,128)(2,1)S(1)}, bf16[128,640]{1,0:T(8,128)(2,1)S(1)}, u32[]{:S(2)}, u32[]{:S(2)}) %collective-permute-start.13) | collective-permute-done | bytes 163872 | tf_op jit(solution)/shard_map/ppermute | solution.py:14
  (112 shorter events, 52.1 us)
Async XLA Ops:
  1.6 17.6 %copy-start.11 = (bf16[1,384,2560]{2,1,0:T(8,128)(2,1)S(1)}, bf16[1,384,2560]{2,1,0:T(8,128)(2,1)}, u32[]{:S(2)}) copy-start(bf16[1,384,2560]{2,1,0:T(8,128)(2,1)} %param.12) | copy-start | bytes 5898244
  4.5 47.2 %all-to-all-start = ((bf16[64,8,1280]{2,1,0:T(8,128)(2,1)}), bf16[64,8,1280]{2,1,0:T(8,128)(2,1)}, u32[]{:S(2)}, u32[]{:S(2)}) async-start(bf16[64,8,1280]{2,1,0:T(8,128)(2,1)} %fusion.4), calls=%async_computation | async-start | bytes 2621440 | tf_op jit(solution)/shard_map/all_to_all | solution.py:32
  17.7 44.8 %collective-permute-start.4 = (bf16[2560,384]{1,0:T(8,128)(2,1)}, bf16[2560,384]{1,0:T(8,128)(2,1)}, u32[]{:S(2)}, u32[]{:S(2)}) collective-permute-start(bf16[2560,384]{1,0:T(8,128)(2,1)} %bitcast.116), channel_id=1, source_target_pairs={{0,1},{1,0},{2,3},{3,2},{4,5},{5,4},{6,7},{7,6},{8,9},{9,8},{10,11... | collective-permute-start | bytes 5898248 | tf_op jit(solution)/shard_map/ppermute | solution.py:14
  19.1 85.0 %collective-permute-start.3 = (bf16[2560,384]{1,0:T(8,128)(2,1)}, bf16[2560,384]{1,0:T(8,128)(2,1)}, u32[]{:S(2)}, u32[]{:S(2)}) collective-permute-start(bf16[2560,384]{1,0:T(8,128)(2,1)} %bitcast.117), channel_id=1, source_target_pairs={{0,1},{1,0},{2,3},{3,2},{4,5},{5,4},{6,7},{7,6},{8,9},{9,8},{10,11... | collective-permute-start | bytes 5898248 | tf_op jit(solution)/shard_map/ppermute | solution.py:14
  20.4 40.8 %collective-permute-start.2 = (bf16[384,1280]{1,0:T(8,128)(2,1)}, bf16[384,1280]{1,0:T(8,128)(2,1)}, u32[]{:S(2)}, u32[]{:S(2)}) collective-permute-start(bf16[384,1280]{1,0:T(8,128)(2,1)} %get-tuple-element.22), channel_id=1, source_target_pairs={{0,3},{3,0},{1,2},{2,1},{4,7},{7,4},{5,6},{6,5},{8,11},{11,8},{9,1... | collective-permute-start | bytes 2949128 | tf_op jit(solution)/shard_map/ppermute | solution.py:18
  51.8 58.7 %all-to-all-start.2 = ((bf16[64,8,1280]{2,1,0:T(8,128)(2,1)}), bf16[64,8,1280]{2,1,0:T(8,128)(2,1)}, u32[]{:S(2)}, u32[]{:S(2)}) async-start(bf16[64,8,1280]{2,1,0:T(8,128)(2,1)} %fusion.5), calls=%async_computation.2 | async-start | bytes 2621440 | tf_op jit(solution)/shard_map/all_to_all | solution.py:32
  58.8 123.4 %collective-permute-start.8 = (bf16[128,1280]{1,0:T(8,128)(2,1)}, bf16[128,1280]{1,0:T(8,128)(2,1)}, u32[]{:S(2)}, u32[]{:S(2)}) collective-permute-start(bf16[128,1280]{1,0:T(8,128)(2,1)} %slice.77), channel_id=1, source_target_pairs={{0,1},{1,0},{2,3},{3,2},{4,5},{5,4},{6,7},{7,6},{8,9},{9,8},{10,11... | collective-permute-start | bytes 983048 | tf_op jit(solution)/shard_map/ppermute | solution.py:14
  61.0 115.2 %collective-permute-start.5 = (bf16[256,1280]{1,0:T(8,128)(2,1)}, bf16[256,1280]{1,0:T(8,128)(2,1)}, u32[]{:S(2)}, u32[]{:S(2)}) collective-permute-start(bf16[256,1280]{1,0:T(8,128)(2,1)} %slice.76), channel_id=1, source_target_pairs={{0,1},{1,0},{2,3},{3,2},{4,5},{5,4},{6,7},{7,6},{8,9},{9,8},{10,11... | collective-permute-start | bytes 1966088 | tf_op jit(solution)/shard_map/ppermute | solution.py:14
  61.2 85.0 %collective-permute-start.7 = (bf16[384,1280]{1,0:T(8,128)(2,1)}, bf16[384,1280]{1,0:T(8,128)(2,1)}, u32[]{:S(2)}, u32[]{:S(2)}) collective-permute-start(bf16[384,1280]{1,0:T(8,128)(2,1)} %collective-permute-done.2), channel_id=1, source_target_pairs={{0,1},{1,0},{2,3},{3,2},{4,5},{5,4},{6,7},{7,6},{8,9},{9,8},{10,11... | collective-permute-start | bytes 2949128 | tf_op jit(solution)/shard_map/ppermute | solution.py:14
  64.2 41.6 %copy-start = (bf16[1280,384]{1,0:T(8,128)(2,1)}, bf16[1280,384]{1,0:T(8,128)(2,1)S(1)}, u32[]{:S(2)}) copy-start(bf16[1280,384]{1,0:T(8,128)(2,1)S(1)} %get-tuple-element.18) | copy-start | bytes 2949124
  64.2 41.6 %copy-start.3 = (bf16[1280,384]{1,0:T(8,128)(2,1)}, bf16[1280,384]{1,0:T(8,128)(2,1)S(1)}, u32[]{:S(2)}) copy-start(bf16[1280,384]{1,0:T(8,128)(2,1)S(1)} %get-tuple-element.19) | copy-start | bytes 2949124
  107.7 50.5 %collective-permute-start = (bf16[512,1280]{1,0:T(8,128)(2,1)}, bf16[512,1280]{1,0:T(8,128)(2,1)}, u32[]{:S(2)}, u32[]{:S(2)}) collective-permute-start(bf16[512,1280]{1,0:T(8,128)(2,1)} %bitcast.4), channel_id=1, source_target_pairs={{0,3},{3,0},{1,2},{2,1},{4,7},{7,4},{5,6},{6,5},{8,11},{11,8},{9,1... | collective-permute-start | bytes 3932168 | tf_op jit(solution)/shard_map/ppermute | solution.py:18
  112.9 38.7 %copy-start.14 = (bf16[1,2560,384]{2,1,0:T(8,128)(2,1)S(1)}, bf16[1,2560,384]{2,1,0:T(8,128)(2,1)}, u32[]{:S(2)}) copy-start(bf16[1,2560,384]{2,1,0:T(8,128)(2,1)} %param.10) | copy-start | bytes 5898244
  112.9 59.2 %collective-permute-start.10 = (bf16[512,384]{1,0:T(8,128)(2,1)S(1)}, bf16[512,384]{1,0:T(8,128)(2,1)S(1)}, u32[]{:S(2)}, u32[]{:S(2)}) collective-permute-start(bf16[512,384]{1,0:T(8,128)(2,1)S(1)} %fusion.19), channel_id=1, source_target_pairs={{0,3},{3,0},{1,2},{2,1},{4,7},{7,4},{5,6},{6,5},{8,11},{11,8},{9,1... | collective-permute-start | bytes 1179656 | tf_op jit(solution)/shard_map/ppermute | solution.py:18
  148.7 27.6 %collective-permute-start.11 = (bf16[512,384]{1,0:T(8,128)(2,1)S(1)}, bf16[512,384]{1,0:T(8,128)(2,1)S(1)}, u32[]{:S(2)}, u32[]{:S(2)}) collective-permute-start(bf16[512,384]{1,0:T(8,128)(2,1)S(1)} %fusion.22), channel_id=1, source_target_pairs={{0,3},{3,0},{1,2},{2,1},{4,7},{7,4},{5,6},{6,5},{8,11},{11,8},{9,1... | collective-permute-start | bytes 1179656 | tf_op jit(solution)/shard_map/ppermute | solution.py:18
  162.7 23.4 %collective-permute-start.1 = (bf16[512,384]{1,0:T(8,128)(2,1)S(1)}, bf16[512,384]{1,0:T(8,128)(2,1)S(1)}, u32[]{:S(2)}, u32[]{:S(2)}) collective-permute-start(bf16[512,384]{1,0:T(8,128)(2,1)S(1)} %get-tuple-element.8), channel_id=1, source_target_pairs={{0,3},{3,0},{1,2},{2,1},{4,7},{7,4},{5,6},{6,5},{8,11},{11,8},{9,1... | collective-permute-start | bytes 1179656 | tf_op jit(solution)/shard_map/ppermute | solution.py:18
  167.4 8.9 %copy-start.19 = (f32[512,384]{1,0:T(8,128)}, f32[512,384]{1,0:T(8,128)S(1)}, u32[]{:S(2)}) copy-start(f32[512,384]{1,0:T(8,128)S(1)} %convolution_add_fusion.10) | copy-start | bytes 2359300
  172.2 17.7 %collective-permute-start.6 = (bf16[512,384]{1,0:T(8,128)(2,1)S(1)}, bf16[512,384]{1,0:T(8,128)(2,1)S(1)}, u32[]{:S(2)}, u32[]{:S(2)}) collective-permute-start(bf16[512,384]{1,0:T(8,128)(2,1)S(1)} %get-tuple-element.9), channel_id=1, source_target_pairs={{0,3},{3,0},{1,2},{2,1},{4,7},{7,4},{5,6},{6,5},{8,11},{11,8},{9,1... | collective-permute-start | bytes 1179656 | tf_op jit(solution)/shard_map/ppermute | solution.py:18
  193.3 51.0 %all-to-all-start.1 = ((bf16[64,8,1280]{2,1,0:T(8,128)(2,1)}), bf16[64,8,1280]{2,1,0:T(8,128)(2,1)S(1)}, u32[]{:S(2)}, u32[]{:S(2)}) async-start(bf16[64,8,1280]{2,1,0:T(8,128)(2,1)} %fusion.7), calls=%async_computation.1 | async-start | bytes 2621440 | tf_op jit(solution)/shard_map/all_to_all | solution.py:32
  211.4 31.2 %collective-permute-start.12 = (bf16[512,1280]{1,0:T(8,128)(2,1)S(1)}, bf16[512,1280]{1,0:T(8,128)(2,1)S(1)}, u32[]{:S(2)}, u32[]{:S(2)}) collective-permute-start(bf16[512,1280]{1,0:T(8,128)(2,1)S(1)} %fusion.3), channel_id=1, source_target_pairs={{0,3},{3,0},{1,2},{2,1},{4,7},{7,4},{5,6},{6,5},{8,11},{11,8},{9,1... | collective-permute-start | bytes 3932168 | tf_op jit(solution)/shard_map/ppermute | solution.py:18
  215.7 26.8 %copy-start.9 = (bf16[1280,256]{1,0:T(8,128)(2,1)S(1)}, bf16[1280,256]{1,0:T(8,128)(2,1)}, u32[]{:S(2)}) copy-start(bf16[1280,256]{1,0:T(8,128)(2,1)} %pad_maximum_fusion) | copy-start | bytes 1966084
  244.2 45.6 %all-to-all-start.3 = ((bf16[64,8,1280]{2,1,0:T(8,128)(2,1)}), bf16[64,8,1280]{2,1,0:T(8,128)(2,1)S(1)}, u32[]{:S(2)}, u32[]{:S(2)}) async-start(bf16[64,8,1280]{2,1,0:T(8,128)(2,1)} %fusion.8), calls=%async_computation.3 | async-start | bytes 2621440 | tf_op jit(solution)/shard_map/all_to_all | solution.py:32
  256.5 33.8 %collective-permute-start.9 = (bf16[128,640]{1,0:T(8,128)(2,1)S(1)}, bf16[128,640]{1,0:T(8,128)(2,1)S(1)}, u32[]{:S(2)}, u32[]{:S(2)}) collective-permute-start(bf16[128,640]{1,0:T(8,128)(2,1)S(1)} %select_convert_fusion.2), channel_id=1, source_target_pairs={{0,1},{1,0},{2,3},{3,2},{4,5},{5,4},{6,7},{7,6},{8,9},{9,8},{10,11... | collective-permute-start | bytes 491528 | tf_op jit(solution)/shard_map/ppermute | solution.py:14
  290.3 6.0 %collective-permute-start.13 = (bf16[128,640]{1,0:T(8,128)(2,1)S(1)}, bf16[128,640]{1,0:T(8,128)(2,1)S(1)}, u32[]{:S(2)}, u32[]{:S(2)}) collective-permute-start(bf16[128,640]{1,0:T(8,128)(2,1)S(1)} %select_convert_fusion.1), channel_id=1, source_target_pairs={{0,1},{1,0},{2,3},{3,2},{4,5},{5,4},{6,7},{7,6},{8,9},{9,8},{10,11... | collective-permute-start | bytes 491528 | tf_op jit(solution)/shard_map/ppermute | solution.py:14
  (16 other events, 44.5 us)

commit v3 on v1

--- a/solution.py
+++ b/solution.py
@@ -1,6 +1,8 @@
 import jax
 import jax.numpy as jnp
 from jax import lax
+from jax.experimental import pallas as pl
+from jax.experimental.pallas import tpu as pltpu
 from jax.sharding import PartitionSpec as P
 
 
@@ -33,6 +35,192 @@
         rows.reshape(num_experts, -1, width), "expert", split_axis=0, concat_axis=0, tiled=True
     )
     return moved.reshape(-1, width)
+
+
+def near_first(j, a):
+    return jnp.where(j < 2, 2 * a + j, 2 * (1 - a) + j - 2)
+
+
+def act_hidden(gate, up):
+    return (gate * jax.nn.sigmoid(gate) * up).astype(BF)
+
+
+def forward_near(a, near, gate_w, up_w):
+    rows, half = near.shape
+    hidden_units = gate_w.shape[1]
+    step = half // 2
+
+    def kernel(a_ref, near_ref, gate_w_ref, up_w_ref, gate_ref, up_ref):
+        gate = dot(near_ref[...], gate_w_ref[...])
+        up = dot(near_ref[...], up_w_ref[...])
+
+        @pl.when(pl.program_id(0) == 0)
+        def _():
+            gate_ref[...] = gate
+            up_ref[...] = up
+
+        @pl.when(pl.program_id(0) == 1)
+        def _():
+            gate_ref[...] += gate
+            up_ref[...] += up
+
+    whole = pl.BlockSpec((rows, hidden_units), lambda j, a_ref: (0, 0))
+    weight = pl.BlockSpec((step, hidden_units), lambda j, a_ref: (near_first(j, a_ref[0]), 0))
+    return pl.pallas_call(
+        kernel,
+        grid_spec=pltpu.PrefetchScalarGridSpec(
+            num_scalar_prefetch=1,
+            grid=(2,),
+            in_specs=[pl.BlockSpec((rows, step), lambda j, a_ref: (0, j)), weight, weight],
+            out_specs=[whole, whole],
+        ),
+        out_shape=[jax.ShapeDtypeStruct((rows, hidden_units), F32)] * 2,
+        name="forward_near",
+    )(a, near, gate_w, up_w)
+
+
+def forward_far(a, far, gate_near, up_near, gate_w, up_w):
+    rows, half = far.shape
+    hidden_units = gate_w.shape[1]
+    step = half // 2
+
+    def kernel(a_ref, far_ref, gn_ref, un_ref, gate_w_ref, up_w_ref, gate_ref, up_ref, hidden_ref):
+        @pl.when(pl.program_id(0) == 0)
+        def _():
+            gate_ref[...] = gn_ref[...] + dot(far_ref[...], gate_w_ref[...])
+            up_ref[...] = un_ref[...] + dot(far_ref[...], up_w_ref[...])
+
+        @pl.when(pl.program_id(0) == 1)
+        def _():
+            gate = gate_ref[...] + dot(far_ref[...], gate_w_ref[...])
+            up = up_ref[...] + dot(far_ref[...], up_w_ref[...])
+            gate_ref[...] = gate
+            up_ref[...] = up
+            hidden_ref[...] = act_hidden(gate, up)
+
+    whole = pl.BlockSpec((rows, hidden_units), lambda j, a_ref: (0, 0))
+    weight = pl.BlockSpec((step, hidden_units), lambda j, a_ref: (2 * (1 - a_ref[0]) + j, 0))
+    wide = jax.ShapeDtypeStruct((rows, hidden_units), F32)
+    return pl.pallas_call(
+        kernel,
+        grid_spec=pltpu.PrefetchScalarGridSpec(
+            num_scalar_prefetch=1,
+            grid=(2,),
+            in_specs=[
+                pl.BlockSpec((rows, step), lambda j, a_ref: (0, j)),
+                whole,
+                whole,
+                weight,
+                weight,
+            ],
+            out_specs=[whole, whole, whole],
+        ),
+        out_shape=[wide, wide, jax.ShapeDtypeStruct((rows, hidden_units), BF)],
+        name="forward_far",
+    )(a, far, gate_near, up_near, gate_w, up_w)
+
+
+def forward(a, near, far, gate_w, up_w):
+    rows, half = near.shape
+    hidden_units = gate_w.shape[1]
+    step = half // 2
+
+    def kernel(a_ref, near_ref, far_ref, gate_w_ref, up_w_ref, gate_ref, up_ref, hidden_ref):
+        j = pl.program_id(0)
+
+        @pl.when(j == 0)
+        def _():
+            gate_ref[...] = dot(near_ref[...], gate_w_ref[...])
+            up_ref[...] = dot(near_ref[...], up_w_ref[...])
+
+        @pl.when(j == 1)
+        def _():
+            gate_ref[...] += dot(near_ref[...], gate_w_ref[...])
+            up_ref[...] += dot(near_ref[...], up_w_ref[...])
+
+        @pl.when(j == 2)
+        def _():
+            gate_ref[...] += dot(far_ref[...], gate_w_ref[...])
+            up_ref[...] += dot(far_ref[...], up_w_ref[...])
+
+        @pl.when(j == 3)
+        def _():
+            gate = gate_ref[...] + dot(far_ref[...], gate_w_ref[...])
+            up = up_ref[...] + dot(far_ref[...], up_w_ref[...])
+            gate_ref[...] = gate
+            up_ref[...] = up
+            hidden_ref[...] = act_hidden(gate, up)
+
+    whole = pl.BlockSpec((rows, hidden_units), lambda j, a_ref: (0, 0))
+    weight = pl.BlockSpec((step, hidden_units), lambda j, a_ref: (near_first(j, a_ref[0]), 0))
+    return pl.pallas_call(
+        kernel,
+        grid_spec=pltpu.PrefetchScalarGridSpec(
+            num_scalar_prefetch=1,
+            grid=(4,),
+            in_specs=[
+                pl.BlockSpec((rows, step), lambda j, a_ref: (0, jnp.minimum(j, 1))),
+                pl.BlockSpec((rows, step), lambda j, a_ref: (0, jnp.maximum(j - 2, 0))),
+                weight,
+                weight,
+            ],
+            out_specs=[whole, whole, whole],
+        ),
+        out_shape=[
+            jax.ShapeDtypeStruct((rows, hidden_units), F32),
+            jax.ShapeDtypeStruct((rows, hidden_units), F32),
+            jax.ShapeDtypeStruct((rows, hidden_units), BF),
+        ],
+        name="forward",
+    )(a, near, far, gate_w, up_w)
+
+
+def gradients(a, grad_rows, down, hidden_in, gate, up, gate_w, up_w, base, dtype):
+    rows, half = grad_rows.shape
+    hidden_units = gate_w.shape[1]
+    step = half // 2
+
+    def kernel(a_ref, c_ref, down_ref, in_ref, gate_ref, up_ref, gw_ref, uw_ref, *rest):
+        base_ref = None if base is None else rest[0]
+        gg_ref, ug_ref, out_ref = rest[-3:]
+
+        @pl.when(pl.program_id(0) == 0)
+        def _():
+            hidden_grad = dot(c_ref[...], down_ref[...], 1, 1) + in_ref[...].astype(F32)
+            gate = gate_ref[...]
+            sig = jax.nn.sigmoid(gate)
+            gg_ref[...] = (
+                hidden_grad * up_ref[...] * sig * (1.0 + gate * (1.0 - sig))
+            ).astype(BF)
+            ug_ref[...] = (hidden_grad * (gate * sig)).astype(BF)
+
+        value = dot(gg_ref[...], gw_ref[...], 1, 1) + dot(ug_ref[...], uw_ref[...], 1, 1)
+        if base_ref is not None:
+            value = value + base_ref[...]
+        out_ref[...] = value.astype(dtype)
+
+    def whole(x):
+        return pl.BlockSpec(x.shape, lambda j, a_ref: (0, 0))
+
+    weight = pl.BlockSpec((step, hidden_units), lambda j, a_ref: (2 * (1 - a_ref[0]) + j, 0))
+    block = pl.BlockSpec((rows, step), lambda j, a_ref: (0, j))
+    operands = [grad_rows, down, hidden_in, gate, up, gate_w, up_w]
+    in_specs = [whole(x) for x in operands[:5]] + [weight, weight]
+    if base is not None:
+        operands.append(base)
+        in_specs.append(block)
+    grad = jax.ShapeDtypeStruct((rows, hidden_units), BF)
+    return pl.pallas_call(
+        kernel,
+        grid_spec=pltpu.PrefetchScalarGridSpec(
+            num_scalar_prefetch=1,
+            grid=(2,),
+            in_specs=in_specs,
+            out_specs=[whole(grad), whole(grad), block],
+        ),
+        out_shape=[grad, grad, jax.ShapeDtypeStruct((rows, half), dtype)],
+        name="gradients",
+    )(a, *operands)
 
 
 def layer(tokens, expert_ids, route_weights, w_gate, w_up, w_down, cotangent):
@@ -49,8 +237,8 @@
     up_b = swap_b(up_w)
     down_own, down_far = halves(down_w, 1, a)
     down_a = swap_a(down_far)
+    down_ab = swap_b(down_a)
     down_b = swap_b(down_own)
-    down_ab = swap_b(down_a)
 
     experts = jnp.arange(num_experts, dtype=jnp.int32)
     hit = expert_ids.T[None, :, :] == experts[:, None, None]
@@ -74,25 +262,10 @@
     packed_grad = (dot(pick, cot_half) * slot_weight).astype(BF)
     grad_rows = exchange(packed_grad, num_experts)
 
-    gate_1n, gate_1f = halves(gate_w, 0, a)
-    up_1n, up_1f = halves(up_w, 0, a)
-    gate_2n, gate_2f = halves(gate_b, 0, a)
-    up_2n, up_2f = halves(up_b, 0, a)
-
-    def forward(gate_n, gate_f, up_n, up_f):
-        gate = dot(rows_near, gate_n) + dot(rows_far, gate_f)
-        up = dot(rows_near, up_n) + dot(rows_far, up_f)
-        hidden = (gate * jax.nn.sigmoid(gate) * up).astype(BF)
-        return lax.optimization_barrier((gate, up, hidden))
-
-    def backward(hidden_grad, gate, up):
-        sig = jax.nn.sigmoid(gate)
-        act = gate * sig
-        gate_grad = (hidden_grad * up * sig * (1.0 + gate * (1.0 - sig))).astype(BF)
-        return gate_grad, (hidden_grad * act).astype(BF)
-
-    gate_1, up_1, hidden_1 = forward(gate_1n, gate_1f, up_1n, up_1f)
-    gate_2, up_2, hidden_2 = forward(gate_2n, gate_2f, up_2n, up_2f)
+    at = a.reshape(1)
+    gate_n, up_n = forward_near(at, rows_near, gate_w, up_w)
+    gate_1, up_1, hidden_1 = forward_far(at, rows_far, gate_n, up_n, gate_w, up_w)
+    gate_2, up_2, hidden_2 = forward(at, rows_near, rows_far, gate_b, up_b)
     hidden_3 = swap_a(hidden_1)
     hidden_4 = swap_a(hidden_2)
     hgrad_3 = dot(grad_rows, down_a, 1, 1).astype(BF)
@@ -101,21 +274,26 @@
     hgrad_4 = swap_a(hgrad_4)
 
     mixed_rows = dot(hidden_1, down_own) + dot(hidden_3, down_a)
-    mixed_rows = mixed_rows + dot(hidden_2, down_b) + dot(hidden_4, down_ab)
-    mixed_back = exchange(mixed_rows.astype(BF), num_experts)
-
-    hgrad_1 = dot(grad_rows, down_own, 1, 1)
-    hgrad_2 = dot(grad_rows, down_b, 1, 1)
-    gg_1, ug_1 = backward(hgrad_1 + hgrad_3.astype(F32), gate_1, up_1)
-    gg_2, ug_2 = backward(hgrad_2 + hgrad_4.astype(F32), gate_2, up_2)
-    far = dot(gg_1, gate_1f, 1, 1) + dot(ug_1, up_1f, 1, 1)
-    far = far + dot(gg_2, gate_2f, 1, 1) + dot(ug_2, up_2f, 1, 1)
-    far = far.astype(BF)
+    mixed_rows = lax.optimization_barrier(mixed_rows + dot(hidden_4, down_ab))
+    mixed_rows = (mixed_rows + dot(hidden_2, down_b)).astype(BF)
+    mixed_back = exchange(mixed_rows, num_experts)
+
+    gg_1, ug_1, base = gradients(
+        at, grad_rows, down_own, hgrad_3, gate_1, up_1, gate_w, up_w, None, F32
+    )
+    gg_2, ug_2, far = gradients(
+        at, grad_rows, down_b, hgrad_4, gate_2, up_2, gate_b, up_b, base, BF
+    )
     far = swap_a(far)
+    gate_1n, _ = halves(gate_w, 0, a)
+    up_1n, _ = halves(up_w, 0, a)
+    gate_2n, _ = halves(gate_b, 0, a)
+    up_2n, _ = halves(up_b, 0, a)
     near = dot(gg_1, gate_1n, 1, 1) + dot(ug_1, up_1n, 1, 1)
     near = near + dot(gg_2, gate_2n, 1, 1) + dot(ug_2, up_2n, 1, 1)
-    near = near + far.astype(F32)
-    grad_back = exchange(near.astype(BF), num_experts)
+    near = lax.optimization_barrier(near)
+    near = (near + far.astype(F32)).astype(BF)
+    grad_back = exchange(near, num_experts)
 
     def finish(partial):
         keep, give = halves(partial, 1, y & 1)
@@ -137,6 +315,4 @@
         P("expert", None),
     )
     out_specs = (P("expert", "replica"), P("expert", "replica"))
-    return jax.shard_map(
-        layer, mesh=mesh, in_specs=in_specs, out_specs=out_specs, check_vma=False
-    )
+    return jax.shard_map(layer, mesh=mesh, in_specs=in_specs, out_specs=out_specs, check_vma=False)

time: 340 us -> 310 us (0.912)
  matrix products: 64.9 us -> 28.5 us
  Pallas kernels: 0 us -> 30.7 us
  waiting for transfers between devices: 209 us -> 181 us
  other arithmetic: 3.38 us -> 7.62 us
    ppermute x6, waiting for transfers between devices: 98.4 us -> 48 us  [swap_b(): return lax.ppermute(value, 'replica', B_PAIRS)]
    dot_general x30 -> x16, matrix products: 64.9 us -> 28.5 us  [dot(): lax.dot_general(lhs, rhs, (((ldim,), (rdim,)), ((), ())), preferred_eleme...]
    pallas_call x0 -> x5, Pallas kernels: none -> 30.7 us  [the longest x2 13.6 us: gradients(): pl.pallas_call(kernel, grid_spec=pltpu.PrefetchScalarGridSpec(num_scalar_...]
    ppermute x7, waiting for transfers between devices: 45.4 us -> 68.9 us  [swap_a(): return lax.ppermute(value, 'replica', A_PAIRS)]
  transfers between devices with their start and end apart: 17 -> 17, of which waited for: 9 -> 9; matrix products, arithmetic and copies ran while one was open for 18% -> 10% of each run, Pallas kernels for 0% -> 10%
where the time goes in v3:
time: 310 us; the launch traced here: 309 us
  waiting for transfers between devices  181 us (58%)
  starting transfers between devices  58 us (19%)
  Pallas kernels  30.7 us (10%)
  matrix products  28.5 us (9%)
  other arithmetic  7.62 us (2%)
    ppermute x7, waiting for transfers between devices, swap_a(): return lax.ppermute(value, 'replica', A_PAIRS)  68.9 us
    all_to_all x4, waiting for transfers between devices, exchange(): lax.all_to_all(rows.reshape(num_experts, -1, width), 'expert', split_axis...  64.3 us
    ppermute x6, waiting for transfers between devices, swap_b(): return lax.ppermute(value, 'replica', B_PAIRS)  48 us
    all_to_all x4, starting transfers between devices, exchange(): lax.all_to_all(rows.reshape(num_experts, -1, width), 'expert', split_axis...  42.6 us
    dot_general x16, matrix products, dot(): lax.dot_general(lhs, rhs, (((ldim,), (rdim,)), ((), ())), preferred_eleme...  28.5 us
    pallas_call x2, Pallas kernels, gradients(): pl.pallas_call(kernel, grid_spec=pltpu.PrefetchScalarGridSpec(num_scalar_...  13.6 us
    ppermute x7, starting transfers between devices, swap_a(): return lax.ppermute(value, 'replica', A_PAIRS)  13.6 us
    pallas_call x1, Pallas kernels, forward(): pl.pallas_call(kernel, grid_spec=pltpu.PrefetchScalarGridSpec(num_scalar_...  7.15 us
  transfers between devices with their start and end apart: 17, of which 9 were waited for; matrix products, arithmetic and copies ran while one was open for 10% of the time, Pallas kernels for 10%

profile of v3, /device:TPU:1, one launch (start us, length us, event | category | flops | bytes accessed | tf_op | source)
XLA Modules:
  0.0 308.9 jit_solution(7477026716174340814)
XLA Ops:
  1.6 2.7 fusion.3
  4.4 13.0 %all-to-all-start = ((bf16[64,8,1280]{2,1,0:T(8,128)(2,1)}), bf16[64,8,1280]{2,1,0:T(8,128)(2,1)S(1)}, u32[]{:S(2)}, u32[]{:S(2)}) async-start(bf16[64,8,1280]{2,1,0:T(8,128)(2,1)} %fusion.3), calls=%async_computation | async-start | bytes 2621440 | tf_op jit(solution)/shard_map/all_to_all | solution.py:34
  17.6 2.8 fusion.4
  20.4 31.1 %all-to-all-done = bf16[64,8,1280]{2,1,0:T(8,128)(2,1)S(1)} async-done(((bf16[64,8,1280]{2,1,0:T(8,128)(2,1)}), bf16[64,8,1280]{2,1,0:T(8,128)(2,1)S(1)}, u32[]{:S(2)}, u32[]{:S(2)}) %all-to-all-start) | async-done | bytes 1310752 | tf_op jit(solution)/shard_map/all_to_all | solution.py:34
  52.6 6.2 %all-to-all-start.2 = ((bf16[64,8,1280]{2,1,0:T(8,128)(2,1)}), bf16[64,8,1280]{2,1,0:T(8,128)(2,1)S(1)}, u32[]{:S(2)}, u32[]{:S(2)}) async-start(bf16[64,8,1280]{2,1,0:T(8,128)(2,1)} %fusion.4), calls=%async_computation.2 | async-start | bytes 2621440 | tf_op jit(solution)/shard_map/all_to_all | solution.py:34
  60.3 2.7 collective-permute-start
  65.6 46.7 %collective-permute-done.2 = bf16[384,1280]{1,0:T(8,128)(2,1)} collective-permute-done((bf16[384,1280]{1,0:T(8,128)(2,1)S(1)}, bf16[384,1280]{1,0:T(8,128)(2,1)}, u32[]{:S(2)}, u32[]{:S(2)}) %collective-permute-start.2) | collective-permute-done | bytes 983072 | tf_op jit(solution)/shard_map/ppermute | solution.py:20
  112.3 4.7 %forward_near.1 = (f32[512,384]{1,0:T(8,128)}, f32[512,384]{1,0:T(8,128)}) custom-call(s32[1]{0:T(128)} %bitcast.2.a_ref, bf16[512,1280]{1,0:T(8,128)(2,1)} %bitcast.66, bf16[2560,384]{1,0:T(8,128)(2,1)} %bitcast.60, bf16[2560,384]{1,0:T(8,128)(2,1)} %bitcast.55), custom_call_target="tpu_custom_call" | custom-call | tf_op jit(solution)/shard_map/forward_near/pallas_call | solution.py:69
  117.0 5.2 %forward_far.1 = (f32[512,384]{1,0:T(8,128)}, f32[512,384]{1,0:T(8,128)}, bf16[512,384]{1,0:T(8,128)(2,1)}) custom-call(s32[1]{0:T(128)} %bitcast.2.a_ref, bf16[512,1280]{1,0:T(8,128)(2,1)} %collective-permute-done.far_ref, f32[512,384]{1,0:T(8,128)} %get-tuple-element.16.gn_ref, f32[512,384]{1,0:T(8,128)} %get-tuple-element.17.un_ref, ...), custom_call_target="tpu_custom_call" | custom-call | tf_op jit(solution)/shard_map/forward_far/pallas_call | solution.py:104
  122.2 2.6 collective-permute-start.1
  124.9 3.3 %convolution_convert_fusion.2 = bf16[512,384]{1,0:T(8,128)(2,1)} fusion(bf16[384,1280]{1,0:T(8,128)(2,1)} %collective-permute-done.2, bf16[64,8,1280]{2,1,0:T(8,128)(2,1)S(1)} %all-to-all-done.2), kind=kOutput, calls=%fused_computation.19 | convolution fusion | flops 503513088 | bytes 2686976 | tf_op jit(solution)/shard_map/dot_general | solution.py:24
  128.2 17.0 %collective-permute-done.4.up_w_ref.uw_ref = bf16[2560,384]{1,0:T(8,128)(2,1)} collective-permute-done((bf16[2560,384]{1,0:T(8,128)(2,1)S(1)}, bf16[2560,384]{1,0:T(8,128)(2,1)}, u32[]{:S(2)}, u32[]{:S(2)}) %collective-permute-start.4) | collective-permute-done | bytes 1966112 | tf_op jit(solution)/shard_map/ppermute | solution.py:16
  145.2 7.2 %forward.1 = (f32[512,384]{1,0:T(8,128)}, f32[512,384]{1,0:T(8,128)}, bf16[512,384]{1,0:T(8,128)(2,1)}) custom-call(s32[1]{0:T(128)} %bitcast.2.a_ref, bf16[512,1280]{1,0:T(8,128)(2,1)} %bitcast.67, bf16[512,1280]{1,0:T(8,128)(2,1)} %collective-permute-done.far_ref, bf16[2560,384]{1,0:T(8,128)(2,1)} %collective-permute-done.3.gate_w_ref.gw_ref, ...), custom_call_target="tpu_custom_call" | custom-call | tf_op jit(solution)/shard_map/forward/pallas_call | solution.py:156
  152.4 2.7 collective-permute-start.5
  155.1 11.2 %collective-permute-done.7.down_ref = bf16[384,1280]{1,0:T(8,128)(2,1)} collective-permute-done((bf16[384,1280]{1,0:T(8,128)(2,1)}, bf16[384,1280]{1,0:T(8,128)(2,1)}, u32[]{:S(2)}, u32[]{:S(2)}) %collective-permute-start.7) | collective-permute-done | bytes 983072 | tf_op jit(solution)/shard_map/ppermute | solution.py:16
  172.7 14.6 %collective-permute-done.6 = bf16[384,1280]{1,0:T(8,128)(2,1)} collective-permute-done((bf16[384,1280]{1,0:T(8,128)(2,1)}, bf16[384,1280]{1,0:T(8,128)(2,1)}, u32[]{:S(2)}, u32[]{:S(2)}) %collective-permute-start.6) | collective-permute-done | bytes 983072 | tf_op jit(solution)/shard_map/ppermute | solution.py:16
  190.7 11.4 %all-to-all-start.1 = ((bf16[64,8,1280]{2,1,0:T(8,128)(2,1)}), bf16[64,8,1280]{2,1,0:T(8,128)(2,1)S(1)}, u32[]{:S(2)}, u32[]{:S(2)}) async-start(bf16[64,8,1280]{2,1,0:T(8,128)(2,1)} %fusion.6), calls=%async_computation.1 | async-start | bytes 2621440 | tf_op jit(solution)/shard_map/all_to_all | solution.py:34
  204.2 2.8 collective-permute-start.10
  207.0 6.6 %gradients.2 = (bf16[512,384]{1,0:T(8,128)(2,1)}, bf16[512,384]{1,0:T(8,128)(2,1)}, f32[512,1280]{1,0:T(8,128)}) custom-call(s32[1]{0:T(128)} %bitcast.2.a_ref, bf16[512,1280]{1,0:T(8,128)(2,1)} %bitcast.63, bf16[384,1280]{1,0:T(8,128)(2,1)} %get-tuple-element.32.down_ref, bf16[512,384]{1,0:T(8,128)(2,1)} %collective-permute-done.9.in_ref, ...), custom_call_target="tpu_custom_call" | custom-call | tf_op jit(solution)/shard_map/gradients/pallas_call | solution.py:213
  216.6 7.0 %gradients.3 = (bf16[512,384]{1,0:T(8,128)(2,1)}, bf16[512,384]{1,0:T(8,128)(2,1)}, bf16[512,1280]{1,0:T(8,128)(2,1)}) custom-call(s32[1]{0:T(128)} %bitcast.2.a_ref, bf16[512,1280]{1,0:T(8,128)(2,1)} %bitcast.64, bf16[384,1280]{1,0:T(8,128)(2,1)} %collective-permute-done.7.down_ref, bf16[512,384]{1,0:T(8,128)(2,1)} %copy-done.7, ...), custom_call_target="tpu_custom_call" | custom-call | tf_op jit(solution)/shard_map/gradients/pallas_call | solution.py:213
  234.1 19.9 %collective-permute-done.11 = bf16[512,1280]{1,0:T(8,128)(2,1)S(1)} collective-permute-done((bf16[512,1280]{1,0:T(8,128)(2,1)}, bf16[512,1280]{1,0:T(8,128)(2,1)S(1)}, u32[]{:S(2)}, u32[]{:S(2)}) %collective-permute-start.11) | collective-permute-done | bytes 1310752 | tf_op jit(solution)/shard_map/ppermute | solution.py:20
  255.5 12.1 %all-to-all-start.3 = ((bf16[64,8,1280]{2,1,0:T(8,128)(2,1)}), bf16[64,8,1280]{2,1,0:T(8,128)(2,1)S(1)}, u32[]{:S(2)}, u32[]{:S(2)}) async-start(bf16[64,8,1280]{2,1,0:T(8,128)(2,1)} %fusion.7), calls=%async_computation.3 | async-start | bytes 2621440 | tf_op jit(solution)/shard_map/all_to_all | solution.py:34
  268.5 33.2 %all-to-all-done.3 = bf16[64,8,1280]{2,1,0:T(8,128)(2,1)S(1)} async-done(((bf16[64,8,1280]{2,1,0:T(8,128)(2,1)}), bf16[64,8,1280]{2,1,0:T(8,128)(2,1)S(1)}, u32[]{:S(2)}, u32[]{:S(2)}) %all-to-all-start.3) | async-done | bytes 1310752 | tf_op jit(solution)/shard_map/all_to_all | solution.py:34
  303.0 5.2 %collective-permute-done.12 = bf16[128,640]{1,0:T(8,128)(2,1)S(1)} collective-permute-done((bf16[128,640]{1,0:T(8,128)(2,1)S(1)}, bf16[128,640]{1,0:T(8,128)(2,1)S(1)}, u32[]{:S(2)}, u32[]{:S(2)}) %collective-permute-start.12) | collective-permute-done | bytes 163872 | tf_op jit(solution)/shard_map/ppermute | solution.py:16
  (65 shorter events, 36.1 us)
Async XLA Ops:
  4.4 47.1 %all-to-all-start = ((bf16[64,8,1280]{2,1,0:T(8,128)(2,1)}), bf16[64,8,1280]{2,1,0:T(8,128)(2,1)S(1)}, u32[]{:S(2)}, u32[]{:S(2)}) async-start(bf16[64,8,1280]{2,1,0:T(8,128)(2,1)} %fusion.3), calls=%async_computation | async-start | bytes 2621440 | tf_op jit(solution)/shard_map/all_to_all | solution.py:34
  17.6 42.5 %copy-start = (bf16[1,2560,384]{2,1,0:T(8,128)(2,1)S(1)}, bf16[1,2560,384]{2,1,0:T(8,128)(2,1)}, u32[]{:S(2)}) copy-start(bf16[1,2560,384]{2,1,0:T(8,128)(2,1)} %param.11) | copy-start | bytes 5898244
  52.6 72.3 %all-to-all-start.2 = ((bf16[64,8,1280]{2,1,0:T(8,128)(2,1)}), bf16[64,8,1280]{2,1,0:T(8,128)(2,1)S(1)}, u32[]{:S(2)}, u32[]{:S(2)}) async-start(bf16[64,8,1280]{2,1,0:T(8,128)(2,1)} %fusion.4), calls=%async_computation.2 | async-start | bytes 2621440 | tf_op jit(solution)/shard_map/all_to_all | solution.py:34
  58.7 69.4 %collective-permute-start.3 = (bf16[2560,384]{1,0:T(8,128)(2,1)}, bf16[2560,384]{1,0:T(8,128)(2,1)}, u32[]{:S(2)}, u32[]{:S(2)}) collective-permute-start(bf16[2560,384]{1,0:T(8,128)(2,1)} %bitcast.59), channel_id=1, source_target_pairs={{0,1},{1,0},{2,3},{3,2},{4,5},{5,4},{6,7},{7,6},{8,9},{9,8},{10,11... | collective-permute-start | bytes 5898248 | tf_op jit(solution)/shard_map/ppermute | solution.py:16
  60.1 85.1 %collective-permute-start.4 = (bf16[2560,384]{1,0:T(8,128)(2,1)S(1)}, bf16[2560,384]{1,0:T(8,128)(2,1)}, u32[]{:S(2)}, u32[]{:S(2)}) collective-permute-start(bf16[2560,384]{1,0:T(8,128)(2,1)S(1)} %bitcast.58), channel_id=1, source_target_pairs={{0,1},{1,0},{2,3},{3,2},{4,5},{5,4},{6,7},{7,6},{8,9},{9,8},{10,11... | collective-permute-start | bytes 5898248 | tf_op jit(solution)/shard_map/ppermute | solution.py:16
  60.3 56.7 %collective-permute-start = (bf16[512,1280]{1,0:T(8,128)(2,1)}, bf16[512,1280]{1,0:T(8,128)(2,1)}, u32[]{:S(2)}, u32[]{:S(2)}) collective-permute-start(bf16[512,1280]{1,0:T(8,128)(2,1)} %bitcast.65), channel_id=1, source_target_pairs={{0,3},{3,0},{1,2},{2,1},{4,7},{7,4},{5,6},{6,5},{8,11},{11,8},{9,1... | collective-permute-start | bytes 3932168 | tf_op jit(solution)/shard_map/ppermute | solution.py:20
  65.6 46.7 %collective-permute-start.2 = (bf16[384,1280]{1,0:T(8,128)(2,1)S(1)}, bf16[384,1280]{1,0:T(8,128)(2,1)}, u32[]{:S(2)}, u32[]{:S(2)}) collective-permute-start(bf16[384,1280]{1,0:T(8,128)(2,1)S(1)} %get-tuple-element.33), channel_id=1, source_target_pairs={{0,3},{3,0},{1,2},{2,1},{4,7},{7,4},{5,6},{6,5},{8,11},{11,8},{9,1... | collective-permute-start | bytes 2949128 | tf_op jit(solution)/shard_map/ppermute | solution.py:20
  65.6 100.7 %collective-permute-start.7 = (bf16[384,1280]{1,0:T(8,128)(2,1)}, bf16[384,1280]{1,0:T(8,128)(2,1)}, u32[]{:S(2)}, u32[]{:S(2)}) collective-permute-start(bf16[384,1280]{1,0:T(8,128)(2,1)} %get-tuple-element.32.down_ref), channel_id=1, source_target_pairs={{0,1},{1,0},{2,3},{3,2},{4,5},{5,4},{6,7},{7,6},{8,9},{9,8},{10,11... | collective-permute-start | bytes 2949128 | tf_op jit(solution)/shard_map/ppermute | solution.py:16
  112.3 75.0 %collective-permute-start.6 = (bf16[384,1280]{1,0:T(8,128)(2,1)}, bf16[384,1280]{1,0:T(8,128)(2,1)}, u32[]{:S(2)}, u32[]{:S(2)}) collective-permute-start(bf16[384,1280]{1,0:T(8,128)(2,1)} %collective-permute-done.2), channel_id=1, source_target_pairs={{0,1},{1,0},{2,3},{3,2},{4,5},{5,4},{6,7},{7,6},{8,9},{9,8},{10,11... | collective-permute-start | bytes 2949128 | tf_op jit(solution)/shard_map/ppermute | solution.py:16
  122.2 46.2 %collective-permute-start.1 = (bf16[512,384]{1,0:T(8,128)(2,1)}, bf16[512,384]{1,0:T(8,128)(2,1)}, u32[]{:S(2)}, u32[]{:S(2)}) collective-permute-start(bf16[512,384]{1,0:T(8,128)(2,1)} %get-tuple-element.18), channel_id=1, source_target_pairs={{0,3},{3,0},{1,2},{2,1},{4,7},{7,4},{5,6},{6,5},{8,11},{11,8},{9,1... | collective-permute-start | bytes 1179656 | tf_op jit(solution)/shard_map/ppermute | solution.py:20
  124.9 27.5 %copy-start.3 = (bf16[64,8,1280]{2,1,0:T(8,128)(2,1)}, bf16[64,8,1280]{2,1,0:T(8,128)(2,1)S(1)}, u32[]{:S(2)}) copy-start(bf16[64,8,1280]{2,1,0:T(8,128)(2,1)S(1)} %all-to-all-done.2) | copy-start | bytes 3932164
  128.1 78.8 %collective-permute-start.9 = (bf16[512,384]{1,0:T(8,128)(2,1)}, bf16[512,384]{1,0:T(8,128)(2,1)}, u32[]{:S(2)}, u32[]{:S(2)}) collective-permute-start(bf16[512,384]{1,0:T(8,128)(2,1)} %convolution_convert_fusion.2), channel_id=1, source_target_pairs={{0,3},{3,0},{1,2},{2,1},{4,7},{7,4},{5,6},{6,5},{8,11},{11,8},{9,1... | collective-permute-start | bytes 1179656 | tf_op jit(solution)/shard_map/ppermute | solution.py:20
  152.4 35.0 %collective-permute-start.5 = (bf16[512,384]{1,0:T(8,128)(2,1)}, bf16[512,384]{1,0:T(8,128)(2,1)S(1)}, u32[]{:S(2)}, u32[]{:S(2)}) collective-permute-start(bf16[512,384]{1,0:T(8,128)(2,1)} %get-tuple-element.19), channel_id=1, source_target_pairs={{0,3},{3,0},{1,2},{2,1},{4,7},{7,4},{5,6},{6,5},{8,11},{11,8},{9,1... | collective-permute-start | bytes 1179656 | tf_op jit(solution)/shard_map/ppermute | solution.py:20
  190.7 11.4 %copy-start.4 = (bf16[64,8,1280]{2,1,0:T(8,128)(2,1)S(1)}, bf16[64,8,1280]{2,1,0:T(8,128)(2,1)}, u32[]{:S(2)}) copy-start(bf16[64,8,1280]{2,1,0:T(8,128)(2,1)} %copy-done.3) | copy-start | bytes 3932164
  190.7 64.7 %all-to-all-start.1 = ((bf16[64,8,1280]{2,1,0:T(8,128)(2,1)}), bf16[64,8,1280]{2,1,0:T(8,128)(2,1)S(1)}, u32[]{:S(2)}, u32[]{:S(2)}) async-start(bf16[64,8,1280]{2,1,0:T(8,128)(2,1)} %fusion.6), calls=%async_computation.1 | async-start | bytes 2621440 | tf_op jit(solution)/shard_map/all_to_all | solution.py:34
  204.2 11.6 %collective-permute-start.10 = (bf16[512,384]{1,0:T(8,128)(2,1)S(1)}, bf16[512,384]{1,0:T(8,128)(2,1)S(1)}, u32[]{:S(2)}, u32[]{:S(2)}) collective-permute-start(bf16[512,384]{1,0:T(8,128)(2,1)S(1)} %convolution_convert_fusion.1), channel_id=1, source_target_pairs={{0,3},{3,0},{1,2},{2,1},{4,7},{7,4},{5,6},{6,5},{8,11},{11,8},{9,1... | collective-permute-start | bytes 1179656 | tf_op jit(solution)/shard_map/ppermute | solution.py:20
  216.5 9.6 %copy-start.1 = (bf16[1,2560,384]{2,1,0:T(8,128)(2,1)S(1)}, bf16[1,2560,384]{2,1,0:T(8,128)(2,1)}, u32[]{:S(2)}) copy-start(bf16[1,2560,384]{2,1,0:T(8,128)(2,1)} %param.11) | copy-start | bytes 5898244
  223.6 30.5 %collective-permute-start.11 = (bf16[512,1280]{1,0:T(8,128)(2,1)}, bf16[512,1280]{1,0:T(8,128)(2,1)S(1)}, u32[]{:S(2)}, u32[]{:S(2)}) collective-permute-start(bf16[512,1280]{1,0:T(8,128)(2,1)} %get-tuple-element.29), channel_id=1, source_target_pairs={{0,3},{3,0},{1,2},{2,1},{4,7},{7,4},{5,6},{6,5},{8,11},{11,8},{9,1... | collective-permute-start | bytes 3932168 | tf_op jit(solution)/shard_map/ppermute | solution.py:20
  228.1 2.4 copy-start.9
  230.6 2.5 copy-start.2
  230.6 2.5 copy-start.6
  255.5 46.3 %all-to-all-start.3 = ((bf16[64,8,1280]{2,1,0:T(8,128)(2,1)}), bf16[64,8,1280]{2,1,0:T(8,128)(2,1)S(1)}, u32[]{:S(2)}, u32[]{:S(2)}) async-start(bf16[64,8,1280]{2,1,0:T(8,128)(2,1)} %fusion.7), calls=%async_computation.3 | async-start | bytes 2621440 | tf_op jit(solution)/shard_map/all_to_all | solution.py:34
  268.4 33.8 %collective-permute-start.8 = (bf16[128,640]{1,0:T(8,128)(2,1)S(1)}, bf16[128,640]{1,0:T(8,128)(2,1)S(1)}, u32[]{:S(2)}, u32[]{:S(2)}) collective-permute-start(bf16[128,640]{1,0:T(8,128)(2,1)S(1)} %select_convert_fusion.2), channel_id=1, source_target_pairs={{0,1},{1,0},{2,3},{3,2},{4,5},{5,4},{6,7},{7,6},{8,9},{9,8},{10,11... | collective-permute-start | bytes 491528 | tf_op jit(solution)/shard_map/ppermute | solution.py:16
  302.1 6.0 %collective-permute-start.12 = (bf16[128,640]{1,0:T(8,128)(2,1)S(1)}, bf16[128,640]{1,0:T(8,128)(2,1)S(1)}, u32[]{:S(2)}, u32[]{:S(2)}) collective-permute-start(bf16[128,640]{1,0:T(8,128)(2,1)S(1)} %select_convert_fusion.1), channel_id=1, source_target_pairs={{0,1},{1,0},{2,3},{3,2},{4,5},{5,4},{6,7},{7,6},{8,9},{9,8},{10,11... | collective-permute-start | bytes 491528 | tf_op jit(solution)/shard_map/ppermute | solution.py:16
  (4 other events, 6.0 us)

commit v4 on v3

v4 whole, which is shorter than its diff:
```python
import jax
import jax.numpy as jnp
from jax import lax
from jax.experimental import pallas as pl
from jax.experimental.pallas import tpu as pltpu
from jax.sharding import PartitionSpec as P


BF = jnp.bfloat16
F32 = jnp.float32
PAIRS_0 = (1, 0, 3, 2)
PAIRS_1 = (3, 2, 1, 0)


def swap(value, even, odd):
    pairs = []
    for expert in range(lax.axis_size("expert")):
        partner = odd if expert % 2 else even
        pairs += [(expert * 4 + y, expert * 4 + partner[y]) for y in range(4)]
    return lax.ppermute(value, ("expert", "replica"), pairs)


def swap_b(value):
    return swap(value, PAIRS_0, PAIRS_1)


def swap_a(value):
    return swap(value, PAIRS_1, PAIRS_0)


def dot(lhs, rhs, ldim=1, rdim=0):
    return lax.dot_general(lhs, rhs, (((ldim,), (rdim,)), ((), ())), preferred_element_type=F32)


def choose(value, index):
    quarters = jnp.split(value, 4, axis=1)
    low = jnp.where(index == 0, quarters[0], quarters[1])
    high = jnp.where(index == 2, quarters[2], quarters[3])
    return jnp.where(index < 2, low, high)


def columns(value, first, second):
    return jnp.concatenate([choose(value, first), choose(value, second)], axis=1)


def rows_of(value, first, second):
    size = value.shape[0] // 4
    return jnp.concatenate(
        [
            lax.dynamic_slice_in_dim(value, first * size, size, 0),
            lax.dynamic_slice_in_dim(value, second * size, size, 0),
        ],
        axis=0,
    )


def exchange(rows, num_experts):
    width = rows.shape[1]
    moved = lax.all_to_all(
        rows.reshape(num_experts, -1, width), "expert", split_axis=0, concat_axis=0, tiled=True
    )
    return moved.reshape(-1, width)


def act_hidden(gate, up):
    return (gate * jax.nn.sigmoid(gate) * up).astype(BF)


def forward_near(order, near, gate_w, up_w):
    rows, half = near.shape
    hidden_units = gate_w.shape[1]
    step = half // 2

    def kernel(order_ref, near_ref, gate_w_ref, up_w_ref, gate_ref, up_ref):
        gate = dot(near_ref[...], gate_w_ref[...])
        up = dot(near_ref[...], up_w_ref[...])

        @pl.when(pl.program_id(0) == 0)
        def _():
            gate_ref[...] = gate
            up_ref[...] = up

        @pl.when(pl.program_id(0) == 1)
        def _():
            gate_ref[...] += gate
            up_ref[...] += up

    whole = pl.BlockSpec((rows, hidden_units), lambda j, order_ref: (0, 0))
    weight = pl.BlockSpec((step, hidden_units), lambda j, order_ref: (order_ref[j], 0))
    return pl.pallas_call(
        kernel,
        grid_spec=pltpu.PrefetchScalarGridSpec(
            num_scalar_prefetch=1,
            grid=(2,),
            in_specs=[pl.BlockSpec((rows, step), lambda j, order_ref: (0, j)), weight, weight],
            out_specs=[whole, whole],
        ),
        out_shape=[jax.ShapeDtypeStruct((rows, hidden_units), F32)] * 2,
        name="forward_near",
    )(order, near, gate_w, up_w)


def forward_far(order, far, gate_near, up_near, gate_w, up_w):
    rows, half = far.shape
    hidden_units = gate_w.shape[1]
    step = half // 2

    def kernel(order_ref, far_ref, gn_ref, un_ref, gate_w_ref, up_w_ref, gate_ref, up_ref, hidden_ref):
        @pl.when(pl.program_id(0) == 0)
        def _():
            gate_ref[...] = gn_ref[...] + dot(far_ref[...], gate_w_ref[...])
            up_ref[...] = un_ref[...] + dot(far_ref[...], up_w_ref[...])

        @pl.when(pl.program_id(0) == 1)
        def _():
            gate = gate_ref[...] + dot(far_ref[...], gate_w_ref[...])
            up = up_ref[...] + dot(far_ref[...], up_w_ref[...])
            gate_ref[...] = gate
            up_ref[...] = up
            hidden_ref[...] = act_hidden(gate, up)

    whole = pl.BlockSpec((rows, hidden_units), lambda j, order_ref: (0, 0))
    weight = pl.BlockSpec((step, hidden_units), lambda j, order_ref: (order_ref[2 + j], 0))
    wide = jax.ShapeDtypeStruct((rows, hidden_units), F32)
    return pl.pallas_call(
        kernel,
        grid_spec=pltpu.PrefetchScalarGridSpec(
            num_scalar_prefetch=1,
            grid=(2,),
            in_specs=[
                pl.BlockSpec((rows, step), lambda j, order_ref: (0, j)),
                whole,
                whole,
                weight,
                weight,
            ],
            out_specs=[whole, whole, whole],
        ),
        out_shape=[wide, wide, jax.ShapeDtypeStruct((rows, hidden_units), BF)],
        name="forward_far",
    )(order, far, gate_near, up_near, gate_w, up_w)


def forward(order, near, far, gate_w, up_w):
    rows, half = near.shape
    hidden_units = gate_w.shape[1]
    step = half // 2

    def kernel(order_ref, near_ref, far_ref, gate_w_ref, up_w_ref, gate_ref, up_ref, hidden_ref):
        j = pl.program_id(0)

        @pl.when(j == 0)
        def _():
            gate_ref[...] = dot(near_ref[...], gate_w_ref[...])
            up_ref[...] = dot(near_ref[...], up_w_ref[...])

        @pl.when(j == 1)
        def _():
            gate_ref[...] += dot(near_ref[...], gate_w_ref[...])
            up_ref[...] += dot(near_ref[...], up_w_ref[...])

        @pl.when(j == 2)
        def _():
            gate_ref[...] += dot(far_ref[...], gate_w_ref[...])
            up_ref[...] += dot(far_ref[...], up_w_ref[...])

        @pl.when(j == 3)
        def _():
            gate = gate_ref[...] + dot(far_ref[...], gate_w_ref[...])
            up = up_ref[...] + dot(far_ref[...], up_w_ref[...])
            gate_ref[...] = gate
            up_ref[...] = up
            hidden_ref[...] = act_hidden(gate, up)

    whole = pl.BlockSpec((rows, hidden_units), lambda j, order_ref: (0, 0))
    weight = pl.BlockSpec((step, hidden_units), lambda j, order_ref: (order_ref[j], 0))
    return pl.pallas_call(
        kernel,
        grid_spec=pltpu.PrefetchScalarGridSpec(
            num_scalar_prefetch=1,
            grid=(4,),
            in_specs=[
                pl.BlockSpec((rows, step), lambda j, order_ref: (0, jnp.minimum(j, 1))),
                pl.BlockSpec((rows, step), lambda j, order_ref: (0, jnp.maximum(j - 2, 0))),
                weight,
                weight,
            ],
            out_specs=[whole, whole, whole],
        ),
        out_shape=[
            jax.ShapeDtypeStruct((rows, hidden_units), F32),
            jax.ShapeDtypeStruct((rows, hidden_units), F32),
            jax.ShapeDtypeStruct((rows, hidden_units), BF),
        ],
        name="forward",
    )(order, near, far, gate_w, up_w)


def gradients(order, grad_rows, down, hidden_in, gate, up, gate_w, up_w, base, dtype):
    rows, half = grad_rows.shape
    hidden_units = gate_w.shape[1]
    step = half // 2

    def kernel(order_ref, c_ref, down_ref, in_ref, gate_ref, up_ref, gw_ref, uw_ref, *rest):
        base_ref = None if base is None else rest[0]
        gg_ref, ug_ref, out_ref = rest[-3:]

        @pl.when(pl.program_id(0) == 0)
        def _():
            hidden_grad = dot(c_ref[...], down_ref[...], 1, 1) + in_ref[...].astype(F32)
            gate = gate_ref[...]
            sig = jax.nn.sigmoid(gate)
            gg_ref[...] = (
                hidden_grad * up_ref[...] * sig * (1.0 + gate * (1.0 - sig))
            ).astype(BF)
            ug_ref[...] = (hidden_grad * (gate * sig)).astype(BF)

        value = dot(gg_ref[...], gw_ref[...], 1, 1) + dot(ug_ref[...], uw_ref[...], 1, 1)
        if base_ref is not None:
            value = value + base_ref[...]
        out_ref[...] = value.astype(dtype)

    def whole(x):
        return pl.BlockSpec(x.shape, lambda j, order_ref: (0, 0))

    weight = pl.BlockSpec((step, hidden_units), lambda j, order_ref: (order_ref[2 + j], 0))
    block = pl.BlockSpec((rows, step), lambda j, order_ref: (0, j))
    operands = [grad_rows, down, hidden_in, gate, up, gate_w, up_w]
    in_specs = [whole(x) for x in operands[:5]] + [weight, weight]
    if base is not None:
        operands.append(base)
        in_specs.append(block)
    grad = jax.ShapeDtypeStruct((rows, hidden_units), BF)
    return pl.pallas_call(
        kernel,
        grid_spec=pltpu.PrefetchScalarGridSpec(
            num_scalar_prefetch=1,
            grid=(2,),
            in_specs=in_specs,
            out_specs=[whole(grad), whole(grad), block],
        ),
        out_shape=[grad, grad, jax.ShapeDtypeStruct((rows, half), dtype)],
        name="gradients",
    )(order, *operands)


def layer(tokens, expert_ids, route_weights, w_gate, w_up, w_down, cotangent):
    num_experts = lax.axis_size("expert")
    tok_rows, top = expert_ids.shape
    capacity = tok_rows * top * 4 // (num_experts * 3)
    slots = capacity // 2
    y = lax.axis_index("replica")
    odd = lax.axis_index("expert") & 1
    outer = y >> 1
    inner = ((y + 1) >> 1) & 1
    near_0 = jnp.where(odd == 0, 2 * outer, inner)
    near_1 = jnp.where(odd == 0, 2 * outer + 1, 3 - inner)
    far_0 = jnp.where(odd == 0, 2 - 2 * outer, 1 - inner)
    far_1 = jnp.where(odd == 0, 3 - 2 * outer, 2 + inner)
    order = jnp.stack([near_0, near_1, far_0, far_1])
    gate_w, up_w, down_w = w_gate[0], w_up[0], w_down[0]

    gate_b = swap_b(gate_w)
    up_b = swap_b(up_w)
    down_own = columns(down_w, near_0, near_1)
    down_far = columns(down_w, far_0, far_1)
    down_a = swap_a(down_far)
    down_ab = swap_b(down_a)
    down_b = swap_b(down_own)

    experts = jnp.arange(num_experts, dtype=jnp.int32)
    hit = expert_ids.T[None, :, :] == experts[:, None, None]
    chosen = jnp.sum(hit.astype(F32), axis=1)
    weight = jnp.sum(jnp.where(hit, route_weights.T[None, :, :], 0.0), axis=1)
    before = jnp.arange(tok_rows)[:, None] < jnp.arange(tok_rows)[None, :]
    rank = dot(chosen.astype(BF), before.astype(BF))
    is_odd = (experts & 1)[:, None] == 1
    first_slot = slots * jnp.where(is_odd, outer, inner)
    place = jnp.where(chosen > 0, rank.astype(jnp.int32) - first_slot, -1)
    pick = place[:, None, :] == jnp.arange(slots, dtype=jnp.int32)[None, :, None]
    pick_w = jnp.where(pick, weight[:, None, :], 0.0)
    slot_weight = jnp.sum(pick_w, axis=2).reshape(-1, 1)
    is_odd = is_odd[:, :, None]

    def by_parity(value):
        parts = [jnp.where(is_odd, 0, value), jnp.where(is_odd, value, 0)]
        return jnp.concatenate(parts, axis=2).reshape(-1, 2 * tok_rows)

    pick = by_parity(pick.astype(BF))
    pick_hi = pick_w.astype(BF)
    pick_lo = by_parity((pick_w - pick_hi.astype(F32)).astype(BF))
    pick_hi = by_parity(pick_hi)

    def both(value):
        even = columns(value, 2 * outer, 2 * outer + 1)
        return jnp.concatenate([even, columns(value, inner, 3 - inner)], axis=0)

    packed = dot(pick, both(tokens)).astype(BF)
    rows_near = exchange(packed, num_experts)
    rows_far = swap_a(rows_near)
    packed_grad = (dot(pick, both(cotangent)) * slot_weight).astype(BF)
    grad_rows = exchange(packed_grad, num_experts)

    gate_n, up_n = forward_near(order, rows_near, gate_w, up_w)
    gate_1, up_1, hidden_1 = forward_far(order, rows_far, gate_n, up_n, gate_w, up_w)
    gate_2, up_2, hidden_2 = forward(order, rows_near, rows_far, gate_b, up_b)
    hidden_3 = swap_a(hidden_1)
    hidden_4 = swap_a(hidden_2)
    hgrad_3 = dot(grad_rows, down_a, 1, 1).astype(BF)
    hgrad_3 = swap_a(hgrad_3)
    hgrad_4 = dot(grad_rows, down_ab, 1, 1).astype(BF)
    hgrad_4 = swap_a(hgrad_4)

    mixed_rows = dot(hidden_1, down_own) + dot(hidden_3, down_a)
    mixed_rows = lax.optimization_barrier(mixed_rows + dot(hidden_4, down_ab))
    mixed_rows = (mixed_rows + dot(hidden_2, down_b)).astype(BF)
    mixed_back = exchange(mixed_rows, num_experts)

    gg_1, ug_1, base = gradients(
        order, grad_rows, down_own, hgrad_3, gate_1, up_1, gate_w, up_w, None, F32
    )
    gg_2, ug_2, far = gradients(
        order, grad_rows, down_b, hgrad_4, gate_2, up_2, gate_b, up_b, base, BF
    )
    far = swap_a(far)
    gate_1n = rows_of(gate_w, near_0, near_1)
    up_1n = rows_of(up_w, near_0, near_1)
    gate_2n = rows_of(gate_b, near_0, near_1)
    up_2n = rows_of(up_b, near_0, near_1)
    near = dot(gg_1, gate_1n, 1, 1) + dot(ug_1, up_1n, 1, 1)
    near = near + dot(gg_2, gate_2n, 1, 1) + dot(ug_2, up_2n, 1, 1)
    near = lax.optimization_barrier(near)
    near = (near + far.astype(F32)).astype(BF)
    grad_back = exchange(near, num_experts)

    def finish(partial):
        def share(value, at, pairs):
            low, high = jnp.split(value, 2, axis=1)
            keep = jnp.where(at == 0, low, high)
            give = jnp.where(at == 0, high, low).astype(BF)
            return keep + lax.ppermute(give, "replica", list(enumerate(pairs))).astype(F32)

        even, odd_part = jnp.split(partial, 2, axis=0)
        total = share(even, y & 1, PAIRS_0) + share(odd_part, outer, PAIRS_1)
        return total.astype(BF)

    mixed = finish(dot(pick_hi, mixed_back, 0, 0) + dot(pick_lo, mixed_back, 0, 0))
    tokens_grad = finish(dot(pick, grad_back, 0, 0))
    return (mixed, tokens_grad)


def solution(mesh):
    in_specs = (
        P("expert", None),
        P("expert", None),
        P("expert", None),
        P("expert", None, "replica"),
        P("expert", None, "replica"),
        P("expert", "replica", None),
        P("expert", None),
    )
    out_specs = (P("expert", "replica"), P("expert", "replica"))
    return jax.shard_map(layer, mesh=mesh, in_specs=in_specs, out_specs=out_specs, check_vma=False)
```

time: 310 us -> 275 us (0.89)
  waiting for transfers between devices: 181 us -> 136 us
  other arithmetic: 7.62 us -> 13.8 us
  local copies, waits for them, and re-layouts: 2.05 us -> 6.74 us
    ppermute x13 -> x15, waiting for transfers between devices: 117 us -> 74.4 us  [the longest x11 68 us: swap(): return lax.ppermute(value, ('expert', 'replica'), pairs)]
    dynamic_slice x0 -> x4, local copies, waits for them, and re-layouts: none -> 4.92 us  [rows_of(): lax.dynamic_slice_in_dim(value, first * size, size, 0)]
    select_n x1 -> x8, other arithmetic: 2.56 us -> 5.91 us  [the longest x6 4.71 us: choose(): return jnp.where(index < 2, low, high)]
    all_to_all x4, waiting for transfers between devices: 64.3 us -> 61.1 us  [exchange(): lax.all_to_all(rows.reshape(num_experts, -1, width), 'expert', split_axis...]
    ppermute x13 -> x15, starting transfers between devices: 15.3 us -> 13 us  [the longest x11 12.7 us: swap(): return lax.ppermute(value, ('expert', 'replica'), pairs)]
  transfers between devices with their start and end apart: 17 -> 19, of which waited for: 9 -> 8; matrix products, arithmetic and copies ran while one was open for 10% -> 15% of each run, Pallas kernels for 10% -> 12%
where the time goes in v4:
time: 275 us; the launch traced here: 274 us
  waiting for transfers between devices  136 us (49%)
  starting transfers between devices  56.9 us (21%)
  Pallas kernels  33.8 us (12%)
  matrix products  25.9 us (9%)
  other arithmetic  13.8 us (5%)
  local copies, waits for them, and re-layouts  6.74 us (2%)
    ppermute x11, waiting for transfers between devices, swap(): return lax.ppermute(value, ('expert', 'replica'), pairs)  68 us
    all_to_all x4, waiting for transfers between devices, exchange(): lax.all_to_all(rows.reshape(num_experts, -1, width), 'expert', split_axis...  61.1 us
    all_to_all x4, starting transfers between devices, exchange(): lax.all_to_all(rows.reshape(num_experts, -1, width), 'expert', split_axis...  43.9 us
    dot_general x16, matrix products, dot(): lax.dot_general(lhs, rhs, (((ldim,), (rdim,)), ((), ())), preferred_eleme...  25.9 us
    pallas_call x2, Pallas kernels, gradients(): pl.pallas_call(kernel, grid_spec=pltpu.PrefetchScalarGridSpec(num_scalar_...  14.7 us
    ppermute x11, starting transfers between devices, swap(): return lax.ppermute(value, ('expert', 'replica'), pairs)  12.7 us
    pallas_call x1, Pallas kernels, forward(): pl.pallas_call(kernel, grid_spec=pltpu.PrefetchScalarGridSpec(num_scalar_...  7.86 us
    ppermute x4, waiting for transfers between devices, share(): lax.ppermute(give, 'replica', list(enumerate(pairs))).astype(F32)  6.38 us
  transfers between devices with their start and end apart: 19, of which 8 were waited for; matrix products, arithmetic and copies ran while one was open for 15% of the time, Pallas kernels for 12%

profile of v4, /device:TPU:1, one launch (start us, length us, event | category | flops | bytes accessed | tf_op | source)
XLA Modules:
  0.0 273.8 jit_solution(7840026793785760646)
XLA Ops:
  5.0 13.3 %all-to-all-start = ((bf16[64,8,1280]{2,1,0:T(8,128)(2,1)}), bf16[64,8,1280]{2,1,0:T(8,128)(2,1)}, u32[]{:S(2)}, u32[]{:S(2)}) async-start(bf16[64,8,1280]{2,1,0:T(8,128)(2,1)} %fusion.4), calls=%async_computation | async-start | bytes 2621440 | tf_op jit(solution)/shard_map/all_to_all | solution.py:59
  20.4 31.9 %all-to-all-done = bf16[64,8,1280]{2,1,0:T(8,128)(2,1)} async-done(((bf16[64,8,1280]{2,1,0:T(8,128)(2,1)}), bf16[64,8,1280]{2,1,0:T(8,128)(2,1)}, u32[]{:S(2)}, u32[]{:S(2)}) %all-to-all-start) | async-done | bytes 1310752 | tf_op jit(solution)/shard_map/all_to_all | solution.py:59
  52.3 6.2 %all-to-all-start.2 = ((bf16[64,8,1280]{2,1,0:T(8,128)(2,1)}), bf16[64,8,1280]{2,1,0:T(8,128)(2,1)S(1)}, u32[]{:S(2)}, u32[]{:S(2)}) async-start(bf16[64,8,1280]{2,1,0:T(8,128)(2,1)} %fusion.5), calls=%async_computation.2 | async-start | bytes 2621440 | tf_op jit(solution)/shard_map/all_to_all | solution.py:59
  58.5 2.8 %collective-permute-start.3 = (bf16[2560,384]{1,0:T(8,128)(2,1)S(1)}, bf16[2560,384]{1,0:T(8,128)(2,1)}, u32[]{:S(2)}, u32[]{:S(2)}) collective-permute-start(bf16[2560,384]{1,0:T(8,128)(2,1)S(1)} %bitcast.63), channel_id=1, source_target_pairs={{0,1},{1,0},{2,3},{3,2},{4,7},{5,6},{6,5},{7,4},{8,9},{9,8},{10,11... | collective-permute-start | bytes 5898248 | tf_op jit(solution)/shard_map/ppermute | solution.py:20
  69.1 2.6 collective-permute-start.7
  72.4 2.3 dynamic-slice_bitcast_fusion.1
  74.6 40.7 %collective-permute-done.2 = bf16[384,1280]{1,0:T(8,128)(2,1)} collective-permute-done((bf16[384,1280]{1,0:T(8,128)(2,1)}, bf16[384,1280]{1,0:T(8,128)(2,1)}, u32[]{:S(2)}, u32[]{:S(2)}) %collective-permute-start.2) | collective-permute-done | bytes 983072 | tf_op jit(solution)/shard_map/ppermute | solution.py:20
  115.4 2.6 collective-permute-start.6
  117.9 5.3 %forward_near.1 = (f32[512,384]{1,0:T(8,128)}, f32[512,384]{1,0:T(8,128)}) custom-call(s32[4]{0:T(128)} %pad_add_fusion.order_ref, bf16[512,1280]{1,0:T(8,128)(2,1)} %bitcast.8.near_ref, bf16[2560,384]{1,0:T(8,128)(2,1)} %bitcast.60, bf16[2560,384]{1,0:T(8,128)(2,1)} %bitcast.65), custom_call_target="tpu_custom_call" | custom-call | tf_op jit(solution)/shard_map/forward_near/pallas_call | solution.py:90
  123.3 5.9 %forward_far.1 = (f32[512,384]{1,0:T(8,128)}, f32[512,384]{1,0:T(8,128)}, bf16[512,384]{1,0:T(8,128)(2,1)}) custom-call(s32[4]{0:T(128)} %pad_add_fusion.order_ref, bf16[512,1280]{1,0:T(8,128)(2,1)} %collective-permute-done.far_ref, f32[512,384]{1,0:T(8,128)} %get-tuple-element.16.gn_ref, f32[512,384]{1,0:T(8,128)} %get-tuple-element.17.un_ref, ...), custom_call_target="tpu_custom_call" | custom-call | tf_op jit(solution)/shard_map/forward_far/pallas_call | solution.py:125
  129.2 3.3 %convolution_convert_fusion.2 = bf16[512,384]{1,0:T(8,128)(2,1)} fusion(bf16[384,1280]{1,0:T(8,128)(2,1)} %collective-permute-done.2, bf16[64,8,1280]{2,1,0:T(8,128)(2,1)S(1)} %all-to-all-done.2), kind=kOutput, calls=%fused_computation.20 | convolution fusion | flops 503513088 | bytes 2686976 | tf_op jit(solution)/shard_map/dot_general | solution.py:32
  133.9 7.9 %forward.1 = (f32[512,384]{1,0:T(8,128)}, f32[512,384]{1,0:T(8,128)}, bf16[512,384]{1,0:T(8,128)(2,1)}) custom-call(s32[4]{0:T(128)} %pad_add_fusion.order_ref, bf16[512,1280]{1,0:T(8,128)(2,1)} %bitcast.8.near_ref, bf16[512,1280]{1,0:T(8,128)(2,1)} %collective-permute-done.far_ref, bf16[2560,384]{1,0:T(8,128)(2,1)} %collective-permute-done.3.gate_w_ref.gw_ref, ...), custom_call_target="tpu_custom_call" | custom-call | tf_op jit(solution)/shard_map/forward/pallas_call | solution.py:177
  141.8 4.7 %collective-permute-done.7.down_ref = bf16[384,1280]{1,0:T(8,128)(2,1)} collective-permute-done((bf16[384,1280]{1,0:T(8,128)(2,1)}, bf16[384,1280]{1,0:T(8,128)(2,1)}, u32[]{:S(2)}, u32[]{:S(2)}) %collective-permute-start.7) | collective-permute-done | bytes 983072 | tf_op jit(solution)/shard_map/ppermute | solution.py:20
  146.5 2.2 fusion.73
  148.7 2.3 fusion.72
  151.9 10.9 %collective-permute-done.6 = bf16[384,1280]{1,0:T(8,128)(2,1)} collective-permute-done((bf16[384,1280]{1,0:T(8,128)(2,1)}, bf16[384,1280]{1,0:T(8,128)(2,1)}, u32[]{:S(2)}, u32[]{:S(2)}) %collective-permute-start.6) | collective-permute-done | bytes 983072 | tf_op jit(solution)/shard_map/ppermute | solution.py:20
  166.2 10.4 %all-to-all-start.1 = ((bf16[64,8,1280]{2,1,0:T(8,128)(2,1)}), bf16[64,8,1280]{2,1,0:T(8,128)(2,1)}, u32[]{:S(2)}, u32[]{:S(2)}) async-start(bf16[64,8,1280]{2,1,0:T(8,128)(2,1)} %fusion.6), calls=%async_computation.1 | async-start | bytes 2621440 | tf_op jit(solution)/shard_map/all_to_all | solution.py:59
  176.6 2.2 convolution_convert_fusion.1
  182.9 7.3 %gradients.2 = (bf16[512,384]{1,0:T(8,128)(2,1)}, bf16[512,384]{1,0:T(8,128)(2,1)}, f32[512,1280]{1,0:T(8,128)}) custom-call(s32[4]{0:T(128)} %pad_add_fusion.order_ref, bf16[512,1280]{1,0:T(8,128)(2,1)} %bitcast.68, bf16[384,1280]{1,0:T(8,128)(2,1)} %pad_maximum_fusion.down_ref, bf16[512,384]{1,0:T(8,128)(2,1)} %collective-permute-done.10.in_ref, ...), custom_call_target="tpu_custom_call" | custom-call | tf_op jit(solution)/shard_map/gradients/pallas_call | solution.py:234
  190.1 7.4 %gradients.3 = (bf16[512,384]{1,0:T(8,128)(2,1)}, bf16[512,384]{1,0:T(8,128)(2,1)}, bf16[512,1280]{1,0:T(8,128)(2,1)}) custom-call(s32[4]{0:T(128)} %pad_add_fusion.order_ref, bf16[512,1280]{1,0:T(8,128)(2,1)} %bitcast.69, bf16[384,1280]{1,0:T(8,128)(2,1)} %collective-permute-done.7.down_ref, bf16[512,384]{1,0:T(8,128)(2,1)} %collective-permute-done.11.in_ref, ...), custom_call_target="tpu_custom_call" | custom-call | tf_op jit(solution)/shard_map/gradients/pallas_call | solution.py:234
  202.9 11.7 %collective-permute-done.12 = bf16[512,1280]{1,0:T(8,128)(2,1)S(1)} collective-permute-done((bf16[512,1280]{1,0:T(8,128)(2,1)}, bf16[512,1280]{1,0:T(8,128)(2,1)S(1)}, u32[]{:S(2)}, u32[]{:S(2)}) %collective-permute-start.12) | collective-permute-done | bytes 1310752 | tf_op jit(solution)/shard_map/ppermute | solution.py:20
  215.9 14.1 %all-to-all-start.3 = ((bf16[64,8,1280]{2,1,0:T(8,128)(2,1)}), bf16[64,8,1280]{2,1,0:T(8,128)(2,1)S(1)}, u32[]{:S(2)}, u32[]{:S(2)}) async-start(bf16[64,8,1280]{2,1,0:T(8,128)(2,1)} %fusion.7), calls=%async_computation.3 | async-start | bytes 2621440 | tf_op jit(solution)/shard_map/all_to_all | solution.py:59
  235.0 29.2 %all-to-all-done.3 = bf16[64,8,1280]{2,1,0:T(8,128)(2,1)S(1)} async-done(((bf16[64,8,1280]{2,1,0:T(8,128)(2,1)}), bf16[64,8,1280]{2,1,0:T(8,128)(2,1)S(1)}, u32[]{:S(2)}, u32[]{:S(2)}) %all-to-all-start.3) | async-done | bytes 1310752 | tf_op jit(solution)/shard_map/all_to_all | solution.py:59
  266.7 5.1 %collective-permute-done.13 = bf16[128,640]{1,0:T(8,128)(2,1)S(1)} collective-permute-done((bf16[128,640]{1,0:T(8,128)(2,1)S(1)}, bf16[128,640]{1,0:T(8,128)(2,1)S(1)}, u32[]{:S(2)}, u32[]{:S(2)}) %collective-permute-start.13) | collective-permute-done | bytes 163872 | tf_op jit(solution)/shard_map/ppermute | solution.py:341
  (96 shorter events, 40.6 us)
Async XLA Ops:
  0.6 2.7 copy-start.7
  5.0 13.6 %copy-start.8 = (bf16[128,2560]{1,0:T(8,128)(2,1)S(1)}, bf16[128,2560]{1,0:T(8,128)(2,1)}, u32[]{:S(2)}) copy-start(bf16[128,2560]{1,0:T(8,128)(2,1)} %param.13) | copy-start | bytes 1966084
  5.0 47.4 %all-to-all-start = ((bf16[64,8,1280]{2,1,0:T(8,128)(2,1)}), bf16[64,8,1280]{2,1,0:T(8,128)(2,1)}, u32[]{:S(2)}, u32[]{:S(2)}) async-start(bf16[64,8,1280]{2,1,0:T(8,128)(2,1)} %fusion.4), calls=%async_computation | async-start | bytes 2621440 | tf_op jit(solution)/shard_map/all_to_all | solution.py:59
  20.4 38.1 %copy-start = (bf16[1,2560,384]{2,1,0:T(8,128)(2,1)S(1)}, bf16[1,2560,384]{2,1,0:T(8,128)(2,1)}, u32[]{:S(2)}) copy-start(bf16[1,2560,384]{2,1,0:T(8,128)(2,1)} %param.10) | copy-start | bytes 5898244
  52.3 76.8 %all-to-all-start.2 = ((bf16[64,8,1280]{2,1,0:T(8,128)(2,1)}), bf16[64,8,1280]{2,1,0:T(8,128)(2,1)S(1)}, u32[]{:S(2)}, u32[]{:S(2)}) async-start(bf16[64,8,1280]{2,1,0:T(8,128)(2,1)} %fusion.5), calls=%async_computation.2 | async-start | bytes 2621440 | tf_op jit(solution)/shard_map/all_to_all | solution.py:59
  58.5 74.0 %collective-permute-start.3 = (bf16[2560,384]{1,0:T(8,128)(2,1)S(1)}, bf16[2560,384]{1,0:T(8,128)(2,1)}, u32[]{:S(2)}, u32[]{:S(2)}) collective-permute-start(bf16[2560,384]{1,0:T(8,128)(2,1)S(1)} %bitcast.63), channel_id=1, source_target_pairs={{0,1},{1,0},{2,3},{3,2},{4,7},{5,6},{6,5},{7,4},{8,9},{9,8},{10,11... | collective-permute-start | bytes 5898248 | tf_op jit(solution)/shard_map/ppermute | solution.py:20
  61.3 72.6 %collective-permute-start.4 = (bf16[2560,384]{1,0:T(8,128)(2,1)}, bf16[2560,384]{1,0:T(8,128)(2,1)}, u32[]{:S(2)}, u32[]{:S(2)}) collective-permute-start(bf16[2560,384]{1,0:T(8,128)(2,1)} %bitcast.64), channel_id=1, source_target_pairs={{0,1},{1,0},{2,3},{3,2},{4,7},{5,6},{6,5},{7,4},{8,9},{9,8},{10,11... | collective-permute-start | bytes 5898248 | tf_op jit(solution)/shard_map/ppermute | solution.py:20
  63.1 60.2 %collective-permute-start = (bf16[512,1280]{1,0:T(8,128)(2,1)}, bf16[512,1280]{1,0:T(8,128)(2,1)}, u32[]{:S(2)}, u32[]{:S(2)}) collective-permute-start(bf16[512,1280]{1,0:T(8,128)(2,1)} %bitcast.8.near_ref), channel_id=1, source_target_pairs={{0,3},{1,2},{2,1},{3,0},{4,5},{5,4},{6,7},{7,6},{8,11},{9,10},{10,... | collective-permute-start | bytes 3932168 | tf_op jit(solution)/shard_map/ppermute | solution.py:20
  64.2 51.1 %collective-permute-start.2 = (bf16[384,1280]{1,0:T(8,128)(2,1)}, bf16[384,1280]{1,0:T(8,128)(2,1)}, u32[]{:S(2)}, u32[]{:S(2)}) collective-permute-start(bf16[384,1280]{1,0:T(8,128)(2,1)} %pad_maximum_fusion.1), channel_id=1, source_target_pairs={{0,3},{1,2},{2,1},{3,0},{4,5},{5,4},{6,7},{7,6},{8,11},{9,10},{10,... | collective-permute-start | bytes 2949128 | tf_op jit(solution)/shard_map/ppermute | solution.py:20
  69.1 77.4 %collective-permute-start.7 = (bf16[384,1280]{1,0:T(8,128)(2,1)}, bf16[384,1280]{1,0:T(8,128)(2,1)}, u32[]{:S(2)}, u32[]{:S(2)}) collective-permute-start(bf16[384,1280]{1,0:T(8,128)(2,1)} %pad_maximum_fusion.down_ref), channel_id=1, source_target_pairs={{0,1},{1,0},{2,3},{3,2},{4,7},{5,6},{6,5},{7,4},{8,9},{9,8},{10,11... | collective-permute-start | bytes 2949128 | tf_op jit(solution)/shard_map/ppermute | solution.py:20
  115.4 47.5 %collective-permute-start.6 = (bf16[384,1280]{1,0:T(8,128)(2,1)}, bf16[384,1280]{1,0:T(8,128)(2,1)}, u32[]{:S(2)}, u32[]{:S(2)}) collective-permute-start(bf16[384,1280]{1,0:T(8,128)(2,1)} %collective-permute-done.2), channel_id=1, source_target_pairs={{0,1},{1,0},{2,3},{3,2},{4,7},{5,6},{6,5},{7,4},{8,9},{9,8},{10,11... | collective-permute-start | bytes 2949128 | tf_op jit(solution)/shard_map/ppermute | solution.py:20
  129.2 19.5 %collective-permute-start.1 = (bf16[512,384]{1,0:T(8,128)(2,1)}, bf16[512,384]{1,0:T(8,128)(2,1)}, u32[]{:S(2)}, u32[]{:S(2)}) collective-permute-start(bf16[512,384]{1,0:T(8,128)(2,1)} %get-tuple-element.18), channel_id=1, source_target_pairs={{0,3},{1,2},{2,1},{3,0},{4,5},{5,4},{6,7},{7,6},{8,11},{9,10},{10,... | collective-permute-start | bytes 1179656 | tf_op jit(solution)/shard_map/ppermute | solution.py:20
  129.2 47.4 %copy-start.2 = (bf16[64,8,1280]{2,1,0:T(8,128)(2,1)}, bf16[64,8,1280]{2,1,0:T(8,128)(2,1)S(1)}, u32[]{:S(2)}) copy-start(bf16[64,8,1280]{2,1,0:T(8,128)(2,1)S(1)} %all-to-all-done.2) | copy-start | bytes 3932164
  132.5 50.4 %collective-permute-start.10 = (bf16[512,384]{1,0:T(8,128)(2,1)}, bf16[512,384]{1,0:T(8,128)(2,1)}, u32[]{:S(2)}, u32[]{:S(2)}) collective-permute-start(bf16[512,384]{1,0:T(8,128)(2,1)} %convolution_convert_fusion.2), channel_id=1, source_target_pairs={{0,3},{1,2},{2,1},{3,0},{4,5},{5,4},{6,7},{7,6},{8,11},{9,10},{10,... | collective-permute-start | bytes 1179656 | tf_op jit(solution)/shard_map/ppermute | solution.py:20
  141.8 21.0 %collective-permute-start.5 = (bf16[512,384]{1,0:T(8,128)(2,1)}, bf16[512,384]{1,0:T(8,128)(2,1)S(1)}, u32[]{:S(2)}, u32[]{:S(2)}) collective-permute-start(bf16[512,384]{1,0:T(8,128)(2,1)} %get-tuple-element.19), channel_id=1, source_target_pairs={{0,3},{1,2},{2,1},{3,0},{4,5},{5,4},{6,7},{7,6},{8,11},{9,10},{10,... | collective-permute-start | bytes 1179656 | tf_op jit(solution)/shard_map/ppermute | solution.py:20
  166.2 49.8 %all-to-all-start.1 = ((bf16[64,8,1280]{2,1,0:T(8,128)(2,1)}), bf16[64,8,1280]{2,1,0:T(8,128)(2,1)}, u32[]{:S(2)}, u32[]{:S(2)}) async-start(bf16[64,8,1280]{2,1,0:T(8,128)(2,1)} %fusion.6), calls=%async_computation.1 | async-start | bytes 2621440 | tf_op jit(solution)/shard_map/all_to_all | solution.py:59
  176.6 3.6 %copy-start.1 = (bf16[1,2560,384]{2,1,0:T(8,128)(2,1)S(1)}, bf16[1,2560,384]{2,1,0:T(8,128)(2,1)}, u32[]{:S(2)}) copy-start(bf16[1,2560,384]{2,1,0:T(8,128)(2,1)} %param.10) | copy-start | bytes 5898244
  178.8 11.3 %collective-permute-start.11 = (bf16[512,384]{1,0:T(8,128)(2,1)S(1)}, bf16[512,384]{1,0:T(8,128)(2,1)}, u32[]{:S(2)}, u32[]{:S(2)}) collective-permute-start(bf16[512,384]{1,0:T(8,128)(2,1)S(1)} %convolution_convert_fusion.1), channel_id=1, source_target_pairs={{0,3},{1,2},{2,1},{3,0},{4,5},{5,4},{6,7},{7,6},{8,11},{9,10},{10,... | collective-permute-start | bytes 1179656 | tf_op jit(solution)/shard_map/ppermute | solution.py:20
  197.6 17.0 %collective-permute-start.12 = (bf16[512,1280]{1,0:T(8,128)(2,1)}, bf16[512,1280]{1,0:T(8,128)(2,1)S(1)}, u32[]{:S(2)}, u32[]{:S(2)}) collective-permute-start(bf16[512,1280]{1,0:T(8,128)(2,1)} %get-tuple-element.29), channel_id=1, source_target_pairs={{0,3},{1,2},{2,1},{3,0},{4,5},{5,4},{6,7},{7,6},{8,11},{9,10},{10,... | collective-permute-start | bytes 3932168 | tf_op jit(solution)/shard_map/ppermute | solution.py:20
  215.9 48.3 %all-to-all-start.3 = ((bf16[64,8,1280]{2,1,0:T(8,128)(2,1)}), bf16[64,8,1280]{2,1,0:T(8,128)(2,1)S(1)}, u32[]{:S(2)}, u32[]{:S(2)}) async-start(bf16[64,8,1280]{2,1,0:T(8,128)(2,1)} %fusion.7), calls=%async_computation.3 | async-start | bytes 2621440 | tf_op jit(solution)/shard_map/all_to_all | solution.py:59
  234.8 31.1 %collective-permute-start.8 = (bf16[128,640]{1,0:T(8,128)(2,1)S(1)}, bf16[128,640]{1,0:T(8,128)(2,1)S(1)}, u32[]{:S(2)}, u32[]{:S(2)}) collective-permute-start(bf16[128,640]{1,0:T(8,128)(2,1)S(1)} %get-tuple-element.46), channel_id=1, source_target_pairs={{0,1},{1,0},{2,3},{3,2},{4,5},{5,4},{6,7},{7,6},{8,9},{9,8},{10,11... | collective-permute-start | bytes 491528 | tf_op jit(solution)/shard_map/ppermute | solution.py:341
  234.9 31.0 %collective-permute-start.9 = (bf16[128,640]{1,0:T(8,128)(2,1)S(1)}, bf16[128,640]{1,0:T(8,128)(2,1)S(1)}, u32[]{:S(2)}, u32[]{:S(2)}) collective-permute-start(bf16[128,640]{1,0:T(8,128)(2,1)S(1)} %get-tuple-element.47), channel_id=1, source_target_pairs={{0,3},{1,2},{2,1},{3,0},{4,7},{5,6},{6,5},{7,4},{8,11},{9,10},{10,... | collective-permute-start | bytes 491528 | tf_op jit(solution)/shard_map/ppermute | solution.py:341
  265.7 6.0 %collective-permute-start.13 = (bf16[128,640]{1,0:T(8,128)(2,1)S(1)}, bf16[128,640]{1,0:T(8,128)(2,1)S(1)}, u32[]{:S(2)}, u32[]{:S(2)}) collective-permute-start(bf16[128,640]{1,0:T(8,128)(2,1)S(1)} %get-tuple-element.44), channel_id=1, source_target_pairs={{0,1},{1,0},{2,3},{3,2},{4,5},{5,4},{6,7},{7,6},{8,9},{9,8},{10,11... | collective-permute-start | bytes 491528 | tf_op jit(solution)/shard_map/ppermute | solution.py:341
  265.8 7.2 %collective-permute-start.14 = (bf16[128,640]{1,0:T(8,128)(2,1)S(1)}, bf16[128,640]{1,0:T(8,128)(2,1)S(1)}, u32[]{:S(2)}, u32[]{:S(2)}) collective-permute-start(bf16[128,640]{1,0:T(8,128)(2,1)S(1)} %get-tuple-element.45), channel_id=1, source_target_pairs={{0,3},{1,2},{2,1},{3,0},{4,7},{5,6},{6,5},{7,4},{8,11},{9,10},{10,... | collective-permute-start | bytes 491528 | tf_op jit(solution)/shard_map/ppermute | solution.py:341
  (10 other events, 15.9 us)

commit v5 on v4

--- a/solution.py
+++ b/solution.py
@@ -196,52 +196,84 @@
     )(order, near, far, gate_w, up_w)
 
 
-def gradients(order, grad_rows, down, hidden_in, gate, up, gate_w, up_w, base, dtype):
+def gradients(order, grad_rows, first, second):
     rows, half = grad_rows.shape
-    hidden_units = gate_w.shape[1]
+    hidden_units = first[2].shape[1]
     step = half // 2
 
-    def kernel(order_ref, c_ref, down_ref, in_ref, gate_ref, up_ref, gw_ref, uw_ref, *rest):
-        base_ref = None if base is None else rest[0]
-        gg_ref, ug_ref, out_ref = rest[-3:]
-
-        @pl.when(pl.program_id(0) == 0)
-        def _():
-            hidden_grad = dot(c_ref[...], down_ref[...], 1, 1) + in_ref[...].astype(F32)
+    def kernel(order_ref, c_hbm, *refs):
+        sources, outs = (refs[:6], refs[6:12]), refs[12:17]
+        far_ref = outs[4]
+        c_ref, scratch, sem = refs[17], (refs[18:24], refs[24:30]), refs[30]
+        copies = []
+
+        def start(source, target):
+            copy = pltpu.make_async_copy(source, target, sem.at[len(copies)])
+            copy.start()
+            copies.append(copy)
+            return copy
+
+        c_copy = start(c_hbm, c_ref)
+        small = [[start(sources[s][k], scratch[s][k]) for k in range(4)] for s in range(2)]
+        large = [
+            [
+                start(
+                    sources[s][4 + k].at[pl.ds(order_ref[2 + n] * step, step), :],
+                    scratch[s][4 + k].at[pl.ds(n * step, step), :],
+                )
+                for s in range(2)
+                for k in range(2)
+            ]
+            for n in range(2)
+        ]
+        c_copy.wait()
+        for s in range(2):
+            down_ref, in_ref, gate_ref, up_ref = scratch[s][:4]
+            gg_ref, ug_ref = outs[2 * s], outs[2 * s + 1]
+            small[s][0].wait()
+            hidden_grad = dot(c_ref[...], down_ref[...], 1, 1)
+            for copy in small[s][1:]:
+                copy.wait()
+            hidden_grad = hidden_grad + in_ref[...].astype(F32)
             gate = gate_ref[...]
             sig = jax.nn.sigmoid(gate)
-            gg_ref[...] = (
-                hidden_grad * up_ref[...] * sig * (1.0 + gate * (1.0 - sig))
-            ).astype(BF)
+            up_part = up_ref[...] * sig * (1.0 + gate * (1.0 - sig))
+            gg_ref[...] = (hidden_grad * up_part).astype(BF)
             ug_ref[...] = (hidden_grad * (gate * sig)).astype(BF)
-
-        value = dot(gg_ref[...], gw_ref[...], 1, 1) + dot(ug_ref[...], uw_ref[...], 1, 1)
-        if base_ref is not None:
-            value = value + base_ref[...]
-        out_ref[...] = value.astype(dtype)
-
-    def whole(x):
-        return pl.BlockSpec(x.shape, lambda j, order_ref: (0, 0))
-
-    weight = pl.BlockSpec((step, hidden_units), lambda j, order_ref: (order_ref[2 + j], 0))
-    block = pl.BlockSpec((rows, step), lambda j, order_ref: (0, j))
-    operands = [grad_rows, down, hidden_in, gate, up, gate_w, up_w]
-    in_specs = [whole(x) for x in operands[:5]] + [weight, weight]
-    if base is not None:
-        operands.append(base)
-        in_specs.append(block)
+        for n in range(2):
+            for copy in large[n]:
+                copy.wait()
+            block = pl.ds(n * step, step)
+            value = dot(outs[0][...], scratch[0][4][block, :], 1, 1)
+            value += dot(outs[1][...], scratch[0][5][block, :], 1, 1)
+            value += dot(outs[2][...], scratch[1][4][block, :], 1, 1)
+            value += dot(outs[3][...], scratch[1][5][block, :], 1, 1)
+            far_ref[:, n * step : (n + 1) * step] = value.astype(BF)
+
+    wide = pltpu.VMEM((rows, hidden_units), F32)
+    weight = pltpu.VMEM((half, hidden_units), BF)
+    one_slice = [
+        pltpu.VMEM((hidden_units, half), BF),
+        pltpu.VMEM((rows, hidden_units), BF),
+        wide,
+        wide,
+        weight,
+        weight,
+    ]
+    anywhere = pl.BlockSpec(memory_space=pl.ANY)
     grad = jax.ShapeDtypeStruct((rows, hidden_units), BF)
     return pl.pallas_call(
         kernel,
-        grid_spec=pltpu.PrefetchScalarGridSpec(
-            num_scalar_prefetch=1,
-            grid=(2,),
-            in_specs=in_specs,
-            out_specs=[whole(grad), whole(grad), block],
-        ),
-        out_shape=[grad, grad, jax.ShapeDtypeStruct((rows, half), dtype)],
+        in_specs=[pl.BlockSpec(memory_space=pltpu.SMEM)] + [anywhere] * 13,
+        out_shape=[grad, grad, grad, grad, jax.ShapeDtypeStruct((rows, half), BF)],
+        scratch_shapes=[
+            pltpu.VMEM((rows, half), BF),
+            *one_slice,
+            *one_slice,
+            pltpu.SemaphoreType.DMA((17,)),
+        ],
         name="gradients",
-    )(order, *operands)
+    )(order, grad_rows, *first, *second)
 
 
 def layer(tokens, expert_ids, route_weights, w_gate, w_up, w_down, cotangent):
@@ -316,11 +348,11 @@
     mixed_rows = (mixed_rows + dot(hidden_2, down_b)).astype(BF)
     mixed_back = exchange(mixed_rows, num_experts)
 
-    gg_1, ug_1, base = gradients(
-        order, grad_rows, down_own, hgrad_3, gate_1, up_1, gate_w, up_w, None, F32
-    )
-    gg_2, ug_2, far = gradients(
-        order, grad_rows, down_b, hgrad_4, gate_2, up_2, gate_b, up_b, base, BF
+    gg_1, ug_1, gg_2, ug_2, far = gradients(
+        order,
+        grad_rows,
+        (down_own, hgrad_3, gate_1, up_1, gate_w, up_w),
+        (down_b, hgrad_4, gate_2, up_2, gate_b, up_b),
     )
     far = swap_a(far)
     gate_1n = rows_of(gate_w, near_0, near_1)

time: 275 us -> 280 us (1.018)
  waiting for transfers between devices: 136 us -> 144 us
  Pallas kernels: 33.8 us -> 28.7 us
    ppermute x11, waiting for transfers between devices: 68 us -> 76.4 us  [swap(): return lax.ppermute(value, ('expert', 'replica'), pairs)]
    pallas_call x2 -> x1, Pallas kernels: 14.7 us -> 9.7 us  [gradients(): pl.pallas_call(kernel, in_specs=[pl.BlockSpec(memory_space=pltpu.SMEM)] +...]
  transfers between devices with their start and end apart: 19 -> 19, of which waited for: 8 -> 10; matrix products, arithmetic and copies ran while one was open for 15% -> 14% of each run, Pallas kernels for 12% -> 10%
where the time goes in v5:
time: 280 us; the launch traced here: 279 us
  waiting for transfers between devices  144 us (51%)
  starting transfers between devices  59.5 us (21%)
  Pallas kernels  28.7 us (10%)
  matrix products  26.2 us (9%)
  other arithmetic  14 us (5%)
  local copies, waits for them, and re-layouts  6.22 us (2%)
    ppermute x11, waiting for transfers between devices, swap(): return lax.ppermute(value, ('expert', 'replica'), pairs)  76.4 us
    all_to_all x4, waiting for transfers between devices, exchange(): lax.all_to_all(rows.reshape(num_experts, -1, width), 'expert', split_axis...  61 us
    all_to_all x4, starting transfers between devices, exchange(): lax.all_to_all(rows.reshape(num_experts, -1, width), 'expert', split_axis...  45.6 us
    dot_general x16, matrix products, dot(): lax.dot_general(lhs, rhs, (((ldim,), (rdim,)), ((), ())), preferred_eleme...  26.2 us
    ppermute x11, starting transfers between devices, swap(): return lax.ppermute(value, ('expert', 'replica'), pairs)  13.2 us
    pallas_call x1, Pallas kernels, gradients(): pl.pallas_call(kernel, in_specs=[pl.BlockSpec(memory_space=pltpu.SMEM)] +...  9.7 us
    pallas_call x1, Pallas kernels, forward(): pl.pallas_call(kernel, grid_spec=pltpu.PrefetchScalarGridSpec(num_scalar_...  7.8 us
    ppermute x4, waiting for transfers between devices, share(): lax.ppermute(give, 'replica', list(enumerate(pairs))).astype(F32)  6.23 us
  transfers between devices with their start and end apart: 19, of which 10 were waited for; matrix products, arithmetic and copies ran while one was open for 14% of the time, Pallas kernels for 10%

profile of v5, /device:TPU:1, one launch (start us, length us, event | category | flops | bytes accessed | tf_op | source)
XLA Modules:
  0.0 279.4 jit_solution(10413388714597163055)
XLA Ops:
  5.0 13.1 %all-to-all-start = ((bf16[64,8,1280]{2,1,0:T(8,128)(2,1)}), bf16[64,8,1280]{2,1,0:T(8,128)(2,1)S(1)}, u32[]{:S(2)}, u32[]{:S(2)}) async-start(bf16[64,8,1280]{2,1,0:T(8,128)(2,1)} %fusion.4), calls=%async_computation | async-start | bytes 2621440 | tf_op jit(solution)/shard_map/all_to_all | solution.py:59
  20.3 32.0 %all-to-all-done = bf16[64,8,1280]{2,1,0:T(8,128)(2,1)S(1)} async-done(((bf16[64,8,1280]{2,1,0:T(8,128)(2,1)}), bf16[64,8,1280]{2,1,0:T(8,128)(2,1)S(1)}, u32[]{:S(2)}, u32[]{:S(2)}) %all-to-all-start) | async-done | bytes 1310752 | tf_op jit(solution)/shard_map/all_to_all | solution.py:59
  52.3 6.3 %all-to-all-start.2 = ((bf16[64,8,1280]{2,1,0:T(8,128)(2,1)}), bf16[64,8,1280]{2,1,0:T(8,128)(2,1)}, u32[]{:S(2)}, u32[]{:S(2)}) async-start(bf16[64,8,1280]{2,1,0:T(8,128)(2,1)} %fusion.5), calls=%async_computation.2 | async-start | bytes 2621440 | tf_op jit(solution)/shard_map/all_to_all | solution.py:59
  65.4 16.9 %collective-permute-done.2 = bf16[384,1280]{1,0:T(8,128)(2,1)} collective-permute-done((bf16[384,1280]{1,0:T(8,128)(2,1)}, bf16[384,1280]{1,0:T(8,128)(2,1)}, u32[]{:S(2)}, u32[]{:S(2)}) %collective-permute-start.2) | collective-permute-done | bytes 983072 | tf_op jit(solution)/shard_map/ppermute | solution.py:20
  82.3 5.0 %collective-permute-start.6 = (bf16[384,1280]{1,0:T(8,128)(2,1)}, bf16[384,1280]{1,0:T(8,128)(2,1)}, u32[]{:S(2)}, u32[]{:S(2)}) collective-permute-start(bf16[384,1280]{1,0:T(8,128)(2,1)} %collective-permute-done.2), channel_id=1, source_target_pairs={{0,1},{1,0},{2,3},{3,2},{4,7},{5,6},{6,5},{7,4},{8,9},{9,8},{10,11... | collective-permute-start | bytes 2949128 | tf_op jit(solution)/shard_map/ppermute | solution.py:20
  91.3 5.3 %forward_near.1 = (f32[512,384]{1,0:T(8,128)}, f32[512,384]{1,0:T(8,128)}) custom-call(s32[4]{0:T(128)} %pad_add_fusion.order_ref, bf16[512,1280]{1,0:T(8,128)(2,1)} %bitcast.65, bf16[2560,384]{1,0:T(8,128)(2,1)} %bitcast.60, bf16[2560,384]{1,0:T(8,128)(2,1)} %bitcast.10.up_w_ref.refs_5_), custom_call_target="tpu_custom_call" | custom-call | tf_op jit(solution)/shard_map/forward_near/pallas_call | solution.py:90
  96.6 13.6 %collective-permute-done.far_ref = bf16[512,1280]{1,0:T(8,128)(2,1)} collective-permute-done((bf16[512,1280]{1,0:T(8,128)(2,1)S(1)}, bf16[512,1280]{1,0:T(8,128)(2,1)}, u32[]{:S(2)}, u32[]{:S(2)}) %collective-permute-start) | collective-permute-done | bytes 1310752 | tf_op jit(solution)/shard_map/ppermute | solution.py:20
  110.3 5.9 %forward_far.1 = (f32[512,384]{1,0:T(8,128)}, f32[512,384]{1,0:T(8,128)}, bf16[512,384]{1,0:T(8,128)(2,1)}) custom-call(s32[4]{0:T(128)} %pad_add_fusion.order_ref, bf16[512,1280]{1,0:T(8,128)(2,1)} %collective-permute-done.far_ref, f32[512,384]{1,0:T(8,128)} %get-tuple-element.15.gn_ref, f32[512,384]{1,0:T(8,128)} %get-tuple-element.16.un_ref, ...), custom_call_target="tpu_custom_call" | custom-call | tf_op jit(solution)/shard_map/forward_far/pallas_call | solution.py:125
  116.2 2.3 collective-permute-start.1
  118.5 29.3 %collective-permute-done.6 = bf16[384,1280]{1,0:T(8,128)(2,1)} collective-permute-done((bf16[384,1280]{1,0:T(8,128)(2,1)}, bf16[384,1280]{1,0:T(8,128)(2,1)}, u32[]{:S(2)}, u32[]{:S(2)}) %collective-permute-start.6) | collective-permute-done | bytes 983072 | tf_op jit(solution)/shard_map/ppermute | solution.py:20
  147.8 3.2 %convolution_convert_fusion.1 = bf16[512,384]{1,0:T(8,128)(2,1)} fusion(bf16[384,1280]{1,0:T(8,128)(2,1)} %collective-permute-done.6, bf16[64,8,1280]{2,1,0:T(8,128)(2,1)} %all-to-all-done.2), kind=kOutput, calls=%fused_computation.19 | convolution fusion | flops 503513088 | bytes 2686976 | tf_op jit(solution)/shard_map/dot_general | solution.py:32
  151.1 7.8 %forward.1 = (f32[512,384]{1,0:T(8,128)}, f32[512,384]{1,0:T(8,128)}, bf16[512,384]{1,0:T(8,128)(2,1)}) custom-call(s32[4]{0:T(128)} %pad_add_fusion.order_ref, bf16[512,1280]{1,0:T(8,128)(2,1)} %bitcast.66, bf16[512,1280]{1,0:T(8,128)(2,1)} %collective-permute-done.far_ref, bf16[2560,384]{1,0:T(8,128)(2,1)} %collective-permute-done.3.gate_w_ref.refs_10_, ...), custom_call_target="tpu_custom_call" | custom-call | tf_op jit(solution)/shard_map/forward/pallas_call | solution.py:177
  160.3 2.4 collective-permute-done.7.refs_6_
  162.7 2.2 fusion.73
  164.9 2.1 fusion.72
  171.3 11.7 %all-to-all-start.1 = ((bf16[64,8,1280]{2,1,0:T(8,128)(2,1)}), bf16[64,8,1280]{2,1,0:T(8,128)(2,1)}, u32[]{:S(2)}, u32[]{:S(2)}) async-start(bf16[64,8,1280]{2,1,0:T(8,128)(2,1)} %fusion.6), calls=%async_computation.1 | async-start | bytes 2621440 | tf_op jit(solution)/shard_map/all_to_all | solution.py:59
  183.1 2.6 convolution_convert_fusion.2
  187.4 2.1 constant_dynamic-slice_fusion.3
  190.8 2.3 collective-permute-done.10.refs_1_
  193.0 9.7 %gradients.1 = (bf16[512,384]{1,0:T(8,128)(2,1)}, bf16[512,384]{1,0:T(8,128)(2,1)}, bf16[512,384]{1,0:T(8,128)(2,1)}, bf16[512,384]{1,0:T(8,128)(2,1)}, bf16[512,1280]{1,0:T(8,128)(2,1)}) custom-call(s32[4]{0:T(128)} %pad_add_fusion.order_ref, bf16[512,1280]{1,0:T(8,128)(2,1)} %bitcast.16.c_hbm, bf16[384,1280]{1,0:T(8,128)(2,1)} %pad_maximum_fusion.refs_0_, ...), custom_call_target="tpu_custom_call" | custom-call | tf_op jit(solution)/shard_map/gradients/pallas_call | solution.py:265
  207.8 12.0 %collective-permute-done.12 = bf16[512,1280]{1,0:T(8,128)(2,1)S(1)} collective-permute-done((bf16[512,1280]{1,0:T(8,128)(2,1)}, bf16[512,1280]{1,0:T(8,128)(2,1)S(1)}, u32[]{:S(2)}, u32[]{:S(2)}) %collective-permute-start.12) | collective-permute-done | bytes 1310752 | tf_op jit(solution)/shard_map/ppermute | solution.py:20
  221.2 14.4 %all-to-all-start.3 = ((bf16[64,8,1280]{2,1,0:T(8,128)(2,1)}), bf16[64,8,1280]{2,1,0:T(8,128)(2,1)S(1)}, u32[]{:S(2)}, u32[]{:S(2)}) async-start(bf16[64,8,1280]{2,1,0:T(8,128)(2,1)} %fusion.7), calls=%async_computation.3 | async-start | bytes 2621440 | tf_op jit(solution)/shard_map/all_to_all | solution.py:59
  240.7 29.0 %all-to-all-done.3 = bf16[64,8,1280]{2,1,0:T(8,128)(2,1)S(1)} async-done(((bf16[64,8,1280]{2,1,0:T(8,128)(2,1)}), bf16[64,8,1280]{2,1,0:T(8,128)(2,1)S(1)}, u32[]{:S(2)}, u32[]{:S(2)}) %all-to-all-start.3) | async-done | bytes 1310752 | tf_op jit(solution)/shard_map/all_to_all | solution.py:59
  272.4 4.9 %collective-permute-done.13 = bf16[128,640]{1,0:T(8,128)(2,1)S(1)} collective-permute-done((bf16[128,640]{1,0:T(8,128)(2,1)S(1)}, bf16[128,640]{1,0:T(8,128)(2,1)S(1)}, u32[]{:S(2)}, u32[]{:S(2)}) %collective-permute-start.13) | collective-permute-done | bytes 163872 | tf_op jit(solution)/shard_map/ppermute | solution.py:373
  (90 shorter events, 42.1 us)
Async XLA Ops:
  0.6 2.7 copy-start.7
  5.0 13.5 %copy-start.8 = (bf16[128,2560]{1,0:T(8,128)(2,1)S(1)}, bf16[128,2560]{1,0:T(8,128)(2,1)}, u32[]{:S(2)}) copy-start(bf16[128,2560]{1,0:T(8,128)(2,1)} %param.13) | copy-start | bytes 1966084
  5.0 47.3 %all-to-all-start = ((bf16[64,8,1280]{2,1,0:T(8,128)(2,1)}), bf16[64,8,1280]{2,1,0:T(8,128)(2,1)S(1)}, u32[]{:S(2)}, u32[]{:S(2)}) async-start(bf16[64,8,1280]{2,1,0:T(8,128)(2,1)} %fusion.4), calls=%async_computation | async-start | bytes 2621440 | tf_op jit(solution)/shard_map/all_to_all | solution.py:59
  52.3 13.2 %copy-start.2 = (bf16[64,8,1280]{2,1,0:T(8,128)(2,1)}, bf16[64,8,1280]{2,1,0:T(8,128)(2,1)S(1)}, u32[]{:S(2)}) copy-start(bf16[64,8,1280]{2,1,0:T(8,128)(2,1)S(1)} %all-to-all-done) | copy-start | bytes 3932164
  52.3 95.6 %all-to-all-start.2 = ((bf16[64,8,1280]{2,1,0:T(8,128)(2,1)}), bf16[64,8,1280]{2,1,0:T(8,128)(2,1)}, u32[]{:S(2)}, u32[]{:S(2)}) async-start(bf16[64,8,1280]{2,1,0:T(8,128)(2,1)} %fusion.5), calls=%async_computation.2 | async-start | bytes 2621440 | tf_op jit(solution)/shard_map/all_to_all | solution.py:59
  58.6 4.1 %copy-start = (bf16[1,2560,384]{2,1,0:T(8,128)(2,1)S(1)}, bf16[1,2560,384]{2,1,0:T(8,128)(2,1)}, u32[]{:S(2)}) copy-start(bf16[1,2560,384]{2,1,0:T(8,128)(2,1)} %param.10) | copy-start | bytes 5898244
  61.5 20.8 %collective-permute-start.2 = (bf16[384,1280]{1,0:T(8,128)(2,1)}, bf16[384,1280]{1,0:T(8,128)(2,1)}, u32[]{:S(2)}, u32[]{:S(2)}) collective-permute-start(bf16[384,1280]{1,0:T(8,128)(2,1)} %pad_maximum_fusion.1), channel_id=1, source_target_pairs={{0,3},{1,2},{2,1},{3,0},{4,5},{5,4},{6,7},{7,6},{8,11},{9,10},{10,... | collective-permute-start | bytes 2949128 | tf_op jit(solution)/shard_map/ppermute | solution.py:20
  62.8 88.3 %collective-permute-start.3 = (bf16[2560,384]{1,0:T(8,128)(2,1)S(1)}, bf16[2560,384]{1,0:T(8,128)(2,1)}, u32[]{:S(2)}, u32[]{:S(2)}) collective-permute-start(bf16[2560,384]{1,0:T(8,128)(2,1)S(1)} %bitcast.63), channel_id=1, source_target_pairs={{0,1},{1,0},{2,3},{3,2},{4,7},{5,6},{6,5},{7,4},{8,9},{9,8},{10,11... | collective-permute-start | bytes 5898248 | tf_op jit(solution)/shard_map/ppermute | solution.py:20
  64.7 86.4 %collective-permute-start.4 = (bf16[2560,384]{1,0:T(8,128)(2,1)}, bf16[2560,384]{1,0:T(8,128)(2,1)}, u32[]{:S(2)}, u32[]{:S(2)}) collective-permute-start(bf16[2560,384]{1,0:T(8,128)(2,1)} %bitcast.10.up_w_ref.refs_5_), channel_id=1, source_target_pairs={{0,1},{1,0},{2,3},{3,2},{4,7},{5,6},{6,5},{7,4},{8,9},{9,8},{10,11... | collective-permute-start | bytes 5898248 | tf_op jit(solution)/shard_map/ppermute | solution.py:20
  65.4 44.8 %collective-permute-start = (bf16[512,1280]{1,0:T(8,128)(2,1)S(1)}, bf16[512,1280]{1,0:T(8,128)(2,1)}, u32[]{:S(2)}, u32[]{:S(2)}) collective-permute-start(bf16[512,1280]{1,0:T(8,128)(2,1)S(1)} %bitcast.64), channel_id=1, source_target_pairs={{0,3},{1,2},{2,1},{3,0},{4,5},{5,4},{6,7},{7,6},{8,11},{9,10},{10,... | collective-permute-start | bytes 3932168 | tf_op jit(solution)/shard_map/ppermute | solution.py:20
  82.3 65.5 %collective-permute-start.6 = (bf16[384,1280]{1,0:T(8,128)(2,1)}, bf16[384,1280]{1,0:T(8,128)(2,1)}, u32[]{:S(2)}, u32[]{:S(2)}) collective-permute-start(bf16[384,1280]{1,0:T(8,128)(2,1)} %collective-permute-done.2), channel_id=1, source_target_pairs={{0,1},{1,0},{2,3},{3,2},{4,7},{5,6},{6,5},{7,4},{8,9},{9,8},{10,11... | collective-permute-start | bytes 2949128 | tf_op jit(solution)/shard_map/ppermute | solution.py:20
  90.7 71.9 %collective-permute-start.7 = (bf16[384,1280]{1,0:T(8,128)(2,1)}, bf16[384,1280]{1,0:T(8,128)(2,1)}, u32[]{:S(2)}, u32[]{:S(2)}) collective-permute-start(bf16[384,1280]{1,0:T(8,128)(2,1)} %pad_maximum_fusion.refs_0_), channel_id=1, source_target_pairs={{0,1},{1,0},{2,3},{3,2},{4,7},{5,6},{6,5},{7,4},{8,9},{9,8},{10,11... | collective-permute-start | bytes 2949128 | tf_op jit(solution)/shard_map/ppermute | solution.py:20
  116.2 48.7 %collective-permute-start.1 = (bf16[512,384]{1,0:T(8,128)(2,1)}, bf16[512,384]{1,0:T(8,128)(2,1)S(1)}, u32[]{:S(2)}, u32[]{:S(2)}) collective-permute-start(bf16[512,384]{1,0:T(8,128)(2,1)} %get-tuple-element.17), channel_id=1, source_target_pairs={{0,3},{1,2},{2,1},{3,0},{4,5},{5,4},{6,7},{7,6},{8,11},{9,10},{10,... | collective-permute-start | bytes 1179656 | tf_op jit(solution)/shard_map/ppermute | solution.py:20
  151.1 39.7 %collective-permute-start.11 = (bf16[512,384]{1,0:T(8,128)(2,1)}, bf16[512,384]{1,0:T(8,128)(2,1)}, u32[]{:S(2)}, u32[]{:S(2)}) collective-permute-start(bf16[512,384]{1,0:T(8,128)(2,1)} %convolution_convert_fusion.1), channel_id=1, source_target_pairs={{0,3},{1,2},{2,1},{3,0},{4,5},{5,4},{6,7},{7,6},{8,11},{9,10},{10,... | collective-permute-start | bytes 1179656 | tf_op jit(solution)/shard_map/ppermute | solution.py:20
  158.9 9.0 %collective-permute-start.5 = (bf16[512,384]{1,0:T(8,128)(2,1)}, bf16[512,384]{1,0:T(8,128)(2,1)S(1)}, u32[]{:S(2)}, u32[]{:S(2)}) collective-permute-start(bf16[512,384]{1,0:T(8,128)(2,1)} %get-tuple-element.18), channel_id=1, source_target_pairs={{0,3},{1,2},{2,1},{3,0},{4,5},{5,4},{6,7},{7,6},{8,11},{9,10},{10,... | collective-permute-start | bytes 1179656 | tf_op jit(solution)/shard_map/ppermute | solution.py:20
  171.3 49.8 %all-to-all-start.1 = ((bf16[64,8,1280]{2,1,0:T(8,128)(2,1)}), bf16[64,8,1280]{2,1,0:T(8,128)(2,1)}, u32[]{:S(2)}, u32[]{:S(2)}) async-start(bf16[64,8,1280]{2,1,0:T(8,128)(2,1)} %fusion.6), calls=%async_computation.1 | async-start | bytes 2621440 | tf_op jit(solution)/shard_map/all_to_all | solution.py:59
  183.1 2.9 %copy-start.1 = (bf16[1,2560,384]{2,1,0:T(8,128)(2,1)S(1)}, bf16[1,2560,384]{2,1,0:T(8,128)(2,1)}, u32[]{:S(2)}) copy-start(bf16[1,2560,384]{2,1,0:T(8,128)(2,1)} %param.10) | copy-start | bytes 5898244
  185.7 7.3 %collective-permute-start.10 = (bf16[512,384]{1,0:T(8,128)(2,1)S(1)}, bf16[512,384]{1,0:T(8,128)(2,1)}, u32[]{:S(2)}, u32[]{:S(2)}) collective-permute-start(bf16[512,384]{1,0:T(8,128)(2,1)S(1)} %convolution_convert_fusion.2), channel_id=1, source_target_pairs={{0,3},{1,2},{2,1},{3,0},{4,5},{5,4},{6,7},{7,6},{8,11},{9,10},{10,... | collective-permute-start | bytes 1179656 | tf_op jit(solution)/shard_map/ppermute | solution.py:20
  202.7 17.1 %collective-permute-start.12 = (bf16[512,1280]{1,0:T(8,128)(2,1)}, bf16[512,1280]{1,0:T(8,128)(2,1)S(1)}, u32[]{:S(2)}, u32[]{:S(2)}) collective-permute-start(bf16[512,1280]{1,0:T(8,128)(2,1)} %get-tuple-element.27), channel_id=1, source_target_pairs={{0,3},{1,2},{2,1},{3,0},{4,5},{5,4},{6,7},{7,6},{8,11},{9,10},{10,... | collective-permute-start | bytes 3932168 | tf_op jit(solution)/shard_map/ppermute | solution.py:20
  221.2 48.6 %all-to-all-start.3 = ((bf16[64,8,1280]{2,1,0:T(8,128)(2,1)}), bf16[64,8,1280]{2,1,0:T(8,128)(2,1)S(1)}, u32[]{:S(2)}, u32[]{:S(2)}) async-start(bf16[64,8,1280]{2,1,0:T(8,128)(2,1)} %fusion.7), calls=%async_computation.3 | async-start | bytes 2621440 | tf_op jit(solution)/shard_map/all_to_all | solution.py:59
  240.4 31.3 %collective-permute-start.8 = (bf16[128,640]{1,0:T(8,128)(2,1)S(1)}, bf16[128,640]{1,0:T(8,128)(2,1)S(1)}, u32[]{:S(2)}, u32[]{:S(2)}) collective-permute-start(bf16[128,640]{1,0:T(8,128)(2,1)S(1)} %get-tuple-element.44), channel_id=1, source_target_pairs={{0,1},{1,0},{2,3},{3,2},{4,5},{5,4},{6,7},{7,6},{8,9},{9,8},{10,11... | collective-permute-start | bytes 491528 | tf_op jit(solution)/shard_map/ppermute | solution.py:373
  240.5 31.2 %collective-permute-start.9 = (bf16[128,640]{1,0:T(8,128)(2,1)S(1)}, bf16[128,640]{1,0:T(8,128)(2,1)S(1)}, u32[]{:S(2)}, u32[]{:S(2)}) collective-permute-start(bf16[128,640]{1,0:T(8,128)(2,1)S(1)} %get-tuple-element.45), channel_id=1, source_target_pairs={{0,3},{1,2},{2,1},{3,0},{4,7},{5,6},{6,5},{7,4},{8,11},{9,10},{10,... | collective-permute-start | bytes 491528 | tf_op jit(solution)/shard_map/ppermute | solution.py:373
  271.3 6.0 %collective-permute-start.13 = (bf16[128,640]{1,0:T(8,128)(2,1)S(1)}, bf16[128,640]{1,0:T(8,128)(2,1)S(1)}, u32[]{:S(2)}, u32[]{:S(2)}) collective-permute-start(bf16[128,640]{1,0:T(8,128)(2,1)S(1)} %get-tuple-element.42), channel_id=1, source_target_pairs={{0,1},{1,0},{2,3},{3,2},{4,5},{5,4},{6,7},{7,6},{8,9},{9,8},{10,11... | collective-permute-start | bytes 491528 | tf_op jit(solution)/shard_map/ppermute | solution.py:373
  271.4 7.2 %collective-permute-start.14 = (bf16[128,640]{1,0:T(8,128)(2,1)S(1)}, bf16[128,640]{1,0:T(8,128)(2,1)S(1)}, u32[]{:S(2)}, u32[]{:S(2)}) collective-permute-start(bf16[128,640]{1,0:T(8,128)(2,1)S(1)} %get-tuple-element.43), channel_id=1, source_target_pairs={{0,3},{1,2},{2,1},{3,0},{4,7},{5,6},{6,5},{7,4},{8,11},{9,10},{10,... | collective-permute-start | bytes 491528 | tf_op jit(solution)/shard_map/ppermute | solution.py:373
  (8 other events, 13.2 us)

commit v6 on v5

--- a/solution.py
+++ b/solution.py
@@ -196,15 +196,82 @@
     )(order, near, far, gate_w, up_w)
 
 
-def gradients(order, grad_rows, first, second):
+def partner_part(grad_rows, down_a, down_ab):
     rows, half = grad_rows.shape
-    hidden_units = first[2].shape[1]
+    hidden_units = down_a.shape[0]
+
+    def kernel(c_hbm, first_hbm, second_hbm, out_ref, c_ref, first_ref, second_ref, sem):
+        c_copy = pltpu.make_async_copy(c_hbm, c_ref, sem.at[0])
+        first = pltpu.make_async_copy(first_hbm, first_ref, sem.at[1])
+        second = pltpu.make_async_copy(second_hbm, second_ref, sem.at[2])
+        c_copy.start()
+        first.start()
+        second.start()
+        c_copy.wait()
+        first.wait()
+        out_ref[:, :hidden_units] = dot(c_ref[...], first_ref[...], 1, 1).astype(BF)
+        second.wait()
+        out_ref[:, hidden_units:] = dot(c_ref[...], second_ref[...], 1, 1).astype(BF)
+
+    weight = pltpu.VMEM((hidden_units, half), BF)
+    return pl.pallas_call(
+        kernel,
+        in_specs=[pl.BlockSpec(memory_space=pl.ANY)] * 3,
+        out_shape=jax.ShapeDtypeStruct((rows, 2 * hidden_units), BF),
+        scratch_shapes=[
+            pltpu.VMEM((rows, half), BF),
+            weight,
+            weight,
+            pltpu.SemaphoreType.DMA((3,)),
+        ],
+        name="partner_part",
+    )(grad_rows, down_a, down_ab)
+
+
+def mix_last(base, hidden_far, down_far, hidden_near, down_near):
+    rows, half = base.shape
     step = half // 2
 
-    def kernel(order_ref, c_hbm, *refs):
-        sources, outs = (refs[:6], refs[6:12]), refs[12:17]
+    def kernel(base_hbm, hf_hbm, df_hbm, hn_hbm, dn_hbm, out_ref, *refs):
+        scratch, sem = refs[:5], refs[5]
+        sources = (hf_hbm, df_hbm, hn_hbm, dn_hbm, base_hbm)
+        copies = [
+            pltpu.make_async_copy(source, target, sem.at[k])
+            for k, (source, target) in enumerate(zip(sources, scratch))
+        ]
+        for copy in copies:
+            copy.start()
+        hf_ref, df_ref, hn_ref, dn_ref, base_ref = scratch
+        for copy in copies:
+            copy.wait()
+        for n in range(2):
+            block = slice(n * step, (n + 1) * step)
+            value = dot(hf_ref[...], df_ref[:, block]) + dot(hn_ref[...], dn_ref[:, block])
+            out_ref[:, block] = (base_ref[:, block] + value).astype(BF)
+
+    operands = (hidden_far, down_far, hidden_near, down_near)
+    return pl.pallas_call(
+        kernel,
+        in_specs=[pl.BlockSpec(memory_space=pl.ANY)] * 5,
+        out_shape=jax.ShapeDtypeStruct((rows, half), BF),
+        scratch_shapes=[
+            *[pltpu.VMEM(x.shape, BF) for x in operands],
+            pltpu.VMEM((rows, half), F32),
+            pltpu.SemaphoreType.DMA((5,)),
+        ],
+        name="mix_last",
+    )(base, *operands)
+
+
+def gradients(order, grad_rows, received, first, second):
+    rows, half = grad_rows.shape
+    hidden_units = first[1].shape[1]
+    step = half // 2
+
+    def kernel(order_ref, c_hbm, in_hbm, *refs):
+        sources, outs = (refs[:5], refs[5:10]), refs[10:15]
         far_ref = outs[4]
-        c_ref, scratch, sem = refs[17], (refs[18:24], refs[24:30]), refs[30]
+        c_ref, in_ref, scratch, sem = refs[15], refs[16], (refs[17:22], refs[22:27]), refs[27]
         copies = []
 
         def start(source, target):
@@ -214,12 +281,14 @@
             return copy
 
         c_copy = start(c_hbm, c_ref)
-        small = [[start(sources[s][k], scratch[s][k]) for k in range(4)] for s in range(2)]
+        small = [[start(sources[0][k], scratch[0][k]) for k in range(3)]]
+        in_copy = start(in_hbm, in_ref)
+        small.append([start(sources[1][k], scratch[1][k]) for k in range(3)])
         large = [
             [
                 start(
-                    sources[s][4 + k].at[pl.ds(order_ref[2 + n] * step, step), :],
-                    scratch[s][4 + k].at[pl.ds(n * step, step), :],
+                    sources[s][3 + k].at[pl.ds(order_ref[2 + n] * step, step), :],
+                    scratch[s][3 + k].at[pl.ds(n * step, step), :],
                 )
                 for s in range(2)
                 for k in range(2)
@@ -228,13 +297,16 @@
         ]
         c_copy.wait()
         for s in range(2):
-            down_ref, in_ref, gate_ref, up_ref = scratch[s][:4]
+            down_ref, gate_ref, up_ref = scratch[s][:3]
             gg_ref, ug_ref = outs[2 * s], outs[2 * s + 1]
             small[s][0].wait()
             hidden_grad = dot(c_ref[...], down_ref[...], 1, 1)
             for copy in small[s][1:]:
                 copy.wait()
-            hidden_grad = hidden_grad + in_ref[...].astype(F32)
+            if s == 0:
+                in_copy.wait()
+            part = in_ref[:, s * hidden_units : (s + 1) * hidden_units]
+            hidden_grad = hidden_grad + part.astype(F32)
             gate = gate_ref[...]
             sig = jax.nn.sigmoid(gate)
             up_part = up_ref[...] * sig * (1.0 + gate * (1.0 - sig))
@@ -244,17 +316,16 @@
             for copy in large[n]:
                 copy.wait()
             block = pl.ds(n * step, step)
-            value = dot(outs[0][...], scratch[0][4][block, :], 1, 1)
-            value += dot(outs[1][...], scratch[0][5][block, :], 1, 1)
-            value += dot(outs[2][...], scratch[1][4][block, :], 1, 1)
-            value += dot(outs[3][...], scratch[1][5][block, :], 1, 1)
+            value = dot(outs[0][...], scratch[0][3][block, :], 1, 1)
+            value += dot(outs[1][...], scratch[0][4][block, :], 1, 1)
+            value += dot(outs[2][...], scratch[1][3][block, :], 1, 1)
+            value += dot(outs[3][...], scratch[1][4][block, :], 1, 1)
             far_ref[:, n * step : (n + 1) * step] = value.astype(BF)
 
     wide = pltpu.VMEM((rows, hidden_units), F32)
     weight = pltpu.VMEM((half, hidden_units), BF)
     one_slice = [
         pltpu.VMEM((hidden_units, half), BF),
-        pltpu.VMEM((rows, hidden_units), BF),
         wide,
         wide,
         weight,
@@ -264,16 +335,17 @@
     grad = jax.ShapeDtypeStruct((rows, hidden_units), BF)
     return pl.pallas_call(
         kernel,
-        in_specs=[pl.BlockSpec(memory_space=pltpu.SMEM)] + [anywhere] * 13,
+        in_specs=[pl.BlockSpec(memory_space=pltpu.SMEM)] + [anywhere] * 12,
         out_shape=[grad, grad, grad, grad, jax.ShapeDtypeStruct((rows, half), BF)],
         scratch_shapes=[
             pltpu.VMEM((rows, half), BF),
+            pltpu.VMEM((rows, 2 * hidden_units), BF),
             *one_slice,
             *one_slice,
-            pltpu.SemaphoreType.DMA((17,)),
+            pltpu.SemaphoreType.DMA((16,)),
         ],
         name="gradients",
-    )(order, grad_rows, *first, *second)
+    )(order, grad_rows, received, *first, *second)
 
 
 def layer(tokens, expert_ids, route_weights, w_gate, w_up, w_down, cotangent):
@@ -338,21 +410,20 @@
     gate_2, up_2, hidden_2 = forward(order, rows_near, rows_far, gate_b, up_b)
     hidden_3 = swap_a(hidden_1)
     hidden_4 = swap_a(hidden_2)
-    hgrad_3 = dot(grad_rows, down_a, 1, 1).astype(BF)
-    hgrad_3 = swap_a(hgrad_3)
-    hgrad_4 = dot(grad_rows, down_ab, 1, 1).astype(BF)
-    hgrad_4 = swap_a(hgrad_4)
+    hgrad = partner_part(grad_rows, down_a, down_ab)
+    hgrad = swap_a(hgrad)
 
     mixed_rows = dot(hidden_1, down_own) + dot(hidden_3, down_a)
-    mixed_rows = lax.optimization_barrier(mixed_rows + dot(hidden_4, down_ab))
-    mixed_rows = (mixed_rows + dot(hidden_2, down_b)).astype(BF)
+    mixed_rows = lax.optimization_barrier(mixed_rows)
+    mixed_rows = mix_last(mixed_rows, hidden_4, down_ab, hidden_2, down_b)
     mixed_back = exchange(mixed_rows, num_experts)
 
     gg_1, ug_1, gg_2, ug_2, far = gradients(
         order,
         grad_rows,
-        (down_own, hgrad_3, gate_1, up_1, gate_w, up_w),
-        (down_b, hgrad_4, gate_2, up_2, gate_b, up_b),
+        hgrad,
+        (down_own, gate_1, up_1, gate_w, up_w),
+        (down_b, gate_2, up_2, gate_b, up_b),
     )
     far = swap_a(far)
     gate_1n = rows_of(gate_w, near_0, near_1)

time: 280 us -> 277 us (0.989)
  waiting for transfers between devices: 144 us -> 134 us
  Pallas kernels: 28.7 us -> 38.5 us
  matrix products: 26.2 us -> 16.6 us
  starting transfers between devices: 59.5 us -> 64.3 us
    pallas_call x0 -> x2, Pallas kernels: none -> 9.69 us  [the longest x1 5.44 us: mix_last(): pl.pallas_call(kernel, in_specs=[pl.BlockSpec(memory_space=pl.ANY)] * 5,...]
    dot_general x16 -> x12, matrix products: 26.2 us -> 16.6 us  [dot(): lax.dot_general(lhs, rhs, (((ldim,), (rdim,)), ((), ())), preferred_eleme...]
    ppermute x11 -> x10, waiting for transfers between devices: 76.4 us -> 68.9 us  [swap(): return lax.ppermute(value, ('expert', 'replica'), pairs)]
    ppermute x11 -> x10, starting transfers between devices: 13.2 us -> 16.5 us  [swap(): return lax.ppermute(value, ('expert', 'replica'), pairs)]
    ppermute x4, starting transfers between devices: 0.7 us -> 3.6 us  [share(): lax.ppermute(give, 'replica', list(enumerate(pairs))).astype(F32)]
  transfers between devices with their start and end apart: 19 -> 18, of which waited for: 10 -> 10; matrix products, arithmetic and copies ran while one was open for 14% -> 11% of each run, Pallas kernels for 10% -> 14%
where the time goes in v6:
time: 277 us; the launch traced here: 276 us
  waiting for transfers between devices  134 us (48%)
  starting transfers between devices  64.3 us (23%)
  Pallas kernels  38.5 us (14%)
  matrix products  16.6 us (6%)
  other arithmetic  13.8 us (5%)
  local copies, waits for them, and re-layouts  7.44 us (3%)
    ppermute x10, waiting for transfers between devices, swap(): return lax.ppermute(value, ('expert', 'replica'), pairs)  68.9 us
    all_to_all x4, waiting for transfers between devices, exchange(): lax.all_to_all(rows.reshape(num_experts, -1, width), 'expert', split_axis...  60.4 us
    all_to_all x4, starting transfers between devices, exchange(): lax.all_to_all(rows.reshape(num_experts, -1, width), 'expert', split_axis...  44.2 us
    dot_general x12, matrix products, dot(): lax.dot_general(lhs, rhs, (((ldim,), (rdim,)), ((), ())), preferred_eleme...  16.6 us
    ppermute x10, starting transfers between devices, swap(): return lax.ppermute(value, ('expert', 'replica'), pairs)  16.5 us
    pallas_call x1, Pallas kernels, gradients(): pl.pallas_call(kernel, in_specs=[pl.BlockSpec(memory_space=pltpu.SMEM)] +...  9.74 us
    pallas_call x1, Pallas kernels, forward(): pl.pallas_call(kernel, grid_spec=pltpu.PrefetchScalarGridSpec(num_scalar_...  7.82 us
    pallas_call x1, Pallas kernels, forward_far(): pl.pallas_call(kernel, grid_spec=pltpu.PrefetchScalarGridSpec(num_scalar_...  5.95 us
  transfers between devices with their start and end apart: 18, of which 10 were waited for; matrix products, arithmetic and copies ran while one was open for 11% of the time, Pallas kernels for 14%

profile of v6, /device:TPU:1, one launch (start us, length us, event | category | flops | bytes accessed | tf_op | source)
XLA Modules:
  0.0 275.9 jit_solution(4152119182659961241)
XLA Ops:
  5.0 13.3 %all-to-all-start = ((bf16[64,8,1280]{2,1,0:T(8,128)(2,1)}), bf16[64,8,1280]{2,1,0:T(8,128)(2,1)}, u32[]{:S(2)}, u32[]{:S(2)}) async-start(bf16[64,8,1280]{2,1,0:T(8,128)(2,1)} %fusion.4), calls=%async_computation | async-start | bytes 2621440 | tf_op jit(solution)/shard_map/all_to_all | solution.py:59
  20.3 32.0 %all-to-all-done = bf16[64,8,1280]{2,1,0:T(8,128)(2,1)} async-done(((bf16[64,8,1280]{2,1,0:T(8,128)(2,1)}), bf16[64,8,1280]{2,1,0:T(8,128)(2,1)}, u32[]{:S(2)}, u32[]{:S(2)}) %all-to-all-start) | async-done | bytes 1310752 | tf_op jit(solution)/shard_map/all_to_all | solution.py:59
  52.3 6.2 %all-to-all-start.2 = ((bf16[64,8,1280]{2,1,0:T(8,128)(2,1)}), bf16[64,8,1280]{2,1,0:T(8,128)(2,1)S(1)}, u32[]{:S(2)}, u32[]{:S(2)}) async-start(bf16[64,8,1280]{2,1,0:T(8,128)(2,1)} %fusion.5), calls=%async_computation.2 | async-start | bytes 2621440 | tf_op jit(solution)/shard_map/all_to_all | solution.py:59
  64.5 16.4 %collective-permute-done.2.first_hbm = bf16[384,1280]{1,0:T(8,128)(2,1)} collective-permute-done((bf16[384,1280]{1,0:T(8,128)(2,1)S(1)}, bf16[384,1280]{1,0:T(8,128)(2,1)}, u32[]{:S(2)}, u32[]{:S(2)}) %collective-permute-start.2) | collective-permute-done | bytes 983072 | tf_op jit(solution)/shard_map/ppermute | solution.py:20
  80.9 5.1 %collective-permute-start.6 = (bf16[384,1280]{1,0:T(8,128)(2,1)}, bf16[384,1280]{1,0:T(8,128)(2,1)}, u32[]{:S(2)}, u32[]{:S(2)}) collective-permute-start(bf16[384,1280]{1,0:T(8,128)(2,1)} %collective-permute-done.2.first_hbm), channel_id=1, source_target_pairs={{0,1},{1,0},{2,3},{3,2},{4,7},{5,6},{6,5},{7,4},{8,9},{9,8},{10,11... | collective-permute-start | bytes 2949128 | tf_op jit(solution)/shard_map/ppermute | solution.py:20
  86.6 2.6 select_select_fusion.3
  89.2 5.3 %forward_near.1 = (f32[512,384]{1,0:T(8,128)}, f32[512,384]{1,0:T(8,128)}) custom-call(s32[4]{0:T(128)} %pad_add_fusion.order_ref, bf16[512,1280]{1,0:T(8,128)(2,1)} %bitcast.8.near_ref, bf16[2560,384]{1,0:T(8,128)(2,1)} %bitcast.49, bf16[2560,384]{1,0:T(8,128)(2,1)} %bitcast.10.up_w_ref.refs_4_), custom_call_target="tpu_custom_call" | custom-call | tf_op jit(solution)/shard_map/forward_near/pallas_call | solution.py:90
  94.5 14.6 %collective-permute-done.far_ref = bf16[512,1280]{1,0:T(8,128)(2,1)} collective-permute-done((bf16[512,1280]{1,0:T(8,128)(2,1)}, bf16[512,1280]{1,0:T(8,128)(2,1)}, u32[]{:S(2)}, u32[]{:S(2)}) %collective-permute-start) | collective-permute-done | bytes 1310752 | tf_op jit(solution)/shard_map/ppermute | solution.py:20
  109.1 5.9 %forward_far.1 = (f32[512,384]{1,0:T(8,128)}, f32[512,384]{1,0:T(8,128)}, bf16[512,384]{1,0:T(8,128)(2,1)}) custom-call(s32[4]{0:T(128)} %pad_add_fusion.order_ref, bf16[512,1280]{1,0:T(8,128)(2,1)} %collective-permute-done.far_ref, f32[512,384]{1,0:T(8,128)} %get-tuple-element.15.gn_ref, f32[512,384]{1,0:T(8,128)} %get-tuple-element.16.un_ref, ...), custom_call_target="tpu_custom_call" | custom-call | tf_op jit(solution)/shard_map/forward_far/pallas_call | solution.py:125
  115.0 2.2 collective-permute-start.1
  117.2 2.2 pad_maximum_fusion.refs_0_
  119.5 3.0 %collective-permute-start.7 = (bf16[384,1280]{1,0:T(8,128)(2,1)}, bf16[384,1280]{1,0:T(8,128)(2,1)}, u32[]{:S(2)}, u32[]{:S(2)}) collective-permute-start(bf16[384,1280]{1,0:T(8,128)(2,1)} %pad_maximum_fusion.refs_0_), channel_id=1, source_target_pairs={{0,1},{1,0},{2,3},{3,2},{4,7},{5,6},{6,5},{7,4},{8,9},{9,8},{10,11... | collective-permute-start | bytes 2949128 | tf_op jit(solution)/shard_map/ppermute | solution.py:20
  122.5 24.1 %collective-permute-done.6.df_hbm.second_hbm = bf16[384,1280]{1,0:T(8,128)(2,1)} collective-permute-done((bf16[384,1280]{1,0:T(8,128)(2,1)}, bf16[384,1280]{1,0:T(8,128)(2,1)}, u32[]{:S(2)}, u32[]{:S(2)}) %collective-permute-start.6) | collective-permute-done | bytes 983072 | tf_op jit(solution)/shard_map/ppermute | solution.py:20
  147.7 4.3 %partner_part.1 = bf16[512,768]{1,0:T(8,128)(2,1)} custom-call(bf16[512,1280]{1,0:T(8,128)(2,1)} %bitcast.53, bf16[384,1280]{1,0:T(8,128)(2,1)} %collective-permute-done.2.first_hbm, bf16[384,1280]{1,0:T(8,128)(2,1)} %collective-permute-done.6.df_hbm.second_hbm), custom_call_target="tpu_custom_call" | custom-call | tf_op jit(solution)/shard_map/partner_part/pallas_call | solution.py:217
  152.6 7.8 %forward.1 = (f32[512,384]{1,0:T(8,128)}, f32[512,384]{1,0:T(8,128)}, bf16[512,384]{1,0:T(8,128)(2,1)}) custom-call(s32[4]{0:T(128)} %pad_add_fusion.order_ref, bf16[512,1280]{1,0:T(8,128)(2,1)} %bitcast.8.near_ref, bf16[512,1280]{1,0:T(8,128)(2,1)} %collective-permute-done.far_ref, bf16[2560,384]{1,0:T(8,128)(2,1)} %collective-permute-done.3.gate_w_ref.refs_8_, ...), custom_call_target="tpu_custom_call" | custom-call | tf_op jit(solution)/shard_map/forward/pallas_call | solution.py:177
  163.8 2.3 convolution_add_fusion.1.base_hbm
  168.6 5.4 %mix_last.1 = bf16[512,1280]{1,0:T(8,128)(2,1)} custom-call(f32[512,1280]{1,0:T(8,128)} %convolution_add_fusion.1.base_hbm, bf16[512,384]{1,0:T(8,128)(2,1)} %copy-done.10, bf16[384,1280]{1,0:T(8,128)(2,1)} %collective-permute-done.6.df_hbm.second_hbm, bf16[512,384]{1,0:T(8,128)(2,1)} %get-tuple-element.18.hn_hbm, ...), custom_call_target="tpu_custom_call" | custom-call | tf_op jit(solution)/shard_map/mix_last/pallas_call | solution.py:253
  174.1 13.3 %all-to-all-start.1 = ((bf16[64,8,1280]{2,1,0:T(8,128)(2,1)}), bf16[64,8,1280]{2,1,0:T(8,128)(2,1)}, u32[]{:S(2)}, u32[]{:S(2)}) async-start(bf16[64,8,1280]{2,1,0:T(8,128)(2,1)} %bitcast.57), calls=%async_computation.1 | async-start | bytes 2621440 | tf_op jit(solution)/shard_map/all_to_all | solution.py:59
  187.4 2.2 dynamic-slice_bitcast_fusion.1
  192.2 9.7 %gradients.1 = (bf16[512,384]{1,0:T(8,128)(2,1)}, bf16[512,384]{1,0:T(8,128)(2,1)}, bf16[512,384]{1,0:T(8,128)(2,1)}, bf16[512,384]{1,0:T(8,128)(2,1)}, bf16[512,1280]{1,0:T(8,128)(2,1)}) custom-call(s32[4]{0:T(128)} %pad_add_fusion.order_ref, bf16[512,1280]{1,0:T(8,128)(2,1)} %bitcast.54, bf16[512,768]{1,0:T(8,128)(2,1)} %collective-permute-done.10.in_hbm, ...), custom_call_target="tpu_custom_call" | custom-call | tf_op jit(solution)/shard_map/gradients/pallas_call | solution.py:336
  207.2 12.1 %collective-permute-done.11 = bf16[512,1280]{1,0:T(8,128)(2,1)S(1)} collective-permute-done((bf16[512,1280]{1,0:T(8,128)(2,1)}, bf16[512,1280]{1,0:T(8,128)(2,1)S(1)}, u32[]{:S(2)}, u32[]{:S(2)}) %collective-permute-start.11) | collective-permute-done | bytes 1310752 | tf_op jit(solution)/shard_map/ppermute | solution.py:20
  221.5 11.4 %all-to-all-start.3 = ((bf16[64,8,1280]{2,1,0:T(8,128)(2,1)}), bf16[64,8,1280]{2,1,0:T(8,128)(2,1)S(1)}, u32[]{:S(2)}, u32[]{:S(2)}) async-start(bf16[64,8,1280]{2,1,0:T(8,128)(2,1)} %fusion.6), calls=%async_computation.3 | async-start | bytes 2621440 | tf_op jit(solution)/shard_map/all_to_all | solution.py:59
  239.5 27.6 %all-to-all-done.3 = bf16[64,8,1280]{2,1,0:T(8,128)(2,1)S(1)} async-done(((bf16[64,8,1280]{2,1,0:T(8,128)(2,1)}), bf16[64,8,1280]{2,1,0:T(8,128)(2,1)S(1)}, u32[]{:S(2)}, u32[]{:S(2)}) %all-to-all-start.3) | async-done | bytes 1310752 | tf_op jit(solution)/shard_map/all_to_all | solution.py:59
  270.3 4.7 %collective-permute-done.13 = bf16[128,640]{1,0:T(8,128)(2,1)S(1)} collective-permute-done((bf16[128,640]{1,0:T(8,128)(2,1)S(1)}, bf16[128,640]{1,0:T(8,128)(2,1)S(1)}, u32[]{:S(2)}, u32[]{:S(2)}) %collective-permute-start.13) | collective-permute-done | bytes 163872 | tf_op jit(solution)/shard_map/ppermute | solution.py:444
  (87 shorter events, 41.1 us)
Async XLA Ops:
  5.0 13.6 %copy-start.6 = (bf16[128,2560]{1,0:T(8,128)(2,1)S(1)}, bf16[128,2560]{1,0:T(8,128)(2,1)}, u32[]{:S(2)}) copy-start(bf16[128,2560]{1,0:T(8,128)(2,1)} %param.13) | copy-start | bytes 1966084
  5.0 47.4 %all-to-all-start = ((bf16[64,8,1280]{2,1,0:T(8,128)(2,1)}), bf16[64,8,1280]{2,1,0:T(8,128)(2,1)}, u32[]{:S(2)}, u32[]{:S(2)}) async-start(bf16[64,8,1280]{2,1,0:T(8,128)(2,1)} %fusion.4), calls=%async_computation | async-start | bytes 2621440 | tf_op jit(solution)/shard_map/all_to_all | solution.py:59
  52.3 94.3 %all-to-all-start.2 = ((bf16[64,8,1280]{2,1,0:T(8,128)(2,1)}), bf16[64,8,1280]{2,1,0:T(8,128)(2,1)S(1)}, u32[]{:S(2)}, u32[]{:S(2)}) async-start(bf16[64,8,1280]{2,1,0:T(8,128)(2,1)} %fusion.5), calls=%async_computation.2 | async-start | bytes 2621440 | tf_op jit(solution)/shard_map/all_to_all | solution.py:59
  60.4 20.5 %collective-permute-start.2 = (bf16[384,1280]{1,0:T(8,128)(2,1)S(1)}, bf16[384,1280]{1,0:T(8,128)(2,1)}, u32[]{:S(2)}, u32[]{:S(2)}) collective-permute-start(bf16[384,1280]{1,0:T(8,128)(2,1)S(1)} %pad_maximum_fusion.1), channel_id=1, source_target_pairs={{0,3},{1,2},{2,1},{3,0},{4,5},{5,4},{6,7},{7,6},{8,11},{9,10},{10,... | collective-permute-start | bytes 2949128 | tf_op jit(solution)/shard_map/ppermute | solution.py:20
  61.8 90.7 %collective-permute-start.3 = (bf16[2560,384]{1,0:T(8,128)(2,1)S(1)}, bf16[2560,384]{1,0:T(8,128)(2,1)}, u32[]{:S(2)}, u32[]{:S(2)}) collective-permute-start(bf16[2560,384]{1,0:T(8,128)(2,1)S(1)} %bitcast.52), channel_id=1, source_target_pairs={{0,1},{1,0},{2,3},{3,2},{4,7},{5,6},{6,5},{7,4},{8,9},{9,8},{10,11... | collective-permute-start | bytes 5898248 | tf_op jit(solution)/shard_map/ppermute | solution.py:20
  63.7 88.8 %collective-permute-start.4 = (bf16[2560,384]{1,0:T(8,128)(2,1)}, bf16[2560,384]{1,0:T(8,128)(2,1)}, u32[]{:S(2)}, u32[]{:S(2)}) collective-permute-start(bf16[2560,384]{1,0:T(8,128)(2,1)} %bitcast.10.up_w_ref.refs_4_), channel_id=1, source_target_pairs={{0,1},{1,0},{2,3},{3,2},{4,7},{5,6},{6,5},{7,4},{8,9},{9,8},{10,11... | collective-permute-start | bytes 5898248 | tf_op jit(solution)/shard_map/ppermute | solution.py:20
  64.5 44.6 %collective-permute-start = (bf16[512,1280]{1,0:T(8,128)(2,1)}, bf16[512,1280]{1,0:T(8,128)(2,1)}, u32[]{:S(2)}, u32[]{:S(2)}) collective-permute-start(bf16[512,1280]{1,0:T(8,128)(2,1)} %bitcast.8.near_ref), channel_id=1, source_target_pairs={{0,3},{1,2},{2,1},{3,0},{4,5},{5,4},{6,7},{7,6},{8,11},{9,10},{10,... | collective-permute-start | bytes 3932168 | tf_op jit(solution)/shard_map/ppermute | solution.py:20
  80.9 65.7 %collective-permute-start.6 = (bf16[384,1280]{1,0:T(8,128)(2,1)}, bf16[384,1280]{1,0:T(8,128)(2,1)}, u32[]{:S(2)}, u32[]{:S(2)}) collective-permute-start(bf16[384,1280]{1,0:T(8,128)(2,1)} %collective-permute-done.2.first_hbm), channel_id=1, source_target_pairs={{0,1},{1,0},{2,3},{3,2},{4,7},{5,6},{6,5},{7,4},{8,9},{9,8},{10,11... | collective-permute-start | bytes 2949128 | tf_op jit(solution)/shard_map/ppermute | solution.py:20
  115.0 46.6 %collective-permute-start.1 = (bf16[512,384]{1,0:T(8,128)(2,1)}, bf16[512,384]{1,0:T(8,128)(2,1)}, u32[]{:S(2)}, u32[]{:S(2)}) collective-permute-start(bf16[512,384]{1,0:T(8,128)(2,1)} %get-tuple-element.17), channel_id=1, source_target_pairs={{0,3},{1,2},{2,1},{3,0},{4,5},{5,4},{6,7},{7,6},{8,11},{9,10},{10,... | collective-permute-start | bytes 1179656 | tf_op jit(solution)/shard_map/ppermute | solution.py:20
  119.5 46.7 %collective-permute-start.7 = (bf16[384,1280]{1,0:T(8,128)(2,1)}, bf16[384,1280]{1,0:T(8,128)(2,1)}, u32[]{:S(2)}, u32[]{:S(2)}) collective-permute-start(bf16[384,1280]{1,0:T(8,128)(2,1)} %pad_maximum_fusion.refs_0_), channel_id=1, source_target_pairs={{0,1},{1,0},{2,3},{3,2},{4,7},{5,6},{6,5},{7,4},{8,9},{9,8},{10,11... | collective-permute-start | bytes 2949128 | tf_op jit(solution)/shard_map/ppermute | solution.py:20
  152.0 40.2 %collective-permute-start.10 = (bf16[512,768]{1,0:T(8,128)(2,1)}, bf16[512,768]{1,0:T(8,128)(2,1)}, u32[]{:S(2)}, u32[]{:S(2)}) collective-permute-start(bf16[512,768]{1,0:T(8,128)(2,1)} %partner_part.1), channel_id=1, source_target_pairs={{0,3},{1,2},{2,1},{3,0},{4,5},{5,4},{6,7},{7,6},{8,11},{9,10},{10,... | collective-permute-start | bytes 2359304 | tf_op jit(solution)/shard_map/ppermute | solution.py:20
  160.4 3.4 %copy-start.3 = (bf16[384,640]{1,0:T(8,128)(2,1)S(1)}, bf16[384,640]{1,0:T(8,128)(2,1)}, u32[]{:S(2)}) copy-start(bf16[384,640]{1,0:T(8,128)(2,1)} %get-tuple-element.38) | copy-start | bytes 1474564
  160.4 3.4 %copy-start.4 = (bf16[384,640]{1,0:T(8,128)(2,1)S(1)}, bf16[384,640]{1,0:T(8,128)(2,1)}, u32[]{:S(2)}) copy-start(bf16[384,640]{1,0:T(8,128)(2,1)} %get-tuple-element.39) | copy-start | bytes 1474564
  160.4 3.4 %copy-start.9 = (bf16[512,384]{1,0:T(8,128)(2,1)S(1)}, bf16[512,384]{1,0:T(8,128)(2,1)}, u32[]{:S(2)}) copy-start(bf16[512,384]{1,0:T(8,128)(2,1)} %get-tuple-element.17) | copy-start | bytes 1179652
  160.4 7.5 %collective-permute-start.5 = (bf16[512,384]{1,0:T(8,128)(2,1)}, bf16[512,384]{1,0:T(8,128)(2,1)S(1)}, u32[]{:S(2)}, u32[]{:S(2)}) collective-permute-start(bf16[512,384]{1,0:T(8,128)(2,1)} %get-tuple-element.18.hn_hbm), channel_id=1, source_target_pairs={{0,3},{1,2},{2,1},{3,0},{4,5},{5,4},{6,7},{7,6},{8,11},{9,10},{10,... | collective-permute-start | bytes 1179656 | tf_op jit(solution)/shard_map/ppermute | solution.py:20
  174.0 13.4 %copy-start.1 = (bf16[1,2560,384]{2,1,0:T(8,128)(2,1)S(1)}, bf16[1,2560,384]{2,1,0:T(8,128)(2,1)}, u32[]{:S(2)}) copy-start(bf16[1,2560,384]{2,1,0:T(8,128)(2,1)} %param.10) | copy-start | bytes 5898244
  174.1 47.4 %all-to-all-start.1 = ((bf16[64,8,1280]{2,1,0:T(8,128)(2,1)}), bf16[64,8,1280]{2,1,0:T(8,128)(2,1)}, u32[]{:S(2)}, u32[]{:S(2)}) async-start(bf16[64,8,1280]{2,1,0:T(8,128)(2,1)} %bitcast.57), calls=%async_computation.1 | async-start | bytes 2621440 | tf_op jit(solution)/shard_map/all_to_all | solution.py:59
  201.9 17.4 %collective-permute-start.11 = (bf16[512,1280]{1,0:T(8,128)(2,1)}, bf16[512,1280]{1,0:T(8,128)(2,1)S(1)}, u32[]{:S(2)}, u32[]{:S(2)}) collective-permute-start(bf16[512,1280]{1,0:T(8,128)(2,1)} %get-tuple-element.27), channel_id=1, source_target_pairs={{0,3},{1,2},{2,1},{3,0},{4,5},{5,4},{6,7},{7,6},{8,11},{9,10},{10,... | collective-permute-start | bytes 3932168 | tf_op jit(solution)/shard_map/ppermute | solution.py:20
  221.5 45.6 %all-to-all-start.3 = ((bf16[64,8,1280]{2,1,0:T(8,128)(2,1)}), bf16[64,8,1280]{2,1,0:T(8,128)(2,1)S(1)}, u32[]{:S(2)}, u32[]{:S(2)}) async-start(bf16[64,8,1280]{2,1,0:T(8,128)(2,1)} %fusion.6), calls=%async_computation.3 | async-start | bytes 2621440 | tf_op jit(solution)/shard_map/all_to_all | solution.py:59
  235.7 31.3 %copy-start.13 = (bf16[64,8,128]{2,0,1:T(8,128)(2,1)S(1)}, bf16[64,8,128]{2,0,1:T(8,128)(2,1)}, u32[]{:S(2)}) copy-start(bf16[64,8,128]{2,0,1:T(8,128)(2,1)} %get-tuple-element.61) | copy-start | bytes 393220
  237.7 31.8 %collective-permute-start.9 = (bf16[128,640]{1,0:T(8,128)(2,1)S(1)}, bf16[128,640]{1,0:T(8,128)(2,1)S(1)}, u32[]{:S(2)}, u32[]{:S(2)}) collective-permute-start(bf16[128,640]{1,0:T(8,128)(2,1)S(1)} %get-tuple-element.45), channel_id=1, source_target_pairs={{0,3},{1,2},{2,1},{3,0},{4,7},{5,6},{6,5},{7,4},{8,11},{9,10},{10,... | collective-permute-start | bytes 491528 | tf_op jit(solution)/shard_map/ppermute | solution.py:444
  239.5 30.0 %collective-permute-start.8 = (bf16[128,640]{1,0:T(8,128)(2,1)S(1)}, bf16[128,640]{1,0:T(8,128)(2,1)S(1)}, u32[]{:S(2)}, u32[]{:S(2)}) collective-permute-start(bf16[128,640]{1,0:T(8,128)(2,1)S(1)} %get-tuple-element.44), channel_id=1, source_target_pairs={{0,1},{1,0},{2,3},{3,2},{4,5},{5,4},{6,7},{7,6},{8,9},{9,8},{10,11... | collective-permute-start | bytes 491528 | tf_op jit(solution)/shard_map/ppermute | solution.py:444
  267.7 7.2 %collective-permute-start.13 = (bf16[128,640]{1,0:T(8,128)(2,1)S(1)}, bf16[128,640]{1,0:T(8,128)(2,1)S(1)}, u32[]{:S(2)}, u32[]{:S(2)}) collective-permute-start(bf16[128,640]{1,0:T(8,128)(2,1)S(1)} %get-tuple-element.43), channel_id=1, source_target_pairs={{0,3},{1,2},{2,1},{3,0},{4,7},{5,6},{6,5},{7,4},{8,11},{9,10},{10,... | collective-permute-start | bytes 491528 | tf_op jit(solution)/shard_map/ppermute | solution.py:444
  269.5 5.7 %collective-permute-start.12 = (bf16[128,640]{1,0:T(8,128)(2,1)S(1)}, bf16[128,640]{1,0:T(8,128)(2,1)S(1)}, u32[]{:S(2)}, u32[]{:S(2)}) collective-permute-start(bf16[128,640]{1,0:T(8,128)(2,1)S(1)} %get-tuple-element.42), channel_id=1, source_target_pairs={{0,1},{1,0},{2,3},{3,2},{4,5},{5,4},{6,7},{7,6},{8,9},{9,8},{10,11... | collective-permute-start | bytes 491528 | tf_op jit(solution)/shard_map/ppermute | solution.py:444
  (8 other events, 12.9 us)

commit v7 on v6

--- a/solution.py
+++ b/solution.py
@@ -226,41 +226,6 @@
         ],
         name="partner_part",
     )(grad_rows, down_a, down_ab)
-
-
-def mix_last(base, hidden_far, down_far, hidden_near, down_near):
-    rows, half = base.shape
-    step = half // 2
-
-    def kernel(base_hbm, hf_hbm, df_hbm, hn_hbm, dn_hbm, out_ref, *refs):
-        scratch, sem = refs[:5], refs[5]
-        sources = (hf_hbm, df_hbm, hn_hbm, dn_hbm, base_hbm)
-        copies = [
-            pltpu.make_async_copy(source, target, sem.at[k])
-            for k, (source, target) in enumerate(zip(sources, scratch))
-        ]
-        for copy in copies:
-            copy.start()
-        hf_ref, df_ref, hn_ref, dn_ref, base_ref = scratch
-        for copy in copies:
-            copy.wait()
-        for n in range(2):
-            block = slice(n * step, (n + 1) * step)
-            value = dot(hf_ref[...], df_ref[:, block]) + dot(hn_ref[...], dn_ref[:, block])
-            out_ref[:, block] = (base_ref[:, block] + value).astype(BF)
-
-    operands = (hidden_far, down_far, hidden_near, down_near)
-    return pl.pallas_call(
-        kernel,
-        in_specs=[pl.BlockSpec(memory_space=pl.ANY)] * 5,
-        out_shape=jax.ShapeDtypeStruct((rows, half), BF),
-        scratch_shapes=[
-            *[pltpu.VMEM(x.shape, BF) for x in operands],
-            pltpu.VMEM((rows, half), F32),
-            pltpu.SemaphoreType.DMA((5,)),
-        ],
-        name="mix_last",
-    )(base, *operands)
 
 
 def gradients(order, grad_rows, received, first, second):
@@ -415,7 +380,8 @@
 
     mixed_rows = dot(hidden_1, down_own) + dot(hidden_3, down_a)
     mixed_rows = lax.optimization_barrier(mixed_rows)
-    mixed_rows = mix_last(mixed_rows, hidden_4, down_ab, hidden_2, down_b)
+    mixed_rows = lax.optimization_barrier(mixed_rows + dot(hidden_4, down_ab))
+    mixed_rows = (mixed_rows + dot(hidden_2, down_b)).astype(BF)
     mixed_back = exchange(mixed_rows, num_experts)
 
     gg_1, ug_1, gg_2, ug_2, far = gradients(

time: 277 us -> 275 us (level)
  Pallas kernels: 38.5 us -> 33.1 us
  waiting for transfers between devices: 134 us -> 139 us
  starting transfers between devices: 64.3 us -> 60.7 us
  matrix products: 16.6 us -> 19.6 us
    pallas_call x1 -> x0, Pallas kernels: 5.44 us -> none  [mix_last(): pl.pallas_call(kernel, in_specs=[pl.BlockSpec(memory_space=pl.ANY)] * 5,...]
    ppermute x10, waiting for transfers between devices: 68.9 us -> 73.5 us  [swap(): return lax.ppermute(value, ('expert', 'replica'), pairs)]
    ppermute x10, starting transfers between devices: 16.5 us -> 13.2 us  [swap(): return lax.ppermute(value, ('expert', 'replica'), pairs)]
    dot_general x12 -> x14, matrix products: 16.6 us -> 19.6 us  [dot(): lax.dot_general(lhs, rhs, (((ldim,), (rdim,)), ((), ())), preferred_eleme...]
  transfers between devices with their start and end apart: 18 -> 18, of which waited for: 10 -> 10; matrix products, arithmetic and copies ran while one was open for 11% -> 12% of each run, Pallas kernels for 14% -> 12%
where the time goes in v7:
time: 275 us; the launch traced here: 274 us
  waiting for transfers between devices  139 us (51%)
  starting transfers between devices  60.7 us (22%)
  Pallas kernels  33.1 us (12%)
  matrix products  19.6 us (7%)
  other arithmetic  14 us (5%)
  local copies, waits for them, and re-layouts  6.68 us (2%)
    ppermute x10, waiting for transfers between devices, swap(): return lax.ppermute(value, ('expert', 'replica'), pairs)  73.5 us
    all_to_all x4, waiting for transfers between devices, exchange(): lax.all_to_all(rows.reshape(num_experts, -1, width), 'expert', split_axis...  60.4 us
    all_to_all x4, starting transfers between devices, exchange(): lax.all_to_all(rows.reshape(num_experts, -1, width), 'expert', split_axis...  44.1 us
    dot_general x14, matrix products, dot(): lax.dot_general(lhs, rhs, (((ldim,), (rdim,)), ((), ())), preferred_eleme...  19.6 us
    ppermute x10, starting transfers between devices, swap(): return lax.ppermute(value, ('expert', 'replica'), pairs)  13.2 us
    pallas_call x1, Pallas kernels, gradients(): pl.pallas_call(kernel, in_specs=[pl.BlockSpec(memory_space=pltpu.SMEM)] +...  9.76 us
    pallas_call x1, Pallas kernels, forward(): pl.pallas_call(kernel, grid_spec=pltpu.PrefetchScalarGridSpec(num_scalar_...  7.83 us
    pallas_call x1, Pallas kernels, forward_far(): pl.pallas_call(kernel, grid_spec=pltpu.PrefetchScalarGridSpec(num_scalar_...  5.92 us
  transfers between devices with their start and end apart: 18, of which 10 were waited for; matrix products, arithmetic and copies ran while one was open for 12% of the time, Pallas kernels for 12%

profile of v7, /device:TPU:1, one launch (start us, length us, event | category | flops | bytes accessed | tf_op | source)
XLA Modules:
  0.0 274.0 jit_solution(2594697510779013756)
XLA Ops:
  5.0 13.1 %all-to-all-start = ((bf16[64,8,1280]{2,1,0:T(8,128)(2,1)}), bf16[64,8,1280]{2,1,0:T(8,128)(2,1)S(1)}, u32[]{:S(2)}, u32[]{:S(2)}) async-start(bf16[64,8,1280]{2,1,0:T(8,128)(2,1)} %fusion.4), calls=%async_computation | async-start | bytes 2621440 | tf_op jit(solution)/shard_map/all_to_all | solution.py:59
  20.3 31.9 %all-to-all-done = bf16[64,8,1280]{2,1,0:T(8,128)(2,1)S(1)} async-done(((bf16[64,8,1280]{2,1,0:T(8,128)(2,1)}), bf16[64,8,1280]{2,1,0:T(8,128)(2,1)S(1)}, u32[]{:S(2)}, u32[]{:S(2)}) %all-to-all-start) | async-done | bytes 1310752 | tf_op jit(solution)/shard_map/all_to_all | solution.py:59
  52.3 6.2 %all-to-all-start.2 = ((bf16[64,8,1280]{2,1,0:T(8,128)(2,1)}), bf16[64,8,1280]{2,1,0:T(8,128)(2,1)S(1)}, u32[]{:S(2)}, u32[]{:S(2)}) async-start(bf16[64,8,1280]{2,1,0:T(8,128)(2,1)} %fusion.5), calls=%async_computation.2 | async-start | bytes 2621440 | tf_op jit(solution)/shard_map/all_to_all | solution.py:59
  62.6 1.9 collective-permute-start.3
  67.0 15.2 %collective-permute-done.2.first_hbm = bf16[384,1280]{1,0:T(8,128)(2,1)} collective-permute-done((bf16[384,1280]{1,0:T(8,128)(2,1)}, bf16[384,1280]{1,0:T(8,128)(2,1)}, u32[]{:S(2)}, u32[]{:S(2)}) %collective-permute-start.2) | collective-permute-done | bytes 983072 | tf_op jit(solution)/shard_map/ppermute | solution.py:20
  82.2 5.0 %collective-permute-start.6 = (bf16[384,1280]{1,0:T(8,128)(2,1)}, bf16[384,1280]{1,0:T(8,128)(2,1)}, u32[]{:S(2)}, u32[]{:S(2)}) collective-permute-start(bf16[384,1280]{1,0:T(8,128)(2,1)} %collective-permute-done.2.first_hbm), channel_id=1, source_target_pairs={{0,1},{1,0},{2,3},{3,2},{4,7},{5,6},{6,5},{7,4},{8,9},{9,8},{10,11... | collective-permute-start | bytes 2949128 | tf_op jit(solution)/shard_map/ppermute | solution.py:20
  88.9 5.3 %forward_near.1 = (f32[512,384]{1,0:T(8,128)}, f32[512,384]{1,0:T(8,128)}) custom-call(s32[4]{0:T(128)} %pad_add_fusion.order_ref, bf16[512,1280]{1,0:T(8,128)(2,1)} %bitcast.61, bf16[2560,384]{1,0:T(8,128)(2,1)} %bitcast.54, bf16[2560,384]{1,0:T(8,128)(2,1)} %bitcast.10.up_w_ref.refs_4_), custom_call_target="tpu_custom_call" | custom-call | tf_op jit(solution)/shard_map/forward_near/pallas_call | solution.py:90
  94.2 16.1 %collective-permute-done.far_ref = bf16[512,1280]{1,0:T(8,128)(2,1)} collective-permute-done((bf16[512,1280]{1,0:T(8,128)(2,1)}, bf16[512,1280]{1,0:T(8,128)(2,1)}, u32[]{:S(2)}, u32[]{:S(2)}) %collective-permute-start) | collective-permute-done | bytes 1310752 | tf_op jit(solution)/shard_map/ppermute | solution.py:20
  110.3 5.9 %forward_far.1 = (f32[512,384]{1,0:T(8,128)}, f32[512,384]{1,0:T(8,128)}, bf16[512,384]{1,0:T(8,128)(2,1)}) custom-call(s32[4]{0:T(128)} %pad_add_fusion.order_ref, bf16[512,1280]{1,0:T(8,128)(2,1)} %collective-permute-done.far_ref, f32[512,384]{1,0:T(8,128)} %get-tuple-element.15.gn_ref, f32[512,384]{1,0:T(8,128)} %get-tuple-element.16.un_ref, ...), custom_call_target="tpu_custom_call" | custom-call | tf_op jit(solution)/shard_map/forward_far/pallas_call | solution.py:125
  116.2 2.2 collective-permute-start.1
  118.4 29.2 %collective-permute-done.6.second_hbm = bf16[384,1280]{1,0:T(8,128)(2,1)} collective-permute-done((bf16[384,1280]{1,0:T(8,128)(2,1)}, bf16[384,1280]{1,0:T(8,128)(2,1)}, u32[]{:S(2)}, u32[]{:S(2)}) %collective-permute-start.6) | collective-permute-done | bytes 983072 | tf_op jit(solution)/shard_map/ppermute | solution.py:20
  148.8 4.3 %partner_part.1 = bf16[512,768]{1,0:T(8,128)(2,1)} custom-call(bf16[512,1280]{1,0:T(8,128)(2,1)} %bitcast.58, bf16[384,1280]{1,0:T(8,128)(2,1)} %collective-permute-done.2.first_hbm, bf16[384,1280]{1,0:T(8,128)(2,1)} %collective-permute-done.6.second_hbm), custom_call_target="tpu_custom_call" | custom-call | tf_op jit(solution)/shard_map/partner_part/pallas_call | solution.py:217
  153.4 7.8 %forward.1 = (f32[512,384]{1,0:T(8,128)}, f32[512,384]{1,0:T(8,128)}, bf16[512,384]{1,0:T(8,128)(2,1)}) custom-call(s32[4]{0:T(128)} %pad_add_fusion.order_ref, bf16[512,1280]{1,0:T(8,128)(2,1)} %bitcast.62, bf16[512,1280]{1,0:T(8,128)(2,1)} %collective-permute-done.far_ref, bf16[2560,384]{1,0:T(8,128)(2,1)} %collective-permute-done.3.gate_w_ref.refs_8_, ...), custom_call_target="tpu_custom_call" | custom-call | tf_op jit(solution)/shard_map/forward/pallas_call | solution.py:177
  162.6 2.2 fusion.71
  164.8 2.3 fusion.70
  168.9 2.1 convolution_add_fusion.1
  172.2 13.3 %all-to-all-start.1 = ((bf16[64,8,1280]{2,1,0:T(8,128)(2,1)}), bf16[64,8,1280]{2,1,0:T(8,128)(2,1)}, u32[]{:S(2)}, u32[]{:S(2)}) async-start(bf16[64,8,1280]{2,1,0:T(8,128)(2,1)} %fusion.6), calls=%async_computation.1 | async-start | bytes 2621440 | tf_op jit(solution)/shard_map/all_to_all | solution.py:59
  185.6 2.2 dynamic-slice_bitcast_fusion.1
  190.3 9.8 %gradients.1 = (bf16[512,384]{1,0:T(8,128)(2,1)}, bf16[512,384]{1,0:T(8,128)(2,1)}, bf16[512,384]{1,0:T(8,128)(2,1)}, bf16[512,384]{1,0:T(8,128)(2,1)}, bf16[512,1280]{1,0:T(8,128)(2,1)}) custom-call(s32[4]{0:T(128)} %pad_add_fusion.order_ref, bf16[512,1280]{1,0:T(8,128)(2,1)} %bitcast.59, bf16[512,768]{1,0:T(8,128)(2,1)} %collective-permute-done.10.in_hbm, ...), custom_call_target="tpu_custom_call" | custom-call | tf_op jit(solution)/shard_map/gradients/pallas_call | solution.py:301
  200.4 1.9 fusion.20
  205.4 12.1 %collective-permute-done.11 = bf16[512,1280]{1,0:T(8,128)(2,1)S(1)} collective-permute-done((bf16[512,1280]{1,0:T(8,128)(2,1)}, bf16[512,1280]{1,0:T(8,128)(2,1)S(1)}, u32[]{:S(2)}, u32[]{:S(2)}) %collective-permute-start.11) | collective-permute-done | bytes 1310752 | tf_op jit(solution)/shard_map/ppermute | solution.py:20
  219.6 11.5 %all-to-all-start.3 = ((bf16[64,8,1280]{2,1,0:T(8,128)(2,1)}), bf16[64,8,1280]{2,1,0:T(8,128)(2,1)S(1)}, u32[]{:S(2)}, u32[]{:S(2)}) async-start(bf16[64,8,1280]{2,1,0:T(8,128)(2,1)} %fusion.7), calls=%async_computation.3 | async-start | bytes 2621440 | tf_op jit(solution)/shard_map/all_to_all | solution.py:59
  237.7 27.7 %all-to-all-done.3 = bf16[64,8,1280]{2,1,0:T(8,128)(2,1)S(1)} async-done(((bf16[64,8,1280]{2,1,0:T(8,128)(2,1)}), bf16[64,8,1280]{2,1,0:T(8,128)(2,1)S(1)}, u32[]{:S(2)}, u32[]{:S(2)}) %all-to-all-start.3) | async-done | bytes 1310752 | tf_op jit(solution)/shard_map/all_to_all | solution.py:59
  268.4 3.6 %collective-permute-done.12 = bf16[128,640]{1,0:T(8,128)(2,1)S(1)} collective-permute-done((bf16[128,640]{1,0:T(8,128)(2,1)S(1)}, bf16[128,640]{1,0:T(8,128)(2,1)S(1)}, u32[]{:S(2)}, u32[]{:S(2)}) %collective-permute-start.12) | collective-permute-done | bytes 163872 | tf_op jit(solution)/shard_map/ppermute | solution.py:410
  (93 shorter events, 40.2 us)
Async XLA Ops:
  5.0 13.5 %copy-start.9 = (bf16[128,2560]{1,0:T(8,128)(2,1)S(1)}, bf16[128,2560]{1,0:T(8,128)(2,1)}, u32[]{:S(2)}) copy-start(bf16[128,2560]{1,0:T(8,128)(2,1)} %param.13) | copy-start | bytes 1966084
  5.0 47.3 %all-to-all-start = ((bf16[64,8,1280]{2,1,0:T(8,128)(2,1)}), bf16[64,8,1280]{2,1,0:T(8,128)(2,1)S(1)}, u32[]{:S(2)}, u32[]{:S(2)}) async-start(bf16[64,8,1280]{2,1,0:T(8,128)(2,1)} %fusion.4), calls=%async_computation | async-start | bytes 2621440 | tf_op jit(solution)/shard_map/all_to_all | solution.py:59
  52.3 6.2 %copy-start.3 = (bf16[64,8,1280]{2,1,0:T(8,128)(2,1)}, bf16[64,8,1280]{2,1,0:T(8,128)(2,1)S(1)}, u32[]{:S(2)}) copy-start(bf16[64,8,1280]{2,1,0:T(8,128)(2,1)S(1)} %all-to-all-done) | copy-start | bytes 3932164
  52.3 95.3 %all-to-all-start.2 = ((bf16[64,8,1280]{2,1,0:T(8,128)(2,1)}), bf16[64,8,1280]{2,1,0:T(8,128)(2,1)S(1)}, u32[]{:S(2)}, u32[]{:S(2)}) async-start(bf16[64,8,1280]{2,1,0:T(8,128)(2,1)} %fusion.5), calls=%async_computation.2 | async-start | bytes 2621440 | tf_op jit(solution)/shard_map/all_to_all | solution.py:59
  61.3 20.9 %collective-permute-start.2 = (bf16[384,1280]{1,0:T(8,128)(2,1)}, bf16[384,1280]{1,0:T(8,128)(2,1)}, u32[]{:S(2)}, u32[]{:S(2)}) collective-permute-start(bf16[384,1280]{1,0:T(8,128)(2,1)} %pad_maximum_fusion.1), channel_id=1, source_target_pairs={{0,3},{1,2},{2,1},{3,0},{4,5},{5,4},{6,7},{7,6},{8,11},{9,10},{10,... | collective-permute-start | bytes 2949128 | tf_op jit(solution)/shard_map/ppermute | solution.py:20
  62.6 90.8 %collective-permute-start.3 = (bf16[2560,384]{1,0:T(8,128)(2,1)S(1)}, bf16[2560,384]{1,0:T(8,128)(2,1)}, u32[]{:S(2)}, u32[]{:S(2)}) collective-permute-start(bf16[2560,384]{1,0:T(8,128)(2,1)S(1)} %bitcast.57), channel_id=1, source_target_pairs={{0,1},{1,0},{2,3},{3,2},{4,7},{5,6},{6,5},{7,4},{8,9},{9,8},{10,11... | collective-permute-start | bytes 5898248 | tf_op jit(solution)/shard_map/ppermute | solution.py:20
  64.5 88.9 %collective-permute-start.4 = (bf16[2560,384]{1,0:T(8,128)(2,1)}, bf16[2560,384]{1,0:T(8,128)(2,1)}, u32[]{:S(2)}, u32[]{:S(2)}) collective-permute-start(bf16[2560,384]{1,0:T(8,128)(2,1)} %bitcast.10.up_w_ref.refs_4_), channel_id=1, source_target_pairs={{0,1},{1,0},{2,3},{3,2},{4,7},{5,6},{6,5},{7,4},{8,9},{9,8},{10,11... | collective-permute-start | bytes 5898248 | tf_op jit(solution)/shard_map/ppermute | solution.py:20
  65.3 45.0 %collective-permute-start = (bf16[512,1280]{1,0:T(8,128)(2,1)}, bf16[512,1280]{1,0:T(8,128)(2,1)}, u32[]{:S(2)}, u32[]{:S(2)}) collective-permute-start(bf16[512,1280]{1,0:T(8,128)(2,1)} %bitcast.60), channel_id=1, source_target_pairs={{0,3},{1,2},{2,1},{3,0},{4,5},{5,4},{6,7},{7,6},{8,11},{9,10},{10,... | collective-permute-start | bytes 3932168 | tf_op jit(solution)/shard_map/ppermute | solution.py:20
  66.9 20.3 %copy-start.4 = (bf16[384,640]{1,0:T(8,128)(2,1)}, bf16[384,640]{1,0:T(8,128)(2,1)S(1)}, u32[]{:S(2)}) copy-start(bf16[384,640]{1,0:T(8,128)(2,1)S(1)} %get-tuple-element.38) | copy-start | bytes 1474564
  67.0 21.3 %copy-start.6 = (bf16[384,640]{1,0:T(8,128)(2,1)}, bf16[384,640]{1,0:T(8,128)(2,1)S(1)}, u32[]{:S(2)}) copy-start(bf16[384,640]{1,0:T(8,128)(2,1)S(1)} %get-tuple-element.39) | copy-start | bytes 1474564
  82.2 65.4 %collective-permute-start.6 = (bf16[384,1280]{1,0:T(8,128)(2,1)}, bf16[384,1280]{1,0:T(8,128)(2,1)}, u32[]{:S(2)}, u32[]{:S(2)}) collective-permute-start(bf16[384,1280]{1,0:T(8,128)(2,1)} %collective-permute-done.2.first_hbm), channel_id=1, source_target_pairs={{0,1},{1,0},{2,3},{3,2},{4,7},{5,6},{6,5},{7,4},{8,9},{9,8},{10,11... | collective-permute-start | bytes 2949128 | tf_op jit(solution)/shard_map/ppermute | solution.py:20
  88.3 74.4 %collective-permute-start.7 = (bf16[384,1280]{1,0:T(8,128)(2,1)}, bf16[384,1280]{1,0:T(8,128)(2,1)}, u32[]{:S(2)}, u32[]{:S(2)}) collective-permute-start(bf16[384,1280]{1,0:T(8,128)(2,1)} %pad_maximum_fusion.refs_0_), channel_id=1, source_target_pairs={{0,1},{1,0},{2,3},{3,2},{4,7},{5,6},{6,5},{7,4},{8,9},{9,8},{10,11... | collective-permute-start | bytes 2949128 | tf_op jit(solution)/shard_map/ppermute | solution.py:20
  116.2 48.6 %collective-permute-start.1 = (bf16[512,384]{1,0:T(8,128)(2,1)}, bf16[512,384]{1,0:T(8,128)(2,1)}, u32[]{:S(2)}, u32[]{:S(2)}) collective-permute-start(bf16[512,384]{1,0:T(8,128)(2,1)} %get-tuple-element.17), channel_id=1, source_target_pairs={{0,3},{1,2},{2,1},{3,0},{4,5},{5,4},{6,7},{7,6},{8,11},{9,10},{10,... | collective-permute-start | bytes 1179656 | tf_op jit(solution)/shard_map/ppermute | solution.py:20
  153.1 37.3 %collective-permute-start.10 = (bf16[512,768]{1,0:T(8,128)(2,1)}, bf16[512,768]{1,0:T(8,128)(2,1)}, u32[]{:S(2)}, u32[]{:S(2)}) collective-permute-start(bf16[512,768]{1,0:T(8,128)(2,1)} %partner_part.1), channel_id=1, source_target_pairs={{0,3},{1,2},{2,1},{3,0},{4,5},{5,4},{6,7},{7,6},{8,11},{9,10},{10,... | collective-permute-start | bytes 2359304 | tf_op jit(solution)/shard_map/ppermute | solution.py:20
  161.3 7.6 %collective-permute-start.5 = (bf16[512,384]{1,0:T(8,128)(2,1)}, bf16[512,384]{1,0:T(8,128)(2,1)S(1)}, u32[]{:S(2)}, u32[]{:S(2)}) collective-permute-start(bf16[512,384]{1,0:T(8,128)(2,1)} %get-tuple-element.18), channel_id=1, source_target_pairs={{0,3},{1,2},{2,1},{3,0},{4,5},{5,4},{6,7},{7,6},{8,11},{9,10},{10,... | collective-permute-start | bytes 1179656 | tf_op jit(solution)/shard_map/ppermute | solution.py:20
  172.2 13.3 %copy-start.1 = (bf16[1,2560,384]{2,1,0:T(8,128)(2,1)S(1)}, bf16[1,2560,384]{2,1,0:T(8,128)(2,1)}, u32[]{:S(2)}) copy-start(bf16[1,2560,384]{2,1,0:T(8,128)(2,1)} %param.10) | copy-start | bytes 5898244
  172.2 47.4 %all-to-all-start.1 = ((bf16[64,8,1280]{2,1,0:T(8,128)(2,1)}), bf16[64,8,1280]{2,1,0:T(8,128)(2,1)}, u32[]{:S(2)}, u32[]{:S(2)}) async-start(bf16[64,8,1280]{2,1,0:T(8,128)(2,1)} %fusion.6), calls=%async_computation.1 | async-start | bytes 2621440 | tf_op jit(solution)/shard_map/all_to_all | solution.py:59
  200.1 17.4 %collective-permute-start.11 = (bf16[512,1280]{1,0:T(8,128)(2,1)}, bf16[512,1280]{1,0:T(8,128)(2,1)S(1)}, u32[]{:S(2)}, u32[]{:S(2)}) collective-permute-start(bf16[512,1280]{1,0:T(8,128)(2,1)} %get-tuple-element.27), channel_id=1, source_target_pairs={{0,3},{1,2},{2,1},{3,0},{4,5},{5,4},{6,7},{7,6},{8,11},{9,10},{10,... | collective-permute-start | bytes 3932168 | tf_op jit(solution)/shard_map/ppermute | solution.py:20
  219.6 45.7 %all-to-all-start.3 = ((bf16[64,8,1280]{2,1,0:T(8,128)(2,1)}), bf16[64,8,1280]{2,1,0:T(8,128)(2,1)S(1)}, u32[]{:S(2)}, u32[]{:S(2)}) async-start(bf16[64,8,1280]{2,1,0:T(8,128)(2,1)} %fusion.7), calls=%async_computation.3 | async-start | bytes 2621440 | tf_op jit(solution)/shard_map/all_to_all | solution.py:59
  234.0 31.3 %copy-start.15 = (bf16[64,8,128]{2,0,1:T(8,128)(2,1)S(1)}, bf16[64,8,128]{2,0,1:T(8,128)(2,1)}, u32[]{:S(2)}) copy-start(bf16[64,8,128]{2,0,1:T(8,128)(2,1)} %get-tuple-element.61) | copy-start | bytes 393220
  236.0 31.7 %collective-permute-start.8 = (bf16[128,640]{1,0:T(8,128)(2,1)S(1)}, bf16[128,640]{1,0:T(8,128)(2,1)S(1)}, u32[]{:S(2)}, u32[]{:S(2)}) collective-permute-start(bf16[128,640]{1,0:T(8,128)(2,1)S(1)} %get-tuple-element.44), channel_id=1, source_target_pairs={{0,1},{1,0},{2,3},{3,2},{4,5},{5,4},{6,7},{7,6},{8,9},{9,8},{10,11... | collective-permute-start | bytes 491528 | tf_op jit(solution)/shard_map/ppermute | solution.py:410
  236.1 31.6 %collective-permute-start.9 = (bf16[128,640]{1,0:T(8,128)(2,1)S(1)}, bf16[128,640]{1,0:T(8,128)(2,1)S(1)}, u32[]{:S(2)}, u32[]{:S(2)}) collective-permute-start(bf16[128,640]{1,0:T(8,128)(2,1)S(1)} %get-tuple-element.45), channel_id=1, source_target_pairs={{0,3},{1,2},{2,1},{3,0},{4,7},{5,6},{6,5},{7,4},{8,11},{9,10},{10,... | collective-permute-start | bytes 491528 | tf_op jit(solution)/shard_map/ppermute | solution.py:410
  265.9 6.0 %collective-permute-start.12 = (bf16[128,640]{1,0:T(8,128)(2,1)S(1)}, bf16[128,640]{1,0:T(8,128)(2,1)S(1)}, u32[]{:S(2)}, u32[]{:S(2)}) collective-permute-start(bf16[128,640]{1,0:T(8,128)(2,1)S(1)} %get-tuple-element.42), channel_id=1, source_target_pairs={{0,1},{1,0},{2,3},{3,2},{4,5},{5,4},{6,7},{7,6},{8,9},{9,8},{10,11... | collective-permute-start | bytes 491528 | tf_op jit(solution)/shard_map/ppermute | solution.py:410
  266.0 7.2 %collective-permute-start.13 = (bf16[128,640]{1,0:T(8,128)(2,1)S(1)}, bf16[128,640]{1,0:T(8,128)(2,1)S(1)}, u32[]{:S(2)}, u32[]{:S(2)}) collective-permute-start(bf16[128,640]{1,0:T(8,128)(2,1)S(1)} %get-tuple-element.43), channel_id=1, source_target_pairs={{0,3},{1,2},{2,1},{3,0},{4,7},{5,6},{6,5},{7,4},{8,11},{9,10},{10,... | collective-permute-start | bytes 491528 | tf_op jit(solution)/shard_map/ppermute | solution.py:410
  (10 other events, 20.8 us)
